TPU v7x, 128 devices: a whole 4x4x4 slice. The times are simulated.
128 devices in a mesh: row: 8 (over y, core), col: 16 (over x, z).
Axes of the slice: x: 4, y: 4, z: 4, core: 2. Of those that a mesh axis runs over, the one named last changes fastest.
Arguments:
- features: bfloat16 [262144, 128], P(('row', 'col')), may hold values from -6 to 6
- new_index: int32 [262144], P(('row', 'col')), may hold values from 0 to 262143, as said below
- tile_values: bfloat16 [8, 16, 640, 128, 128], P('row', 'col'), may hold values from -0.125 to 0.125
- tile_index: int32 [8, 16, 2, 640], P('row', 'col'), may hold values from 0 to 255, as said below
- tile_count: int32 [8, 16], P('row', 'col'), may hold values from 80 to 640, as said below
- weight: bfloat16 [128, 256], replicated, may hold values from -0.5 to 0.5
- bias: float32 [256], replicated, may hold values from -3 to 3
Outputs:
- hidden: bfloat16 [262144, 256], P(('row', 'col'))
Inputs may be any that keep to these rules, and one draw needn't show every extreme that they name: A permutation. The new owner of a vertex is k = new_index // 2048; owner k is the device at grid row k mod the number of grid rows and grid column k div that number. From one device to one new owner at most 32 vertices move, and exactly 32 do for some pair in every draw. `tile_index`: entry 0 of a slot is a row tile below 256, entry 1 a column tile below 128; the slots of one grid block name distinct tiles. `tile_count`: some grid block holds 640 nonzero tiles in every draw.
All inputs are finite; a program needn't handle non-finite values.
Results may differ from a plain program's by a relative error of at most 0.017.
Values may be sent and summed in bfloat16 or wider, within the bound.
No kernel may reach another device: no remote copies, remote signals or barrier semaphores. Data moves between devices by JAX's collectives and lax.ppermute only.
A program may use at most 128 MiB of HBM per device.

v0:
```python
import jax
import jax.numpy as jnp
from jax import lax
from jax.sharding import PartitionSpec as P

GROUP = 64


def body(features, new_index, tile_values, tile_index, tile_count, weight, bias):
    grid_rows = lax.axis_size("row")
    grid_cols = lax.axis_size("col")
    device_total = grid_rows * grid_cols
    local_rows = features.shape[0]
    feature_width = features.shape[1]
    capacity = 2 * local_rows // device_total
    new_owner = new_index // local_rows
    new_slot = new_index % local_rows
    target_peer = new_owner % grid_rows * grid_cols + new_owner // grid_rows
    peer_hits = (target_peer[:, None] == jnp.arange(device_total, dtype=jnp.int32)[None, :]).astype(
        jnp.int32
    )
    peer_rank = jnp.sum((jnp.cumsum(peer_hits, axis=0) - peer_hits) * peer_hits, axis=1)
    outgoing = (
        jnp.zeros((device_total, capacity, feature_width), jnp.bfloat16)
        .at[target_peer, peer_rank]
        .set(features)
    )
    slots_out = (
        jnp.full((device_total, capacity), local_rows, jnp.int32)
        .at[target_peer, peer_rank]
        .set(new_slot)
    )
    rows_in, slots_in = (
        lax.all_to_all(outgoing, ("row", "col"), split_axis=0, concat_axis=0, tiled=True),
        lax.all_to_all(slots_out, ("row", "col"), split_axis=0, concat_axis=0, tiled=True),
    )
    moved_rows = (
        jnp.zeros((local_rows, feature_width), jnp.bfloat16)
        .at[slots_in.reshape(-1)]
        .set(rows_in.reshape(-1, feature_width), mode="drop")
    )
    column_block = lax.all_gather(moved_rows, "row", axis=0, tiled=True)
    tile_set = tile_values[0, 0]
    tile_coords = tile_index[0, 0]
    tile_total = tile_count[0, 0]
    tile_edge = tile_set.shape[1]
    col_tiles = column_block.shape[0] // tile_edge
    row_tiles = local_rows * grid_cols // tile_edge
    input_tiles = column_block.reshape(col_tiles, tile_edge, feature_width)

    def add_tiles(step_index, totals):
        first_tile = step_index * GROUP
        part_tiles = lax.dynamic_slice_in_dim(tile_set, first_tile, GROUP, 0)
        part_rows = lax.dynamic_slice_in_dim(tile_coords[0], first_tile, GROUP, 0)
        part_cols = lax.dynamic_slice_in_dim(tile_coords[1], first_tile, GROUP, 0)
        inputs = input_tiles[part_cols]
        products = jnp.einsum(
            "tab,tbf->taf", part_tiles, inputs, preferred_element_type=jnp.float32
        )
        live_mask = first_tile + jnp.arange(GROUP, dtype=jnp.int32) < tile_total
        products = jnp.where(live_mask[:, None, None], products, jnp.zeros_like(products))
        return totals.at[part_rows].add(products)

    trips = (tile_total + GROUP - 1) // GROUP
    totals = lax.fori_loop(
        0, trips, add_tiles, jnp.zeros((row_tiles, tile_edge, feature_width), jnp.float32)
    )
    partial_rows = totals.reshape(row_tiles * tile_edge, feature_width)
    row_totals = lax.psum_scatter(
        partial_rows.astype(jnp.bfloat16), "col", scatter_dimension=0, tiled=True
    )
    hidden = jnp.dot(row_totals, weight, preferred_element_type=jnp.float32) + bias
    return jnp.maximum(hidden, 0.0).astype(jnp.bfloat16)


def solution(mesh):
    in_specs = (
        P(("row", "col"), None),
        P(("row", "col")),
        P("row", "col", None, None, None),
        P("row", "col", None, None),
        P("row", "col"),
        P(),
        P(),
    )
    out_specs = P(("row", "col"), None)
    return jax.shard_map(body, mesh=mesh, in_specs=in_specs, out_specs=out_specs, check_vma=False)
```

profile of v0, /device:TPU:0, one launch (start us, length us, event | category | flops | bytes accessed | tf_op | source)
XLA Modules:
  0.0 434.2 jit_solution(357774305717248672)
XLA Ops:
  6.5 0.0 copy-start
  6.5 0.0 copy-start.4
  6.5 0.0 copy-start.2
  6.5 0.7 compare_select_fusion.4
  7.3 0.1 copy.13
  7.4 0.3 fusion.10
  7.8 0.1 broadcast_add_fusion
  7.9 0.3 copy.14
  8.2 0.6 fusion.9
  8.9 0.0 copy-done.4
  8.9 0.1 and_reduce_fusion
  9.0 0.0 copy-done.2
  9.0 0.0 copy-done.3
  9.0 0.1 multiply_reduce_fusion
  9.1 8.1 %scatter_custom_fusion.2 = s32[4096]{0:T(1024)S(1)} fusion(s32[2048]{0:T(1024)S(1)} %get-tuple-element.68, s32[2048]{0:T(1024)S(1)} %get-tuple-element.66, s32[]{:T(128)} %constant.93.clone.1), kind=kCustom, calls=%fused_computation.54 | custom fusion | bytes 16388
  17.2 0.7 copy.15
  17.9 11.1 %all-to-all-start = ((s32[128,1,32]{2,1,0:T(1,128)}), s32[128,1,32]{2,1,0:T(1,128)S(1)}, u32[]{:S(2)}, u32[]{:S(2)}) async-start(s32[128,1,32]{2,1,0:T(1,128)} %copy.15), calls=%async_computation | async-start | bytes 131072 | tf_op jit(solution)/shard_map/all_to_all | solution.py:35
  29.1 7.1 %scatter_custom_fusion.3 = bf16[4096,128]{1,0:T(8,128)(2,1)} fusion(s32[2048]{0:T(1024)S(1)} %get-tuple-element.67, bf16[2048,128]{1,0:T(8,128)(2,1)} %param.9, bf16[]{:T(256)} %constant.92.clone.1), kind=kCustom, calls=%fused_computation.28 | custom fusion | bytes 1049088
  36.2 2.3 all-to-all-done
  38.5 7.4 %all-to-all-start.1 = ((bf16[128,32,128]{2,1,0:T(8,128)(2,1)}), bf16[128,32,128]{2,1,0:T(8,128)(2,1)S(1)}, u32[]{:S(2)}, u32[]{:S(2)}) async-start(bf16[128,32,128]{2,1,0:T(8,128)(2,1)} %bitcast.17), calls=%async_computation.1 | async-start | bytes 2097152 | tf_op jit(solution)/shard_map/all_to_all | solution.py:34
  46.0 0.0 all-gather.2.cloned.1.call-start
  46.0 0.6 broadcast.174
  46.6 0.8 reduce.10
  47.5 0.1 reshape.136
  47.6 17.4 %all-to-all-done.1 = bf16[128,32,128]{2,1,0:T(8,128)(2,1)S(1)} async-done(((bf16[128,32,128]{2,1,0:T(8,128)(2,1)}), bf16[128,32,128]{2,1,0:T(8,128)(2,1)S(1)}, u32[]{:S(2)}, u32[]{:S(2)}) %all-to-all-start.1) | async-done | bytes 1048608 | tf_op jit(solution)/shard_map/all_to_all | solution.py:34
  65.0 11.6 %scatter_custom_fusion.1 = bf16[2048,128]{1,0:T(8,128)(2,1)} fusion(s32[4096]{0:T(1024)S(1)} %bitcast.65, bf16[4096,128]{1,0:T(8,128)(2,1)S(1)} %bitcast.58, bf16[]{:T(256)} %constant.92.clone.1), kind=kCustom, calls=%fused_computation.32 | custom fusion | bytes 524290 | tf_op jit(solution)/shard_map/scatter | solution.py:40
  76.6 0.0 all-gather.2.cloned.1.call-update
  76.6 0.0 reduce-scatter.2.cloned.1.call-start
  77.3 27.0 %all-gather.2.cloned.1.call-done = bf16[16384,128]{1,0:T(8,128)(2,1)} async-done(((bf16[2048,128]{1,0:T(8,128)(2,1)}), bf16[16384,128]{1,0:T(8,128)(2,1)}) %all-gather.2.cloned.1.call-update) | async-done | bytes 4194320 | tf_op jit(solution)/shard_map/all_gather | solution.py:42
  104.4 7.8 %broadcast_in_dim.15 = f32[256,128,128]{2,1,0:T(8,128)} broadcast(f32[]{:T(128)} %constant.87.clone.1), dimensions={} | broadcast | bytes 16777220 | tf_op jit(solution)/shard_map/broadcast_in_dim | solution.py:66
  112.2 0.0 copy-done.1
  112.2 43.7 %while.10 = (s32[]{:T(128)}, f32[256,128,128]{2,1,0:T(8,128)}, s32[]{:T(128)}, s32[2,640]{1,0:T(2,128)S(1)}, s32[]{:T(128)}, /*index=5*/bf16[640,128,128]{2,1,0:...) while((s32[]{:T(128)}, f32[256,128,128]{2,1,0:T(8,128)}, ...), condition=%wide.region_8.9_spmd, body=%wide.region_6.8_spmd.sunk | while | flops 270534144 | bytes 25182252 | solution.py:65
  112.2 0.7 add_compare_fusion.2
  112.9 0.1 fusion.39
  113.0 3.1 gather_fusion
  116.1 4.3 convolution_select_fusion.2
  120.4 13.7 %scatter_fusion = f32[256,128,128]{2,1,0:T(8,128)} fusion(f32[256,128,128]{2,1,0:T(8,128)} %get-tuple-element.133, s32[64]{0:T(128)S(1)} %get-tuple-element.119, f32[64,128,128]{2,1,0:T(8,128)} %convolution_select_fusion.2), kind=kCustom, calls=%fused_computation.1.clone.1 | custom fusion | flops 1048576 | bytes 12583168 | tf_op jit(solution)/shard_map/while/body/scatter-add | solution.py:62
  134.1 0.7 add_compare_fusion.2
  134.7 0.1 fusion.39
  134.8 3.1 gather_fusion
  138.0 4.3 convolution_select_fusion.2
  142.2 13.7 %scatter_fusion = f32[256,128,128]{2,1,0:T(8,128)} fusion(f32[256,128,128]{2,1,0:T(8,128)} %get-tuple-element.133, s32[64]{0:T(128)S(1)} %get-tuple-element.119, f32[64,128,128]{2,1,0:T(8,128)} %convolution_select_fusion.2), kind=kCustom, calls=%fused_computation.1.clone.1 | custom fusion | flops 1048576 | bytes 12583168 | tf_op jit(solution)/shard_map/while/body/scatter-add | solution.py:62
  155.9 9.2 %convert_element_type.18 = bf16[256,128,128]{2,1,0:T(8,128)(2,1)} convert(f32[256,128,128]{2,1,0:T(8,128)} %get-tuple-element.43) | non-fusion elementwise | flops 4194304 | bytes 25165824 | tf_op jit(solution)/shard_map/convert_element_type | solution.py:70
  165.1 0.0 reduce-scatter.2.cloned.1.call-update
  165.1 259.8 %reduce-scatter.2.cloned.1.call-done = bf16[2048,128]{1,0:T(8,128)(2,1)} async-done(((bf16[32768,128]{1,0:T(8,128)(2,1)}), bf16[2048,128]{1,0:T(8,128)(2,1)}) %reduce-scatter.2.cloned.1.call-update) | async-done | bytes 524304 | tf_op jit(solution)/shard_map/reduce_scatter | solution.py:69
  424.9 0.0 copy-done
  424.9 0.0 copy-done.5
  424.9 2.4 fusion.7
  (13 shorter events, 0.1 us)
Async XLA Ops:
  6.5 418.4 %copy-start = (bf16[128,256]{1,0:T(8,128)(2,1)S(1)}, bf16[128,256]{1,0:T(8,128)(2,1)}, u32[]{:S(2)}) copy-start(bf16[128,256]{1,0:T(8,128)(2,1)} %param.14) | copy-start | bytes 196612
  6.5 2.3 copy-start.4
  6.5 2.4 copy-start.2
  6.5 2.5 copy-start.3
  17.9 20.6 %all-to-all-start = ((s32[128,1,32]{2,1,0:T(1,128)}), s32[128,1,32]{2,1,0:T(1,128)S(1)}, u32[]{:S(2)}, u32[]{:S(2)}) async-start(s32[128,1,32]{2,1,0:T(1,128)} %copy.15), calls=%async_computation | async-start | bytes 131072 | tf_op jit(solution)/shard_map/all_to_all | solution.py:35
  38.5 26.5 %all-to-all-start.1 = ((bf16[128,32,128]{2,1,0:T(8,128)(2,1)}), bf16[128,32,128]{2,1,0:T(8,128)(2,1)S(1)}, u32[]{:S(2)}, u32[]{:S(2)}) async-start(bf16[128,32,128]{2,1,0:T(8,128)(2,1)} %bitcast.17), calls=%async_computation.1 | async-start | bytes 2097152 | tf_op jit(solution)/shard_map/all_to_all | solution.py:34
  46.0 58.4 %all-gather.2.cloned.1.call-start = ((), (), s32[]{:S(2)}) async-start(), calls=%async_computation.3 | async-start | bytes 4718592 | tf_op jit(solution)/shard_map/all_gather | solution.py:42
  76.6 348.3 %reduce-scatter.2.cloned.1.call-start = ((), (), s32[]{:S(2)}) async-start(), calls=%async_computation.4 | async-start | bytes 8912896 | tf_op jit(solution)/shard_map/reduce_scatter | solution.py:69
  104.4 7.9 %copy-start.1 = (s32[1,1,2,640]{3,2,1,0:T(2,128)S(1)}, s32[1,1,2,640]{3,2,1,0:T(2,128)}, u32[]{:S(2)}) copy-start(s32[1,1,2,640]{3,2,1,0:T(2,128)} %param.12) | copy-start | bytes 15364
  165.1 259.8 %copy-start.5 = (f32[256]{0:T(256)S(1)}, f32[256]{0:T(256)}, u32[]{:S(2)}) copy-start(f32[256]{0:T(256)} %param.15) | copy-start | bytes 3076
Sparse Core Ops, SparseCore 0:
  76.8 27.5 all-gather.1
  165.2 259.6 reduce-scatter.1
where the time goes:
time: 437 us; the launch traced here: 434 us
  waiting for transfers between devices  307 us (70%)
  local copies, waits for them, and re-layouts  42.8 us (10%)
  other arithmetic  40.9 us (9%)
  starting transfers between devices  18.7 us (4%)
  between operations  14.2 us (3%)
  matrix products  11 us (3%)
    reduce_scatter x1, waiting for transfers between devices, body(): lax.psum_scatter(partial_rows.astype(jnp.bfloat16), 'col', scatter_dimens...  260 us
    scatter-add x2, other arithmetic, add_tiles(): return totals.at[part_rows].add(products)  27.3 us
    all_gather x1, waiting for transfers between devices, body(): column_block = lax.all_gather(moved_rows, 'row', axis=0, tiled=True)  27 us
    all_to_all x1, waiting for transfers between devices, body(): lax.all_to_all(outgoing, ('row', 'col'), split_axis=0, concat_axis=0, til...  17.4 us
    unnamed x14, local copies, waits for them, and re-layouts  15.2 us
    scatter x1, local copies, waits for them, and re-layouts, body(): moved_rows = jnp.zeros((local_rows, feature_width), jnp.bfloat16).at[slot...  11.6 us
    all_to_all x1, starting transfers between devices, body(): lax.all_to_all(slots_out, ('row', 'col'), split_axis=0, concat_axis=0, ti...  11.1 us
    convert_element_type x1, other arithmetic, body(): partial_rows.astype(jnp.bfloat16)  9.2 us
  transfers between devices with their start and end apart: 4, of which 4 were waited for; matrix products, arithmetic and copies ran while one was open for 2% of the time, Pallas kernels for 0%

commit v1 on v0

--- a/solution.py
+++ b/solution.py
@@ -1,9 +1,72 @@
+import functools
+
 import jax
 import jax.numpy as jnp
 from jax import lax
+from jax.experimental import pallas as pl
+from jax.experimental.pallas import tpu as pltpu
 from jax.sharding import PartitionSpec as P
 
-GROUP = 64
+BLOCK = 64
+UNROLL = 16
+
+
+def tile_kernel(row_tiles, count_ref, index_ref, x_ref, tiles_ref, out_ref, totals):
+    edge = tiles_ref.shape[1]
+    first = pl.program_id(0) * BLOCK
+    count = count_ref[0]
+
+    @pl.when(pl.program_id(0) == 0)
+    def _():
+        totals[...] = jnp.zeros_like(totals)
+
+    def add_group(group, carry):
+        for step in range(UNROLL):
+            slot = group * UNROLL + step
+            row = jnp.where(first + slot < count, index_ref[0, first + slot], row_tiles)
+            col = index_ref[1, first + slot]
+            product = jnp.dot(
+                tiles_ref[slot],
+                x_ref[pl.ds(pl.multiple_of(col * edge, edge), edge), :],
+                preferred_element_type=jnp.float32,
+            )
+            totals[pl.ds(pl.multiple_of(row * edge, edge), edge), :] += product
+        return carry
+
+    groups = jnp.clip((count - first + UNROLL - 1) // UNROLL, 0, BLOCK // UNROLL)
+    lax.fori_loop(0, groups, add_group, 0)
+
+    @pl.when(pl.program_id(0) == pl.num_programs(0) - 1)
+    def _():
+        out_ref[...] = totals[: row_tiles * edge, :].astype(out_ref.dtype)
+
+
+def tile_products(count, index, x, tiles, rows):
+    slots, edge, _ = tiles.shape
+    width = x.shape[1]
+    row_tiles = rows // edge
+
+    def tile_block(step, count_ref, index_ref):
+        return jnp.minimum(step, jnp.maximum(count_ref[0] - 1, 0) // BLOCK), 0, 0
+
+    return pl.pallas_call(
+        functools.partial(tile_kernel, row_tiles),
+        out_shape=jax.ShapeDtypeStruct((rows, width), jnp.bfloat16),
+        grid_spec=pltpu.PrefetchScalarGridSpec(
+            num_scalar_prefetch=2,
+            grid=(slots // BLOCK,),
+            in_specs=[
+                pl.BlockSpec(x.shape, lambda *_: (0, 0), pipeline_mode=pl.Buffered(1)),
+                pl.BlockSpec((BLOCK, edge, edge), tile_block),
+            ],
+            out_specs=pl.BlockSpec(
+                (rows, width), lambda *_: (0, 0), pipeline_mode=pl.Buffered(1)
+            ),
+            scratch_shapes=[pltpu.VMEM((rows + edge, width), jnp.float32)],
+        ),
+        compiler_params=pltpu.CompilerParams(vmem_limit_bytes=56 << 20),
+        name="tile_products",
+    )(count, index, x, tiles)
 
 
 def body(features, new_index, tile_values, tile_index, tile_count, weight, bias):
@@ -41,33 +104,11 @@
     )
     column_block = lax.all_gather(moved_rows, "row", axis=0, tiled=True)
     tile_set = tile_values[0, 0]
-    tile_coords = tile_index[0, 0]
-    tile_total = tile_count[0, 0]
-    tile_edge = tile_set.shape[1]
-    col_tiles = column_block.shape[0] // tile_edge
-    row_tiles = local_rows * grid_cols // tile_edge
-    input_tiles = column_block.reshape(col_tiles, tile_edge, feature_width)
-
-    def add_tiles(step_index, totals):
-        first_tile = step_index * GROUP
-        part_tiles = lax.dynamic_slice_in_dim(tile_set, first_tile, GROUP, 0)
-        part_rows = lax.dynamic_slice_in_dim(tile_coords[0], first_tile, GROUP, 0)
-        part_cols = lax.dynamic_slice_in_dim(tile_coords[1], first_tile, GROUP, 0)
-        inputs = input_tiles[part_cols]
-        products = jnp.einsum(
-            "tab,tbf->taf", part_tiles, inputs, preferred_element_type=jnp.float32
-        )
-        live_mask = first_tile + jnp.arange(GROUP, dtype=jnp.int32) < tile_total
-        products = jnp.where(live_mask[:, None, None], products, jnp.zeros_like(products))
-        return totals.at[part_rows].add(products)
-
-    trips = (tile_total + GROUP - 1) // GROUP
-    totals = lax.fori_loop(
-        0, trips, add_tiles, jnp.zeros((row_tiles, tile_edge, feature_width), jnp.float32)
+    partial_rows = tile_products(
+        tile_count.reshape(1), tile_index[0, 0], column_block, tile_set, local_rows * grid_cols
     )
-    partial_rows = totals.reshape(row_tiles * tile_edge, feature_width)
     row_totals = lax.psum_scatter(
-        partial_rows.astype(jnp.bfloat16), "col", scatter_dimension=0, tiled=True
+        partial_rows, "col", scatter_dimension=0, tiled=True
     )
     hidden = jnp.dot(row_totals, weight, preferred_element_type=jnp.float32) + bias
     return jnp.maximum(hidden, 0.0).astype(jnp.bfloat16)

time: 437 us -> 222 us (0.51)
  waiting for transfers between devices: 307 us -> 144 us
  other arithmetic: 40.9 us -> 2.94 us
  local copies, waits for them, and re-layouts: 42.8 us -> 28.7 us
  Pallas kernels: 0 us -> 10.8 us
  matrix products: 11 us -> 2.43 us
    reduce_scatter x1, waiting for transfers between devices: 260 us -> 97.6 us  [body(): lax.psum_scatter(partial_rows, 'col', scatter_dimension=0, tiled=True)]
    scatter-add x2 -> x0, other arithmetic: 27.3 us -> none  [add_tiles(): return totals.at[part_rows].add(products)]
    pallas_call x0 -> x1, Pallas kernels: none -> 10.8 us  [tile_products(): pl.pallas_call(functools.partial(tile_kernel, row_tiles), out_shape=jax.S...]
    convert_element_type x1 -> x0, other arithmetic: 9.2 us -> none  [body(): partial_rows.astype(jnp.bfloat16)]
    dot_general x2 -> x0, matrix products: 8.53 us -> none  [add_tiles(): jnp.einsum('tab,tbf->taf', part_tiles, inputs, preferred_element_type=jnp...]
    broadcast_in_dim x1 -> x0, local copies, waits for them, and re-layouts: 7.85 us -> none  [body(): jnp.zeros((row_tiles, tile_edge, feature_width), jnp.float32)]
    gather x2 -> x0, local copies, waits for them, and re-layouts: 6.28 us -> none  [add_tiles(): inputs = input_tiles[part_cols]]
    unnamed x14 -> x12, local copies, waits for them, and re-layouts: 15.2 us -> 15.2 us
  transfers between devices with their start and end apart: 4 -> 4, of which waited for: 4 -> 4; matrix products, arithmetic and copies ran while one was open for 2% -> 4% of each run, Pallas kernels for 0% -> 0%
where the time goes in v1:
time: 222 us
  waiting for transfers between devices  144 us (65%)
  local copies, waits for them, and re-layouts  28.7 us (13%)
  starting transfers between devices  18.7 us (8%)
  between operations  14.2 us (6%)
  Pallas kernels  10.8 us (5%)
  other arithmetic  2.94 us (1%)
  matrix products  2.43 us (1%)
    reduce_scatter x1, waiting for transfers between devices, body(): lax.psum_scatter(partial_rows, 'col', scatter_dimension=0, tiled=True)  97.6 us
    all_gather x1, waiting for transfers between devices, body(): column_block = lax.all_gather(moved_rows, 'row', axis=0, tiled=True)  27 us
    all_to_all x1, waiting for transfers between devices, body(): lax.all_to_all(outgoing, ('row', 'col'), split_axis=0, concat_axis=0, til...  17.4 us
    unnamed x12, local copies, waits for them, and re-layouts  15.2 us
    scatter x1, local copies, waits for them, and re-layouts, body(): moved_rows = jnp.zeros((local_rows, feature_width), jnp.bfloat16).at[slot...  11.6 us
    all_to_all x1, starting transfers between devices, body(): lax.all_to_all(slots_out, ('row', 'col'), split_axis=0, concat_axis=0, ti...  11.1 us
    pallas_call x1, Pallas kernels, tile_products(): pl.pallas_call(functools.partial(tile_kernel, row_tiles), out_shape=jax.S...  10.8 us
    all_to_all x1, starting transfers between devices, body(): lax.all_to_all(outgoing, ('row', 'col'), split_axis=0, concat_axis=0, til...  7.43 us
  transfers between devices with their start and end apart: 4, of which 4 were waited for; matrix products, arithmetic and copies ran while one was open for 4% of the time, Pallas kernels for 0%

profile of v1, /device:TPU:0, one launch (start us, length us, event | category | flops | bytes accessed | tf_op | source)
XLA Modules:
  0.0 222.1 jit_solution(17707637336618331208)
XLA Ops:
  6.5 0.0 copy-start
  6.5 0.8 compare_select_fusion.2
  7.3 0.1 copy.13
  7.4 0.3 fusion.4
  7.8 0.1 broadcast_add_fusion
  7.9 0.0 copy-start.3
  7.9 0.0 copy-start.1
  7.9 0.0 copy-start.2
  7.9 0.3 copy.14
  8.2 0.6 fusion.3
  8.9 0.0 copy-done.3
  8.9 0.1 and_reduce_fusion
  9.0 0.0 copy-done.1
  9.0 0.0 copy-done.2
  9.0 0.1 multiply_reduce_fusion
  9.2 8.1 %scatter_custom_fusion.1 = s32[4096]{0:T(1024)S(1)} fusion(s32[2048]{0:T(1024)S(1)} %get-tuple-element.11, s32[2048]{0:T(1024)S(1)} %get-tuple-element.9, s32[]{:T(128)} %constant.55.clone.1), kind=kCustom, calls=%fused_computation.39 | custom fusion | bytes 16388
  17.2 0.7 copy.15
  18.0 11.1 %all-to-all-start = ((s32[128,1,32]{2,1,0:T(1,128)}), s32[128,1,32]{2,1,0:T(1,128)S(1)}, u32[]{:S(2)}, u32[]{:S(2)}) async-start(s32[128,1,32]{2,1,0:T(1,128)} %copy.15), calls=%async_computation | async-start | bytes 131072 | tf_op jit(solution)/shard_map/all_to_all | solution.py:98
  29.1 7.1 %scatter_custom_fusion.2 = bf16[4096,128]{1,0:T(8,128)(2,1)} fusion(s32[2048]{0:T(1024)S(1)} %get-tuple-element.10, bf16[2048,128]{1,0:T(8,128)(2,1)} %param.7, bf16[]{:T(256)} %constant.54.clone.1), kind=kCustom, calls=%fused_computation.13 | custom fusion | bytes 1049088
  36.3 2.3 %all-to-all-done = s32[128,1,32]{2,1,0:T(1,128)S(1)} async-done(((s32[128,1,32]{2,1,0:T(1,128)}), s32[128,1,32]{2,1,0:T(1,128)S(1)}, u32[]{:S(2)}, u32[]{:S(2)}) %all-to-all-start) | async-done | bytes 16416 | tf_op jit(solution)/shard_map/all_to_all | solution.py:98
  38.6 7.4 %all-to-all-start.1 = ((bf16[128,32,128]{2,1,0:T(8,128)(2,1)}), bf16[128,32,128]{2,1,0:T(8,128)(2,1)S(1)}, u32[]{:S(2)}, u32[]{:S(2)}) async-start(bf16[128,32,128]{2,1,0:T(8,128)(2,1)} %bitcast.12), calls=%async_computation.1 | async-start | bytes 2097152 | tf_op jit(solution)/shard_map/all_to_all | solution.py:97
  46.0 0.0 all-gather.2.cloned.1.call-start
  46.1 0.6 broadcast.110
  46.7 0.8 reduce.10
  47.5 0.1 reshape.72
  47.6 17.4 %all-to-all-done.1 = bf16[128,32,128]{2,1,0:T(8,128)(2,1)S(1)} async-done(((bf16[128,32,128]{2,1,0:T(8,128)(2,1)}), bf16[128,32,128]{2,1,0:T(8,128)(2,1)S(1)}, u32[]{:S(2)}, u32[]{:S(2)}) %all-to-all-start.1) | async-done | bytes 1048608 | tf_op jit(solution)/shard_map/all_to_all | solution.py:97
  65.1 11.6 %scatter_custom_fusion = bf16[2048,128]{1,0:T(8,128)(2,1)} fusion(s32[4096]{0:T(1024)S(1)} %bitcast.37, bf16[4096,128]{1,0:T(8,128)(2,1)S(1)} %bitcast.31, bf16[]{:T(256)} %constant.54.clone.1), kind=kCustom, calls=%fused_computation.17 | custom fusion | bytes 524290 | tf_op jit(solution)/shard_map/scatter | solution.py:103
  76.6 0.0 all-gather.2.cloned.1.call-update
  76.7 0.0 reduce-scatter.2.cloned.1.call-start
  77.4 27.0 %all-gather.2.cloned.1.call-done.x_ref = bf16[16384,128]{1,0:T(8,128)(2,1)} async-done(((bf16[2048,128]{1,0:T(8,128)(2,1)}), bf16[16384,128]{1,0:T(8,128)(2,1)}) %all-gather.2.cloned.1.call-update) | async-done | bytes 4194320 | tf_op jit(solution)/shard_map/all_gather | solution.py:105
  104.4 10.8 %tile_products.1 = bf16[32768,128]{1,0:T(8,128)(2,1)} custom-call(s32[1]{0:T(128)} %bitcast.26.count_ref, s32[2,640]{1,0:T(2,128)} %bitcast.38, bf16[16384,128]{1,0:T(8,128)(2,1)} %all-gather.2.cloned.1.call-done.x_ref, bf16[640,128,128]{2,1,0:T(8,128)(2,1)} %bitcast.30), custom_call_target="tpu_custom_call" | custom-call | tf_op jit(solution)/shard_map/tile_products/pallas_call | solution.py:52
  115.2 0.0 copy-start.4
  115.2 0.0 reduce-scatter.2.cloned.1.call-update
  115.2 97.6 %reduce-scatter.2.cloned.1.call-done = bf16[2048,128]{1,0:T(8,128)(2,1)} async-done(((bf16[32768,128]{1,0:T(8,128)(2,1)}), bf16[2048,128]{1,0:T(8,128)(2,1)}) %reduce-scatter.2.cloned.1.call-update) | async-done | bytes 524304 | tf_op jit(solution)/shard_map/reduce_scatter | solution.py:110
  212.8 0.0 copy-done
  212.8 0.0 copy-done.4
  212.8 2.4 %fusion.1 = bf16[2048,256]{1,0:T(8,128)(2,1)} fusion(bf16[2048,128]{1,0:T(8,128)(2,1)} %reduce-scatter.2.cloned.1.call-done, bf16[128,256]{1,0:T(8,128)(2,1)S(1)} %copy-done, f32[256]{0:T(256)S(1)} %copy-done.4), kind=kOutput, calls=%fused_computation.5 | convolution fusion | flops 135790592 | bytes 1639424 | tf_op jit(solution)/shard_map/dot_general | solution.py:113
  (6 shorter events, 0.1 us)
Async XLA Ops:
  6.5 206.3 %copy-start = (bf16[128,256]{1,0:T(8,128)(2,1)S(1)}, bf16[128,256]{1,0:T(8,128)(2,1)}, u32[]{:S(2)}) copy-start(bf16[128,256]{1,0:T(8,128)(2,1)} %param.12) | copy-start | bytes 196612
  7.9 1.1 copy-start.3
  7.9 1.2 copy-start.1
  7.9 1.1 copy-start.2
  18.0 20.6 %all-to-all-start = ((s32[128,1,32]{2,1,0:T(1,128)}), s32[128,1,32]{2,1,0:T(1,128)S(1)}, u32[]{:S(2)}, u32[]{:S(2)}) async-start(s32[128,1,32]{2,1,0:T(1,128)} %copy.15), calls=%async_computation | async-start | bytes 131072 | tf_op jit(solution)/shard_map/all_to_all | solution.py:98
  38.6 26.5 %all-to-all-start.1 = ((bf16[128,32,128]{2,1,0:T(8,128)(2,1)}), bf16[128,32,128]{2,1,0:T(8,128)(2,1)S(1)}, u32[]{:S(2)}, u32[]{:S(2)}) async-start(bf16[128,32,128]{2,1,0:T(8,128)(2,1)} %bitcast.12), calls=%async_computation.1 | async-start | bytes 2097152 | tf_op jit(solution)/shard_map/all_to_all | solution.py:97
  46.0 58.4 %all-gather.2.cloned.1.call-start = ((), (), s32[]{:S(2)}) async-start(), calls=%async_computation.3 | async-start | bytes 4718592 | tf_op jit(solution)/shard_map/all_gather | solution.py:105
  76.7 136.2 %reduce-scatter.2.cloned.1.call-start = ((), (), s32[]{:S(2)}) async-start(), calls=%async_computation.4 | async-start | bytes 8912896 | tf_op jit(solution)/shard_map/reduce_scatter | solution.py:110
  115.2 97.6 %copy-start.4 = (f32[256]{0:T(256)S(1)}, f32[256]{0:T(256)}, u32[]{:S(2)}) copy-start(f32[256]{0:T(256)} %param.13) | copy-start | bytes 3076
Sparse Core Ops, SparseCore 0:
  76.8 27.5 all-gather.1
  115.4 97.4 reduce-scatter.1

commit v2 on v0

v2 whole, which is shorter than its diff:
```python
import functools

import jax
import jax.numpy as jnp
from jax import lax
from jax.experimental import pallas as pl
from jax.experimental.pallas import tpu as pltpu
from jax.sharding import Mesh
from jax.sharding import PartitionSpec as P

EXTRA = 8
PICK = 256
UNROLL = 16
SLOTS = 6
STREAMS = 4
SIDE = 4
LANES = 128
F32 = jnp.float32
BF16 = jnp.bfloat16


def iota(shape, axis):
    return lax.broadcasted_iota(jnp.int32, shape, axis)


def log2(size):
    assert size & (size - 1) == 0
    return size.bit_length() - 1


def params(mib, **rest):
    return pltpu.CompilerParams(vmem_limit_bytes=mib << 20, **rest)


VMEM = pl.BlockSpec(memory_space=pltpu.VMEM)
SMEM = pl.BlockSpec(memory_space=pltpu.SMEM)


def pack_kernel(grid_rows, grid_cols, capacity, index_ref, rows_ref, out_ref):
    local_rows, width = rows_ref.shape
    peers = grid_rows * grid_cols
    lower = (iota((LANES, LANES), 0) < iota((LANES, LANES), 1)).astype(F32).astype(BF16)
    nt = (((1,), (1,)), ((), ()))
    seen = jnp.zeros((peers, 1), F32)
    high = jnp.zeros((peers, LANES), F32)
    low = jnp.zeros((peers, LANES), F32)
    zero = jnp.zeros((LANES, LANES), F32)
    places = []
    for block in range(local_rows // LANES):
        index = index_ref[block : block + 1, :]
        owner = index >> log2(local_rows)
        slot = index & (local_rows - 1)
        peer = (owner & (grid_rows - 1)) * grid_cols + (owner >> log2(grid_rows))
        hit = (iota((peers, LANES), 0) == peer).astype(F32)
        hit16 = hit.astype(BF16)
        before = jnp.dot(hit16, lower, preferred_element_type=F32) + seen
        rank = jnp.sum(before * hit, axis=0, keepdims=True).astype(jnp.int32)
        seen = seen + jnp.sum(hit, axis=1, keepdims=True)
        places.append(peer * capacity + rank)
        same = (iota((LANES, LANES), 0) & (capacity - 1)) == rank
        slot_high = jnp.where(same, ((slot >> 7) + 1).astype(F32), zero).astype(BF16)
        slot_low = jnp.where(same, (slot & 127).astype(F32), zero).astype(BF16)
        high += lax.dot_general(hit16, slot_high, nt, preferred_element_type=F32)
        low += lax.dot_general(hit16, slot_low, nt, preferred_element_type=F32)
    place = jnp.concatenate(places, axis=1)
    part = PICK // capacity

    def pick_rows(step, carry):
        pick = (iota((PICK, local_rows), 0) + step * PICK == place).astype(F32).astype(BF16)
        rows = jnp.dot(pick, rows_ref[...], preferred_element_type=F32).astype(BF16)
        out_ref[pl.ds(step * part, part), 0:capacity, :] = rows.reshape(part, capacity, width)
        return carry

    lax.fori_loop(0, peers * capacity // PICK, pick_rows, 0)
    at = iota((peers, EXTRA, LANES), 1)
    none = jnp.zeros((peers, EXTRA, LANES), F32)
    extra = jnp.where(
        at == 0,
        high.reshape(peers, 1, LANES) + none,
        jnp.where(at == 1, low.reshape(peers, 1, LANES) + none, none),
    )
    out_ref[:, capacity:, :] = extra.astype(BF16)


def pack_rows(index, rows, grid_rows, grid_cols, capacity):
    peers = grid_rows * grid_cols
    return pl.pallas_call(
        functools.partial(pack_kernel, grid_rows, grid_cols, capacity),
        out_shape=jax.ShapeDtypeStruct((peers, capacity + EXTRA, rows.shape[1]), BF16),
        in_specs=[VMEM] * 2,
        out_specs=VMEM,
        compiler_params=params(32),
        name="pack_rows",
    )(index.reshape(-1, LANES), rows)


def place_kernel(in_ref, out_ref, slot_ref, rows_ref):
    peers, held, width = in_ref.shape
    capacity = held - EXTRA
    local_rows = out_ref.shape[0]
    per = LANES // capacity
    extra = in_ref[:, capacity:, :].astype(F32)
    high, low = extra[:, 0, :], extra[:, 1, :]
    slot_ref[...] = jnp.where(high > 0.5, (high - 1.0) * 128.0 + low, -1.0)
    rows_ref[...] = in_ref[:, 0:capacity, :].reshape(peers * capacity, width)
    which = iota((peers // per, LANES), 1) >> log2(capacity)
    slot = jnp.zeros((peers // per, LANES), F32)
    for i in range(per):
        slot = jnp.where(which == i, slot_ref[pl.ds(i, peers // per, stride=per), :], slot)
    slot = slot.astype(jnp.int32)
    slot = jnp.concatenate([slot[q : q + 1, :] for q in range(peers // per)], axis=1)

    def place_rows(step, carry):
        pick = (iota((PICK, peers * capacity), 0) + step * PICK == slot).astype(F32).astype(BF16)
        rows = jnp.dot(pick, rows_ref[...], preferred_element_type=F32)
        out_ref[pl.ds(pl.multiple_of(step * PICK, PICK), PICK), :] = rows.astype(BF16)
        return carry

    lax.fori_loop(0, local_rows // PICK, place_rows, 0)


def place_rows(got, local_rows):
    peers, held, width = got.shape
    return pl.pallas_call(
        place_kernel,
        out_shape=jax.ShapeDtypeStruct((local_rows, width), BF16),
        in_specs=[VMEM],
        out_specs=VMEM,
        scratch_shapes=[
            pltpu.VMEM((peers, LANES), F32),
            pltpu.VMEM((peers * (held - EXTRA), width), BF16),
        ],
        compiler_params=params(32),
        name="place_rows",
    )(got)


def plan_kernel(row_tiles, me_ref, count_ref, index_ref, slot_ref, row_ref, col_ref, size_ref):
    me_x, me_z = me_ref[0], me_ref[1]
    half = row_tiles // 2
    groups = (0b01111000, 0b10110100)

    def group_of(delta, pairing):
        table = jnp.where(pairing == 0, groups[0], groups[1])
        return (table >> (2 * delta)) & 3

    def visit(tile, sizes):
        row, col = index_ref[0, tile], index_ref[1, tile]
        dest, inner = row // 16, row % 16
        stream, sub = inner // 4, inner % 4
        d_x, d_z = (dest // SIDE) ^ me_x, (dest % SIDE) ^ me_z
        first = jnp.where(stream < 2, d_x, d_z)
        second = jnp.where(stream < 2, d_z, d_x)
        g_1 = group_of(first, stream % 2)
        g_2 = group_of(second, stream % 2)
        kept = jnp.where(g_1 < 2, 1, 0)
        place = stream * 32 + (g_1 % 2) * 16 + g_2 * 4 + sub
        at = jnp.where(kept == 1, sizes[1], sizes[0])
        slot_ref[kept, at] = tile
        row_ref[kept, at] = place
        col_ref[kept, at] = col
        return sizes[0] + 1 - kept, sizes[1] + kept

    sizes = lax.fori_loop(0, count_ref[0], visit, (jnp.int32(0), jnp.int32(0)))
    for kept in range(2):
        size_ref[kept] = (sizes[kept] + UNROLL - 1) // UNROLL
        for step in range(UNROLL):
            slot_ref[kept, sizes[kept] + step] = 0
            row_ref[kept, sizes[kept] + step] = half
            col_ref[kept, sizes[kept] + step] = 0


def plan_tiles(me, count, index, row_tiles):
    slots = index.shape[1] + UNROLL
    table = jax.ShapeDtypeStruct((2, slots), jnp.int32)
    return pl.pallas_call(
        functools.partial(plan_kernel, row_tiles),
        out_shape=[table, table, table, jax.ShapeDtypeStruct((2,), jnp.int32)],
        in_specs=[SMEM] * 3,
        out_specs=[SMEM] * 4,
        name="plan_tiles",
    )(me, count, index)


def tile_kernel(kept, slot_ref, row_ref, col_ref, size_ref, x_ref, tiles_ref, *refs):
    out_refs, (held, totals, sems) = refs[:STREAMS], refs[STREAMS:]
    edge = held.shape[2]
    groups = size_ref[kept]

    def fetch(group):
        lane = lax.rem(group, SLOTS)
        for step in range(UNROLL):
            tile = slot_ref[kept, group * UNROLL + step]
            pltpu.make_async_copy(tiles_ref.at[tile], held.at[lane, step], sems.at[lane]).start()

    for ahead in range(SLOTS - 1):

        @pl.when(ahead < groups)
        def _():
            fetch(ahead)

    totals[...] = jnp.zeros_like(totals)

    def add_group(group, carry):
        @pl.when(group + SLOTS - 1 < groups)
        def _():
            fetch(group + SLOTS - 1)

        lane = lax.rem(group, SLOTS)
        pltpu.make_async_copy(tiles_ref.at[pl.ds(0, UNROLL)], held.at[lane], sems.at[lane]).wait()
        for step in range(UNROLL):
            row = row_ref[kept, group * UNROLL + step]
            col = col_ref[kept, group * UNROLL + step]
            product = jnp.dot(
                held[lane, step],
                x_ref[pl.ds(pl.multiple_of(col * edge, edge), edge), :],
                preferred_element_type=F32,
            )
            totals[pl.ds(pl.multiple_of(row * edge, edge), edge), :] += product
        return carry

    lax.fori_loop(0, groups, add_group, 0)
    rows = out_refs[0].shape[0]
    for stream, out_ref in enumerate(out_refs):
        out_ref[...] = totals[stream * rows : (stream + 1) * rows, :].astype(BF16)


def tile_products(kept, plan, x, tiles, row_tiles):
    _, edge, _ = tiles.shape
    width = x.shape[1]
    half = row_tiles // 2 * edge
    return pl.pallas_call(
        functools.partial(tile_kernel, kept),
        out_shape=[jax.ShapeDtypeStruct((half // STREAMS, width), BF16)] * STREAMS,
        in_specs=[SMEM] * 4 + [VMEM, pl.BlockSpec(memory_space=pl.ANY)],
        out_specs=[VMEM] * STREAMS,
        scratch_shapes=[
            pltpu.VMEM((SLOTS, UNROLL, edge, edge), BF16),
            pltpu.VMEM((half + edge, width), F32),
            pltpu.SemaphoreType.DMA((SLOTS,)),
        ],
        compiler_params=params(32),
        cost_estimate=pl.CostEstimate(
            flops=40_000_000_000, bytes_accessed=40_000_000, transcendentals=0
        ),
        name="tile_products",
    )(*plan, x, tiles)


def wide(ref, start, rows):
    return ref[start : start + rows, :].astype(F32)


def forward_kernel(*refs):
    for stream in range(STREAMS):
        kept, got, out = refs[2 * stream], refs[2 * stream + 1], refs[2 * STREAMS + stream]
        rows = out.shape[0]
        out[...] = (wide(kept, rows, rows) + wide(got, rows, rows)).astype(BF16)


def forward_sums(kept, got):
    pairs = [array for pair in zip(kept, got) for array in pair]
    out = jax.ShapeDtypeStruct((kept[0].shape[0] // 2, kept[0].shape[1]), BF16)
    return pl.pallas_call(
        forward_kernel,
        out_shape=[out] * STREAMS,
        in_specs=[VMEM] * len(pairs),
        out_specs=[VMEM] * STREAMS,
        compiler_params=params(32),
        name="forward_sums",
    )(*pairs)


def turn_kernel(*refs):
    for stream in range(STREAMS):
        kept, got, last = refs[3 * stream : 3 * stream + 3]
        keep, send = refs[3 * STREAMS + 2 * stream : 3 * STREAMS + 2 * stream + 2]
        rows = last.shape[0] // 2
        for out, start in ((keep, 0), (send, rows)):
            total = wide(kept, start, rows) + wide(got, start, rows) + wide(last, start, rows)
            out[...] = total.astype(out.dtype)


def turn_sums(kept, got, last):
    ins = [array for three in zip(kept, got, last) for array in three]
    rows, width = last[0].shape
    outs = [
        jax.ShapeDtypeStruct((rows // 2, width), F32),
        jax.ShapeDtypeStruct((rows // 2, width), BF16),
    ] * STREAMS
    done = pl.pallas_call(
        turn_kernel,
        out_shape=outs,
        in_specs=[VMEM] * len(ins),
        out_specs=[VMEM] * len(outs),
        compiler_params=params(32),
        name="turn_sums",
    )(*ins)
    return done[0::2], done[1::2]


def dense_kernel(*refs):
    weight_ref, bias_ref, out_ref = refs[3 * STREAMS :]
    for stream in range(STREAMS):
        kept, got, last = refs[3 * stream : 3 * stream + 3]
        rows = last.shape[0]
        total = wide(kept, 0, rows) + wide(got, 0, rows) + wide(last, 0, rows)
        hidden = jnp.dot(total.astype(BF16), weight_ref[...], preferred_element_type=F32)
        hidden = jnp.maximum(hidden + bias_ref[...], 0.0)
        out_ref[stream * rows : (stream + 1) * rows, :] = hidden.astype(BF16)


def dense(kept, got, last, weight, bias):
    ins = [array for three in zip(kept, got, last) for array in three]
    rows = last[0].shape[0] * STREAMS
    return pl.pallas_call(
        dense_kernel,
        out_shape=jax.ShapeDtypeStruct((rows, weight.shape[1]), BF16),
        in_specs=[VMEM] * (len(ins) + 2),
        out_specs=VMEM,
        compiler_params=params(32),
        name="dense",
    )(*ins, weight, bias.reshape(1, -1))


def swap(arrays, axes, first):
    out = []
    for stream, array in enumerate(arrays):
        bits = (1, 3) if stream % 2 == 0 else (3, 1)
        bit = bits[0] if first else bits[1]
        axis = axes[0] if stream < 2 else axes[1]
        out.append(lax.ppermute(array, axis, [(c, c ^ bit) for c in range(SIDE)]))
    return out


def body(features, new_index, tile_values, tile_index, tile_count, weight, bias):
    grid_rows = lax.axis_size("y") * lax.axis_size("core")
    grid_cols = lax.axis_size("x") * lax.axis_size("z")
    local_rows = features.shape[0]
    everyone = ("y", "core", "x", "z")
    capacity = 2 * local_rows // (grid_rows * grid_cols)
    tiles = tile_values[0, 0]
    row_tiles = local_rows * grid_cols // tiles.shape[1]
    assert row_tiles == 256 and grid_cols == SIDE * SIDE

    me = jnp.stack([lax.axis_index("x"), lax.axis_index("z")]).astype(jnp.int32)
    plan = plan_tiles(me, tile_count.reshape(1), tile_index[0, 0], row_tiles)
    packed = pack_rows(new_index, features, grid_rows, grid_cols, capacity)
    got = lax.all_to_all(packed, everyone, split_axis=0, concat_axis=0, tiled=True)
    moved_rows = place_rows(got, local_rows)
    column_block = lax.all_gather(moved_rows, ("y", "core"), axis=0, tiled=True)

    sent = tile_products(0, plan, column_block, tiles, row_tiles)
    got_1 = swap(sent, ("x", "z"), True)
    kept = tile_products(1, plan, column_block, tiles, row_tiles)
    got_2 = swap(forward_sums(kept, got_1), ("x", "z"), False)
    keep, send = turn_sums(kept, got_1, got_2)
    got_3 = swap(send, ("z", "x"), True)
    got_4 = swap(forward_sums(keep, got_3), ("z", "x"), False)
    return dense(keep, got_3, got_4, weight, bias)


def solution(mesh):
    fine = Mesh(mesh.devices.reshape(-1, 2, SIDE, SIDE), ("y", "core", "x", "z"))
    grid = (("y", "core"), ("x", "z"))
    flat = ("y", "core", "x", "z")
    in_specs = (
        P(flat, None),
        P(flat),
        P(*grid, None, None, None),
        P(*grid, None, None),
        P(*grid),
        P(),
        P(),
    )
    return jax.shard_map(
        body, mesh=fine, in_specs=in_specs, out_specs=P(flat, None), check_vma=False
    )
```

time: 437 us -> 178 us (0.41)
  waiting for transfers between devices: 307 us -> 64 us
  other arithmetic: 40.9 us -> 0.6 us
  local copies, waits for them, and re-layouts: 42.8 us -> 6.67 us
  blocking collectives: 0 us -> 32.7 us
  Pallas kernels: 0 us -> 31.3 us
  matrix products: 11 us -> 0 us
  starting transfers between devices: 18.7 us -> 27.9 us
    reduce_scatter x1 -> x0, waiting for transfers between devices: 260 us -> none  [body(): lax.psum_scatter(partial_rows.astype(jnp.bfloat16), 'col', scatter_dimens...]
    ppermute x0 -> x16, waiting for transfers between devices: none -> 42.4 us  [swap(): out.append(lax.ppermute(array, axis, [(c, c ^ bit) for c in range(SIDE)]))]
    all_to_all x0 -> x1, blocking collectives: none -> 32.7 us  [body(): lax.all_to_all(packed, everyone, split_axis=0, concat_axis=0, tiled=True)]
    pallas_call x0 -> x9, Pallas kernels: none -> 31.3 us  [the longest x1 10.2 us: pack_rows(): pl.pallas_call(functools.partial(pack_kernel, grid_rows, grid_cols, capac...]
    ppermute x0 -> x16, starting transfers between devices: none -> 27.9 us  [swap(): out.append(lax.ppermute(array, axis, [(c, c ^ bit) for c in range(SIDE)]))]
    scatter-add x2 -> x0, other arithmetic: 27.3 us -> none  [add_tiles(): return totals.at[part_rows].add(products)]
    all_to_all x2 -> x0, waiting for transfers between devices: 19.8 us -> none  [the longest x1 17.4 us: body(): lax.all_to_all(outgoing, ('row', 'col'), split_axis=0, concat_axis=0, til...]
    all_to_all x2 -> x0, starting transfers between devices: 18.6 us -> none  [the longest x1 11.1 us: body(): lax.all_to_all(slots_out, ('row', 'col'), split_axis=0, concat_axis=0, ti...]
  transfers between devices with their start and end apart: 4 -> 17, of which waited for: 4 -> 16; matrix products, arithmetic and copies ran while one was open for 2% -> 0% of each run, Pallas kernels for 0% -> 5%
where the time goes in v2:
time: 178 us; the launch traced here: 177 us
  waiting for transfers between devices  64 us (36%)
  blocking collectives  32.7 us (18%)
  Pallas kernels  31.3 us (18%)
  starting transfers between devices  27.9 us (16%)
  between operations  14.1 us (8%)
  local copies, waits for them, and re-layouts  6.67 us (4%)
    ppermute x16, waiting for transfers between devices, swap(): out.append(lax.ppermute(array, axis, [(c, c ^ bit) for c in range(SIDE)]))  42.4 us
    all_to_all x1, blocking collectives, body(): lax.all_to_all(packed, everyone, split_axis=0, concat_axis=0, tiled=True)  32.7 us
    ppermute x16, starting transfers between devices, swap(): out.append(lax.ppermute(array, axis, [(c, c ^ bit) for c in range(SIDE)]))  27.9 us
    all_gather x1, waiting for transfers between devices, body(): column_block = lax.all_gather(moved_rows, ('y', 'core'), axis=0, tiled=True)  21.5 us
    pallas_call x1, Pallas kernels, pack_rows(): pl.pallas_call(functools.partial(pack_kernel, grid_rows, grid_cols, capac...  10.2 us
    unnamed x18, local copies, waits for them, and re-layouts  6.67 us
    pallas_call x1, Pallas kernels, place_rows(): pl.pallas_call(place_kernel, out_shape=jax.ShapeDtypeStruct((local_rows,...  6.67 us
    pallas_call x2, Pallas kernels, tile_products(): pl.pallas_call(functools.partial(tile_kernel, kept), out_shape=[jax.Shape...  6.53 us
  transfers between devices with their start and end apart: 17, of which 16 were waited for; matrix products, arithmetic and copies ran while one was open for 0% of the time, Pallas kernels for 5%

profile of v2, /device:TPU:0, one launch (start us, length us, event | category | flops | bytes accessed | tf_op | source)
XLA Modules:
  0.0 177.3 jit_solution(11089761597255843470)
XLA Ops:
  6.5 1.0 copy-done
  7.6 0.7 copy-done.2
  8.3 10.2 %pack_rows.1 = bf16[128,40,128]{2,1,0:T(8,128)(2,1)S(1)} custom-call(s32[16,128]{1,0:T(8,128)S(1)} %bitcast.8, bf16[2048,128]{1,0:T(8,128)(2,1)S(1)} %copy-done), custom_call_target="tpu_custom_call" | custom-call | tf_op jit(solution)/shard_map/pack_rows/pallas_call | solution.py:87
  18.5 32.7 %all_to_all.5.in_ref = bf16[128,40,128]{2,1,0:T(8,128)(2,1)S(1)} all-to-all(bf16[128,40,128]{2,1,0:T(8,128)(2,1)S(1)} %pack_rows.1), channel_id=1, replica_groups=mesh['y'=4,'core'=2,'x'=4,'z'=4] {'y','core','x','z'}, dimensions={0} | all-to-all | bytes 2621440 | tf_op jit(solution)/shard_map/all_to_all | solution.py:349
  51.2 6.7 %place_rows.1 = bf16[2048,128]{1,0:T(8,128)(2,1)} custom-call(bf16[128,40,128]{2,1,0:T(8,128)(2,1)S(1)} %all_to_all.5.in_ref), custom_call_target="tpu_custom_call" | custom-call | tf_op jit(solution)/shard_map/place_rows/pallas_call | solution.py:124
  58.6 0.6 pad_add_fusion.me_ref
  59.2 5.0 %plan_tiles.1 = (s32[2,656]{1,0:T(2,128)}, s32[2,656]{1,0:T(2,128)}, s32[2,656]{1,0:T(2,128)}, s32[2]{0:T(128)}) custom-call(s32[2]{0:T(128)} %pad_add_fusion.me_ref, s32[1]{0:T(128)} %bitcast.7.count_ref, s32[2,640]{1,0:T(2,128)} %bitcast.10), custom_call_target="tpu_custom_call" | custom-call | tf_op jit(solution)/shard_map/plan_tiles/pallas_call | solution.py:176
  64.2 21.5 %all-gather.2.cloned.1.call-done.x_ref = bf16[16384,128]{1,0:T(8,128)(2,1)} async-done(((bf16[2048,128]{1,0:T(8,128)(2,1)}), bf16[16384,128]{1,0:T(8,128)(2,1)}) %all-gather.2.cloned.1.call-update) | async-done | bytes 4194320 | tf_op jit(solution)/shard_map/all_gather | solution.py:351
  85.7 2.2 %copy-done.4 = bf16[16384,128]{1,0:T(8,128)(2,1)S(1)} copy-done((bf16[16384,128]{1,0:T(8,128)(2,1)S(1)}, bf16[16384,128]{1,0:T(8,128)(2,1)}, u32[]{:S(2)}) %copy-start.4) | copy-done | bytes 4194328
  87.9 0.7 copy-done.5
  88.6 0.7 copy-done.6
  89.3 0.7 copy-done.7
  90.0 0.7 copy-done.8
  90.6 3.3 %tile_products.3 = (bf16[4096,128]{1,0:T(8,128)(2,1)S(1)}, bf16[4096,128]{1,0:T(8,128)(2,1)S(1)}, bf16[4096,128]{1,0:T(8,128)(2,1)S(1)}, bf16[4096,128]{1,0:T(8,128)(2,1)S(1)}) custom-call(s32[2,656]{1,0:T(2,128)S(1)} %copy-done.5, s32[2,656]{1,0:T(2,128)S(1)} %copy-done.6, s32[2,656]{1,0:T(2,128)S(1)} %copy-done.7, s32[2]{0:T(128)S(1)} %copy-done.8, ...), custom_call_target="tpu_custom_call" | custom-call | flops 40000000000 | bytes 40000000 | tf_op jit(solution)/shard_map/tile_products/pallas_call | solution.py:232
  93.9 4.0 %collective-permute-start = (bf16[4096,128]{1,0:T(8,128)(2,1)S(1)}, bf16[4096,128]{1,0:T(8,128)(2,1)S(1)}, u32[]{:S(2)}, u32[]{:S(2)}) collective-permute-start(bf16[4096,128]{1,0:T(8,128)(2,1)S(1)} %get-tuple-element.38), channel_id=1, source_target_pairs={{0,4},{4,0},{8,12},{12,8},{1,5},{5,1},{9,13},{13,9},{2,6},{6,2},{1... | collective-permute-start | bytes 3145736 | tf_op jit(solution)/shard_map/ppermute | solution.py:332
  97.9 2.1 %collective-permute-start.1 = (bf16[4096,128]{1,0:T(8,128)(2,1)S(1)}, bf16[4096,128]{1,0:T(8,128)(2,1)S(1)}, u32[]{:S(2)}, u32[]{:S(2)}) collective-permute-start(bf16[4096,128]{1,0:T(8,128)(2,1)S(1)} %get-tuple-element.40), channel_id=1, source_target_pairs={{0,12},{4,8},{8,4},{12,0},{1,13},{5,9},{9,5},{13,1},{2,14},{6,10},... | collective-permute-start | bytes 3145736 | tf_op jit(solution)/shard_map/ppermute | solution.py:332
  100.0 4.1 %collective-permute-start.2 = (bf16[4096,128]{1,0:T(8,128)(2,1)S(1)}, bf16[4096,128]{1,0:T(8,128)(2,1)S(1)}, u32[]{:S(2)}, u32[]{:S(2)}) collective-permute-start(bf16[4096,128]{1,0:T(8,128)(2,1)S(1)} %get-tuple-element.42), channel_id=1, source_target_pairs={{0,1},{1,0},{2,3},{3,2},{4,5},{5,4},{6,7},{7,6},{8,9},{9,8},{10,11... | collective-permute-start | bytes 3145736 | tf_op jit(solution)/shard_map/ppermute | solution.py:332
  104.1 3.7 %collective-permute-start.3 = (bf16[4096,128]{1,0:T(8,128)(2,1)S(1)}, bf16[4096,128]{1,0:T(8,128)(2,1)S(1)}, u32[]{:S(2)}, u32[]{:S(2)}) collective-permute-start(bf16[4096,128]{1,0:T(8,128)(2,1)S(1)} %get-tuple-element.44), channel_id=1, source_target_pairs={{0,3},{1,2},{2,1},{3,0},{4,7},{5,6},{6,5},{7,4},{8,11},{9,10},{10,... | collective-permute-start | bytes 3145736 | tf_op jit(solution)/shard_map/ppermute | solution.py:332
  107.8 3.3 %tile_products.2 = (bf16[4096,128]{1,0:T(8,128)(2,1)S(1)}, bf16[4096,128]{1,0:T(8,128)(2,1)S(1)}, bf16[4096,128]{1,0:T(8,128)(2,1)S(1)}, bf16[4096,128]{1,0:T(8,128)(2,1)S(1)}) custom-call(s32[2,656]{1,0:T(2,128)S(1)} %copy-done.5, s32[2,656]{1,0:T(2,128)S(1)} %copy-done.6, s32[2,656]{1,0:T(2,128)S(1)} %copy-done.7, s32[2]{0:T(128)S(1)} %copy-done.8, ...), custom_call_target="tpu_custom_call" | custom-call | flops 40000000000 | bytes 40000000 | tf_op jit(solution)/shard_map/tile_products/pallas_call | solution.py:232
  111.0 7.0 %collective-permute-done.refs_1_ = bf16[4096,128]{1,0:T(8,128)(2,1)S(1)} collective-permute-done((bf16[4096,128]{1,0:T(8,128)(2,1)S(1)}, bf16[4096,128]{1,0:T(8,128)(2,1)S(1)}, u32[]{:S(2)}, u32[]{:S(2)}) %collective-permute-start) | collective-permute-done | bytes 1048608 | tf_op jit(solution)/shard_map/ppermute | solution.py:332
  118.0 4.1 %collective-permute-done.1.refs_3_.refs_4_ = bf16[4096,128]{1,0:T(8,128)(2,1)S(1)} collective-permute-done((bf16[4096,128]{1,0:T(8,128)(2,1)S(1)}, bf16[4096,128]{1,0:T(8,128)(2,1)S(1)}, u32[]{:S(2)}, u32[]{:S(2)}) %collective-permute-start.1) | collective-permute-done | bytes 1048608 | tf_op jit(solution)/shard_map/ppermute | solution.py:332
  122.1 5.6 %collective-permute-done.2.refs_5_.refs_7_ = bf16[4096,128]{1,0:T(8,128)(2,1)S(1)} collective-permute-done((bf16[4096,128]{1,0:T(8,128)(2,1)S(1)}, bf16[4096,128]{1,0:T(8,128)(2,1)S(1)}, u32[]{:S(2)}, u32[]{:S(2)}) %collective-permute-start.2) | collective-permute-done | bytes 1048608 | tf_op jit(solution)/shard_map/ppermute | solution.py:332
  127.7 3.6 %collective-permute-done.3.refs_7_.refs_10_ = bf16[4096,128]{1,0:T(8,128)(2,1)S(1)} collective-permute-done((bf16[4096,128]{1,0:T(8,128)(2,1)S(1)}, bf16[4096,128]{1,0:T(8,128)(2,1)S(1)}, u32[]{:S(2)}, u32[]{:S(2)}) %collective-permute-start.3) | collective-permute-done | bytes 1048608 | tf_op jit(solution)/shard_map/ppermute | solution.py:332
  131.3 0.5 forward_sums.2
  131.8 0.4 collective-permute-start.4
  132.2 0.2 collective-permute-start.5
  132.3 2.2 %collective-permute-start.6 = (bf16[2048,128]{1,0:T(8,128)(2,1)S(1)}, bf16[2048,128]{1,0:T(8,128)(2,1)S(1)}, u32[]{:S(2)}, u32[]{:S(2)}) collective-permute-start(bf16[2048,128]{1,0:T(8,128)(2,1)S(1)} %get-tuple-element.47), channel_id=1, source_target_pairs={{0,3},{1,2},{2,1},{3,0},{4,7},{5,6},{6,5},{7,4},{8,11},{9,10},{10,... | collective-permute-start | bytes 1572872 | tf_op jit(solution)/shard_map/ppermute | solution.py:332
  134.6 12.1 %collective-permute-done.4.refs_2_ = bf16[2048,128]{1,0:T(8,128)(2,1)S(1)} collective-permute-done((bf16[2048,128]{1,0:T(8,128)(2,1)S(1)}, bf16[2048,128]{1,0:T(8,128)(2,1)S(1)}, u32[]{:S(2)}, u32[]{:S(2)}) %collective-permute-start.4) | collective-permute-done | bytes 524320 | tf_op jit(solution)/shard_map/ppermute | solution.py:332
  146.7 0.2 collective-permute-done.6.refs_8_
  146.8 0.2 collective-permute-done.7.refs_11_
  147.1 0.8 turn_sums.1
  147.9 0.4 collective-permute-start.8
  148.3 1.5 collective-permute-start.9
  149.8 1.7 collective-permute-start.10
  151.4 2.9 %collective-permute-start.11 = (bf16[1024,128]{1,0:T(8,128)(2,1)S(1)}, bf16[1024,128]{1,0:T(8,128)(2,1)S(1)}, u32[]{:S(2)}, u32[]{:S(2)}) collective-permute-start(bf16[1024,128]{1,0:T(8,128)(2,1)S(1)} %get-tuple-element.56), channel_id=1, source_target_pairs={{0,12},{4,8},{8,4},{12,0},{1,13},{5,9},{9,5},{13,1},{2,14},{6,10},... | collective-permute-start | bytes 786440 | tf_op jit(solution)/shard_map/ppermute | solution.py:332
  154.3 0.3 collective-permute-done.8.refs_1_
  154.6 1.3 collective-permute-done.9.refs_3_.refs_4_
  155.9 0.2 collective-permute-done.10.refs_5_.refs_7_
  156.2 2.9 %collective-permute-done.11.refs_7_.refs_10_ = bf16[1024,128]{1,0:T(8,128)(2,1)S(1)} collective-permute-done((bf16[1024,128]{1,0:T(8,128)(2,1)S(1)}, bf16[1024,128]{1,0:T(8,128)(2,1)S(1)}, u32[]{:S(2)}, u32[]{:S(2)}) %collective-permute-start.11) | collective-permute-done | bytes 262176 | tf_op jit(solution)/shard_map/ppermute | solution.py:332
  159.0 0.1 forward_sums.3
  159.1 1.4 collective-permute-start.12
  160.5 0.7 collective-permute-start.13
  161.2 2.9 %collective-permute-start.14 = (bf16[512,128]{1,0:T(8,128)(2,1)S(1)}, bf16[512,128]{1,0:T(8,128)(2,1)S(1)}, u32[]{:S(2)}, u32[]{:S(2)}) collective-permute-start(bf16[512,128]{1,0:T(8,128)(2,1)S(1)} %get-tuple-element.59), channel_id=1, source_target_pairs={{0,12},{4,8},{8,4},{12,0},{1,13},{5,9},{9,5},{13,1},{2,14},{6,10},... | collective-permute-start | bytes 393224 | tf_op jit(solution)/shard_map/ppermute | solution.py:332
  164.1 1.3 collective-permute-done.12.refs_2_
  165.4 0.1 collective-permute-done.13.refs_5_
  165.5 1.9 %collective-permute-done.14.refs_8_ = bf16[512,128]{1,0:T(8,128)(2,1)S(1)} collective-permute-done((bf16[512,128]{1,0:T(8,128)(2,1)S(1)}, bf16[512,128]{1,0:T(8,128)(2,1)S(1)}, u32[]{:S(2)}, u32[]{:S(2)}) %collective-permute-start.14) | collective-permute-done | bytes 131104 | tf_op jit(solution)/shard_map/ppermute | solution.py:332
  167.4 1.7 collective-permute-done.15.refs_11_
  169.1 1.4 dense.1
  (16 shorter events, 0.0 us)
Async XLA Ops:
  6.5 79.2 %all-gather.2.cloned.1.call-start = ((), (), s32[]{:S(2)}) async-start(), calls=%async_computation.1 | async-start | bytes 4718592 | tf_op jit(solution)/shard_map/all_gather | solution.py:351
  6.5 1.0 copy-start
  7.6 0.7 copy-start.2
  85.7 2.2 %copy-start.4 = (bf16[16384,128]{1,0:T(8,128)(2,1)S(1)}, bf16[16384,128]{1,0:T(8,128)(2,1)}, u32[]{:S(2)}) copy-start(bf16[16384,128]{1,0:T(8,128)(2,1)} %all-gather.2.cloned.1.call-done.x_ref) | copy-start | bytes 12582916
  87.9 0.7 copy-start.5
  88.6 0.7 copy-start.6
  89.3 0.7 copy-start.7
  90.0 0.7 copy-start.8
  93.9 24.1 %collective-permute-start = (bf16[4096,128]{1,0:T(8,128)(2,1)S(1)}, bf16[4096,128]{1,0:T(8,128)(2,1)S(1)}, u32[]{:S(2)}, u32[]{:S(2)}) collective-permute-start(bf16[4096,128]{1,0:T(8,128)(2,1)S(1)} %get-tuple-element.38), channel_id=1, source_target_pairs={{0,4},{4,0},{8,12},{12,8},{1,5},{5,1},{9,13},{13,9},{2,6},{6,2},{1... | collective-permute-start | bytes 3145736 | tf_op jit(solution)/shard_map/ppermute | solution.py:332
  97.9 24.2 %collective-permute-start.1 = (bf16[4096,128]{1,0:T(8,128)(2,1)S(1)}, bf16[4096,128]{1,0:T(8,128)(2,1)S(1)}, u32[]{:S(2)}, u32[]{:S(2)}) collective-permute-start(bf16[4096,128]{1,0:T(8,128)(2,1)S(1)} %get-tuple-element.40), channel_id=1, source_target_pairs={{0,12},{4,8},{8,4},{12,0},{1,13},{5,9},{9,5},{13,1},{2,14},{6,10},... | collective-permute-start | bytes 3145736 | tf_op jit(solution)/shard_map/ppermute | solution.py:332
  100.0 27.7 %collective-permute-start.2 = (bf16[4096,128]{1,0:T(8,128)(2,1)S(1)}, bf16[4096,128]{1,0:T(8,128)(2,1)S(1)}, u32[]{:S(2)}, u32[]{:S(2)}) collective-permute-start(bf16[4096,128]{1,0:T(8,128)(2,1)S(1)} %get-tuple-element.42), channel_id=1, source_target_pairs={{0,1},{1,0},{2,3},{3,2},{4,5},{5,4},{6,7},{7,6},{8,9},{9,8},{10,11... | collective-permute-start | bytes 3145736 | tf_op jit(solution)/shard_map/ppermute | solution.py:332
  104.1 27.2 %collective-permute-start.3 = (bf16[4096,128]{1,0:T(8,128)(2,1)S(1)}, bf16[4096,128]{1,0:T(8,128)(2,1)S(1)}, u32[]{:S(2)}, u32[]{:S(2)}) collective-permute-start(bf16[4096,128]{1,0:T(8,128)(2,1)S(1)} %get-tuple-element.44), channel_id=1, source_target_pairs={{0,3},{1,2},{2,1},{3,0},{4,7},{5,6},{6,5},{7,4},{8,11},{9,10},{10,... | collective-permute-start | bytes 3145736 | tf_op jit(solution)/shard_map/ppermute | solution.py:332
  131.8 14.8 %collective-permute-start.4 = (bf16[2048,128]{1,0:T(8,128)(2,1)S(1)}, bf16[2048,128]{1,0:T(8,128)(2,1)S(1)}, u32[]{:S(2)}, u32[]{:S(2)}) collective-permute-start(bf16[2048,128]{1,0:T(8,128)(2,1)S(1)} %get-tuple-element.45), channel_id=1, source_target_pairs={{0,12},{4,8},{8,4},{12,0},{1,13},{5,9},{9,5},{13,1},{2,14},{6,10},... | collective-permute-start | bytes 1572872 | tf_op jit(solution)/shard_map/ppermute | solution.py:332
  132.2 14.5 %collective-permute-start.5 = (bf16[2048,128]{1,0:T(8,128)(2,1)S(1)}, bf16[2048,128]{1,0:T(8,128)(2,1)S(1)}, u32[]{:S(2)}, u32[]{:S(2)}) collective-permute-start(bf16[2048,128]{1,0:T(8,128)(2,1)S(1)} %get-tuple-element.46), channel_id=1, source_target_pairs={{0,4},{4,0},{8,12},{12,8},{1,5},{5,1},{9,13},{13,9},{2,6},{6,2},{1... | collective-permute-start | bytes 1572872 | tf_op jit(solution)/shard_map/ppermute | solution.py:332
  132.3 14.5 %collective-permute-start.6 = (bf16[2048,128]{1,0:T(8,128)(2,1)S(1)}, bf16[2048,128]{1,0:T(8,128)(2,1)S(1)}, u32[]{:S(2)}, u32[]{:S(2)}) collective-permute-start(bf16[2048,128]{1,0:T(8,128)(2,1)S(1)} %get-tuple-element.47), channel_id=1, source_target_pairs={{0,3},{1,2},{2,1},{3,0},{4,7},{5,6},{6,5},{7,4},{8,11},{9,10},{10,... | collective-permute-start | bytes 1572872 | tf_op jit(solution)/shard_map/ppermute | solution.py:332
  134.6 34.5 %copy-start.1 = (bf16[128,256]{1,0:T(8,128)(2,1)S(1)}, bf16[128,256]{1,0:T(8,128)(2,1)}, u32[]{:S(2)}) copy-start(bf16[128,256]{1,0:T(8,128)(2,1)} %refs_12_.1) | copy-start | bytes 196612
  134.6 34.5 %copy-start.3 = (f32[256]{0:T(256)S(1)}, f32[256]{0:T(256)}, u32[]{:S(2)}) copy-start(f32[256]{0:T(256)} %param.13) | copy-start | bytes 3076
  134.6 12.5 %collective-permute-start.7 = (bf16[2048,128]{1,0:T(8,128)(2,1)S(1)}, bf16[2048,128]{1,0:T(8,128)(2,1)S(1)}, u32[]{:S(2)}, u32[]{:S(2)}) collective-permute-start(bf16[2048,128]{1,0:T(8,128)(2,1)S(1)} %get-tuple-element.48), channel_id=1, source_target_pairs={{0,1},{1,0},{2,3},{3,2},{4,5},{5,4},{6,7},{7,6},{8,9},{9,8},{10,11... | collective-permute-start | bytes 1572872 | tf_op jit(solution)/shard_map/ppermute | solution.py:332
  147.9 6.7 %collective-permute-start.8 = (bf16[1024,128]{1,0:T(8,128)(2,1)S(1)}, bf16[1024,128]{1,0:T(8,128)(2,1)S(1)}, u32[]{:S(2)}, u32[]{:S(2)}) collective-permute-start(bf16[1024,128]{1,0:T(8,128)(2,1)S(1)} %get-tuple-element.50), channel_id=1, source_target_pairs={{0,1},{1,0},{2,3},{3,2},{4,5},{5,4},{6,7},{7,6},{8,9},{9,8},{10,11... | collective-permute-start | bytes 786440 | tf_op jit(solution)/shard_map/ppermute | solution.py:332
  148.3 7.6 %collective-permute-start.9 = (bf16[1024,128]{1,0:T(8,128)(2,1)S(1)}, bf16[1024,128]{1,0:T(8,128)(2,1)S(1)}, u32[]{:S(2)}, u32[]{:S(2)}) collective-permute-start(bf16[1024,128]{1,0:T(8,128)(2,1)S(1)} %get-tuple-element.52), channel_id=1, source_target_pairs={{0,3},{1,2},{2,1},{3,0},{4,7},{5,6},{6,5},{7,4},{8,11},{9,10},{10,... | collective-permute-start | bytes 786440 | tf_op jit(solution)/shard_map/ppermute | solution.py:332
  149.8 6.4 %collective-permute-start.10 = (bf16[1024,128]{1,0:T(8,128)(2,1)S(1)}, bf16[1024,128]{1,0:T(8,128)(2,1)S(1)}, u32[]{:S(2)}, u32[]{:S(2)}) collective-permute-start(bf16[1024,128]{1,0:T(8,128)(2,1)S(1)} %get-tuple-element.54), channel_id=1, source_target_pairs={{0,4},{4,0},{8,12},{12,8},{1,5},{5,1},{9,13},{13,9},{2,6},{6,2},{1... | collective-permute-start | bytes 786440 | tf_op jit(solution)/shard_map/ppermute | solution.py:332
  151.4 7.6 %collective-permute-start.11 = (bf16[1024,128]{1,0:T(8,128)(2,1)S(1)}, bf16[1024,128]{1,0:T(8,128)(2,1)S(1)}, u32[]{:S(2)}, u32[]{:S(2)}) collective-permute-start(bf16[1024,128]{1,0:T(8,128)(2,1)S(1)} %get-tuple-element.56), channel_id=1, source_target_pairs={{0,12},{4,8},{8,4},{12,0},{1,13},{5,9},{9,5},{13,1},{2,14},{6,10},... | collective-permute-start | bytes 786440 | tf_op jit(solution)/shard_map/ppermute | solution.py:332
  159.1 6.3 %collective-permute-start.12 = (bf16[512,128]{1,0:T(8,128)(2,1)S(1)}, bf16[512,128]{1,0:T(8,128)(2,1)S(1)}, u32[]{:S(2)}, u32[]{:S(2)}) collective-permute-start(bf16[512,128]{1,0:T(8,128)(2,1)S(1)} %get-tuple-element.57), channel_id=1, source_target_pairs={{0,3},{1,2},{2,1},{3,0},{4,7},{5,6},{6,5},{7,4},{8,11},{9,10},{10,... | collective-permute-start | bytes 393224 | tf_op jit(solution)/shard_map/ppermute | solution.py:332
  160.5 5.0 %collective-permute-start.13 = (bf16[512,128]{1,0:T(8,128)(2,1)S(1)}, bf16[512,128]{1,0:T(8,128)(2,1)S(1)}, u32[]{:S(2)}, u32[]{:S(2)}) collective-permute-start(bf16[512,128]{1,0:T(8,128)(2,1)S(1)} %get-tuple-element.58), channel_id=1, source_target_pairs={{0,1},{1,0},{2,3},{3,2},{4,5},{5,4},{6,7},{7,6},{8,9},{9,8},{10,11... | collective-permute-start | bytes 393224 | tf_op jit(solution)/shard_map/ppermute | solution.py:332
  161.2 6.2 %collective-permute-start.14 = (bf16[512,128]{1,0:T(8,128)(2,1)S(1)}, bf16[512,128]{1,0:T(8,128)(2,1)S(1)}, u32[]{:S(2)}, u32[]{:S(2)}) collective-permute-start(bf16[512,128]{1,0:T(8,128)(2,1)S(1)} %get-tuple-element.59), channel_id=1, source_target_pairs={{0,12},{4,8},{8,4},{12,0},{1,13},{5,9},{9,5},{13,1},{2,14},{6,10},... | collective-permute-start | bytes 393224 | tf_op jit(solution)/shard_map/ppermute | solution.py:332
  164.1 5.0 %collective-permute-start.15 = (bf16[512,128]{1,0:T(8,128)(2,1)S(1)}, bf16[512,128]{1,0:T(8,128)(2,1)S(1)}, u32[]{:S(2)}, u32[]{:S(2)}) collective-permute-start(bf16[512,128]{1,0:T(8,128)(2,1)S(1)} %get-tuple-element.60), channel_id=1, source_target_pairs={{0,4},{4,0},{8,12},{12,8},{1,5},{5,1},{9,13},{13,9},{2,6},{6,2},{1... | collective-permute-start | bytes 393224 | tf_op jit(solution)/shard_map/ppermute | solution.py:332
Sparse Core Ops, SparseCore 0:
  58.0 27.6 all-gather.1

commit v3 on v2

v3 whole, which is shorter than its diff:
```python
import functools

import jax
import jax.numpy as jnp
from jax import lax
from jax.experimental import pallas as pl
from jax.experimental.pallas import tpu as pltpu
from jax.sharding import Mesh
from jax.sharding import PartitionSpec as P

EXTRA = 8
PICK = 1024
UNROLL = 16
SLOTS = 6
STREAMS = 4
PAIR = 2
SIDE = 4
LANES = 128
F32 = jnp.float32
BF16 = jnp.bfloat16


def iota(shape, axis):
    return lax.broadcasted_iota(jnp.int32, shape, axis)


def log2(size):
    assert size & (size - 1) == 0
    return size.bit_length() - 1


def params(mib, **rest):
    return pltpu.CompilerParams(vmem_limit_bytes=mib << 20, **rest)


VMEM = pl.BlockSpec(memory_space=pltpu.VMEM)
SMEM = pl.BlockSpec(memory_space=pltpu.SMEM)
HBM = pl.BlockSpec(memory_space=pltpu.HBM)


def pack_kernel(
    grid_rows,
    grid_cols,
    capacity,
    index_hbm,
    rows_hbm,
    out_ref,
    index_ref,
    rows_ref,
    hits_ref,
    marks_ref,
    sems,
):
    local_rows, width = rows_ref.shape
    index_copy = pltpu.make_async_copy(index_hbm, index_ref, sems.at[0])
    index_copy.start()
    copy = pltpu.make_async_copy(rows_hbm, rows_ref, sems.at[1])
    copy.start()
    peers = grid_rows * grid_cols
    lanes = (LANES, 2 * LANES)
    earlier = jnp.where(iota(lanes, 0) < iota(lanes, 1), 1.0, 0.0).astype(BF16)
    rank_lane = iota((LANES, LANES), 0) & (capacity - 1)
    seen = jnp.zeros((peers, LANES), F32)
    zero = jnp.zeros((LANES, LANES), F32)
    places = []
    index_copy.wait()
    for block in range(local_rows // LANES):
        here = slice(block * LANES, (block + 1) * LANES)
        index = index_ref[block : block + 1, :]
        owner = index >> log2(local_rows)
        slot = index & (local_rows - 1)
        row = owner & (grid_rows - 1)
        peer = ((row & 1) * (grid_rows // 2) + (row >> 1)) * grid_cols + (owner >> log2(grid_rows))
        hit = jnp.where(iota((peers, LANES), 0) == peer, 1.0, 0.0)
        hits_ref[:, here] = hit.astype(BF16)
        counts = jnp.dot(hit.astype(BF16), earlier, preferred_element_type=F32)
        rank = jnp.sum((counts[:, :LANES] + seen) * hit, axis=0, keepdims=True).astype(jnp.int32)
        seen = seen + counts[:, LANES:]
        places.append(peer * capacity + rank)
        same = rank_lane == rank
        high = jnp.where(same, ((slot >> 7) + 1).astype(F32), zero)
        low = jnp.where(same, (slot & 127).astype(F32), zero)
        marks_ref[:LANES, here] = high.astype(BF16)
        marks_ref[LANES:, here] = low.astype(BF16)
    marks = lax.dot_general(
        hits_ref[...], marks_ref[...], (((1,), (1,)), ((), ())), preferred_element_type=F32
    )
    at = iota((peers, EXTRA, LANES), 1)
    none = jnp.zeros((peers, EXTRA, LANES), F32)
    extra = jnp.where(
        at == 0,
        marks[:, :LANES].reshape(peers, 1, LANES) + none,
        jnp.where(at == 1, marks[:, LANES:].reshape(peers, 1, LANES) + none, none),
    )
    out_ref[:, capacity:, :] = extra.astype(BF16)
    place = jnp.concatenate(places, axis=1)
    part = PICK // capacity
    copy.wait()

    def pick_rows(step, carry):
        pick = (iota((PICK, local_rows), 0) + step * PICK == place).astype(F32).astype(BF16)
        rows = jnp.dot(pick, rows_ref[...], preferred_element_type=F32).astype(BF16)
        out_ref[pl.ds(step * part, part), 0:capacity, :] = rows.reshape(part, capacity, width)
        return carry

    lax.fori_loop(0, peers * capacity // PICK, pick_rows, 0)


def pack_rows(index, rows, grid_rows, grid_cols, capacity):
    peers = grid_rows * grid_cols
    local_rows, width = rows.shape
    return pl.pallas_call(
        functools.partial(pack_kernel, grid_rows, grid_cols, capacity),
        out_shape=jax.ShapeDtypeStruct((peers, capacity + EXTRA, width), BF16),
        in_specs=[HBM] * 2,
        out_specs=VMEM,
        scratch_shapes=[
            pltpu.VMEM((local_rows // LANES, LANES), jnp.int32),
            pltpu.VMEM((local_rows, width), BF16),
            pltpu.VMEM((peers, local_rows), BF16),
            pltpu.VMEM((2 * LANES, local_rows), BF16),
            pltpu.SemaphoreType.DMA((2,)),
        ],
        compiler_params=params(60),
        name="pack_rows",
    )(index.reshape(-1, LANES), rows)


def place_kernel(in_ref, out_ref, slot_ref, rows_ref):
    peers, held, width = in_ref.shape
    capacity = held - EXTRA
    local_rows = out_ref.shape[0]
    per = LANES // capacity
    extra = in_ref[:, capacity:, :].astype(F32)
    high, low = extra[:, 0, :], extra[:, 1, :]
    slot_ref[...] = jnp.where(high > 0.5, (high - 1.0) * 128.0 + low, -1.0)
    rows_ref[...] = in_ref[:, 0:capacity, :].reshape(peers * capacity, width)
    which = iota((peers // per, LANES), 1) >> log2(capacity)
    slot = jnp.zeros((peers // per, LANES), F32)
    for i in range(per):
        slot = jnp.where(which == i, slot_ref[pl.ds(i, peers // per, stride=per), :], slot)
    slot = slot.astype(jnp.int32)
    slot = jnp.concatenate([slot[q : q + 1, :] for q in range(peers // per)], axis=1)

    def place_rows(step, carry):
        pick = (iota((PICK, peers * capacity), 0) + step * PICK == slot).astype(F32).astype(BF16)
        rows = jnp.dot(pick, rows_ref[...], preferred_element_type=F32)
        out_ref[pl.ds(pl.multiple_of(step * PICK, PICK), PICK), :] = rows.astype(BF16)
        return carry

    lax.fori_loop(0, local_rows // PICK, place_rows, 0)


def place_rows(got, local_rows):
    peers, held, width = got.shape
    return pl.pallas_call(
        place_kernel,
        out_shape=jax.ShapeDtypeStruct((local_rows, width), BF16),
        in_specs=[VMEM],
        out_specs=VMEM,
        scratch_shapes=[
            pltpu.VMEM((peers, LANES), F32),
            pltpu.VMEM((peers * (held - EXTRA), width), BF16),
        ],
        compiler_params=params(32),
        name="place_rows",
    )(got)


def tile_codes(index, me_x, me_z):
    row, col = index[0], index[1]
    tile = jnp.arange(index.shape[1], dtype=jnp.int32)
    dest, inner = row >> 4, row & 15
    stream, sub = inner >> 2, inner & 3
    d_x, d_z = (dest >> 2) ^ me_x, (dest & 3) ^ me_z
    first = jnp.where(stream < 2, d_x, d_z)
    second = jnp.where(stream < 2, d_z, d_x)
    near = jnp.where(stream & 1 == 0, 1, 3)
    place = stream * 16 + second * 4 + sub
    group = jnp.where(first == 0, 2, jnp.where(first == 2, 0, 1))
    place = place + jnp.where((group == 1) & (first != near), 64, 0)
    return (group << 25) | (tile << 15) | (place << 7) | col


def plan_kernel(count_ref, code_ref, table_ref):
    for group in range(3):
        table_ref[3, group] = 0

    def visit(step, carry):
        for sub in range(8):
            code = code_ref[step * 8 + sub]
            group = code >> 25
            at = table_ref[3, group]
            table_ref[group, at] = code
            table_ref[3, group] = at + 1
        return carry

    count = count_ref[0]
    full = count // 8
    lax.fori_loop(0, full, visit, 0)

    def visit_one(tile, carry):
        code = code_ref[tile]
        group = code >> 25
        at = table_ref[3, group]
        table_ref[group, at] = code
        table_ref[3, group] = at + 1
        return carry

    lax.fori_loop(full * 8, count, visit_one, 0)
    for group in range(3):
        for step in range(UNROLL):
            table_ref[group, table_ref[3, group] + step] = 128 << 7


def plan_tiles(count, codes):
    return pl.pallas_call(
        plan_kernel,
        out_shape=jax.ShapeDtypeStruct((4, codes.shape[0] + UNROLL), jnp.int32),
        in_specs=[SMEM] * 2,
        out_specs=SMEM,
        name="plan_tiles",
    )(count, codes)


def tile_kernel(group, arrays, table_ref, x_ref, tiles_ref, *refs):
    out_refs, (held, totals, sems) = refs[:arrays], refs[arrays:]
    edge = held.shape[2]
    steps = (table_ref[3, group] + UNROLL - 1) // UNROLL

    def fetch(step):
        lane = lax.rem(step, SLOTS)
        for sub in range(UNROLL):
            tile = (table_ref[group, step * UNROLL + sub] >> 15) & 1023
            pltpu.make_async_copy(tiles_ref.at[tile], held.at[lane, sub], sems.at[lane]).start()

    for ahead in range(SLOTS - 1):

        @pl.when(ahead < steps)
        def _():
            fetch(ahead)

    totals[...] = jnp.zeros_like(totals)

    def add_tiles(step, carry):
        @pl.when(step + SLOTS - 1 < steps)
        def _():
            fetch(step + SLOTS - 1)

        lane = lax.rem(step, SLOTS)
        pltpu.make_async_copy(tiles_ref.at[pl.ds(0, UNROLL)], held.at[lane], sems.at[lane]).wait()
        for sub in range(UNROLL):
            code = table_ref[group, step * UNROLL + sub]
            row = jnp.minimum((code >> 7) & 255, totals.shape[0] // edge - 1)
            col = code & 127
            product = jnp.dot(
                held[lane, sub],
                x_ref[pl.ds(pl.multiple_of(col * edge, edge), edge), :],
                preferred_element_type=F32,
            )
            totals[pl.ds(pl.multiple_of(row * edge, edge), edge), :] += product
        return carry

    lax.fori_loop(0, steps, add_tiles, 0)
    rows = out_refs[0].shape[0]
    for array, out_ref in enumerate(out_refs):
        out_ref[...] = totals[array * rows : (array + 1) * rows, :].astype(BF16)


def tile_products(group, arrays, table, x, tiles, rows):
    _, edge, _ = tiles.shape
    width = x.shape[1]
    return pl.pallas_call(
        functools.partial(tile_kernel, group, arrays),
        out_shape=[jax.ShapeDtypeStruct((rows, width), BF16)] * arrays,
        in_specs=[SMEM, VMEM, HBM],
        out_specs=[VMEM] * arrays,
        scratch_shapes=[
            pltpu.VMEM((SLOTS, UNROLL, edge, edge), BF16),
            pltpu.VMEM((arrays * rows + edge, width), F32),
            pltpu.SemaphoreType.DMA((SLOTS,)),
        ],
        compiler_params=params(32),
        cost_estimate=pl.CostEstimate(
            flops=5_000_000_000 * arrays, bytes_accessed=5_000_000 * arrays, transcendentals=0
        ),
        name="tile_products",
    )(table, x, tiles)


def wide(ref, start, rows):
    return ref[start : start + rows, :].astype(F32)


def forward_kernel(*refs):
    for stream in range(STREAMS):
        kept, got, out = refs[2 * stream], refs[2 * stream + 1], refs[2 * STREAMS + stream]
        out[...] = (kept[...].astype(F32) + got[...].astype(F32)).astype(BF16)


def forward_sums(kept, got):
    pairs = [array for pair in zip(kept, got) for array in pair]
    return pl.pallas_call(
        forward_kernel,
        out_shape=[jax.ShapeDtypeStruct(kept[0].shape, BF16)] * STREAMS,
        in_specs=[VMEM] * len(pairs),
        out_specs=[VMEM] * STREAMS,
        compiler_params=params(32),
        name="forward_sums",
    )(*pairs)


def turn_kernel(*refs):
    outs = refs[3 * STREAMS :]
    for stream in range(STREAMS):
        kept, got, last = refs[3 * stream : 3 * stream + 3]
        rows = last.shape[0] // SIDE
        at = stream % PAIR * rows
        for delta in range(SIDE):
            start = delta * rows
            total = wide(kept, start, rows) + wide(got, start, rows) + wide(last, start, rows)
            out = outs[stream // PAIR * SIDE + delta]
            out[at : at + rows, :] = total.astype(out.dtype)


def turn_sums(kept, got, last):
    ins = [array for three in zip(kept, got, last) for array in three]
    rows, width = last[0].shape
    shape = (PAIR * rows // SIDE, width)
    outs = [jax.ShapeDtypeStruct(shape, F32)] + [jax.ShapeDtypeStruct(shape, BF16)] * (SIDE - 1)
    done = pl.pallas_call(
        turn_kernel,
        out_shape=outs * 2,
        in_specs=[VMEM] * len(ins),
        out_specs=[VMEM] * (2 * SIDE),
        compiler_params=params(32),
        name="turn_sums",
    )(*ins)
    return done[:SIDE], done[SIDE:]


def dense_kernel(*refs):
    weight_ref, bias_ref, out_ref = refs[2 * SIDE :]
    for side in range(2):
        own, *got = refs[side * SIDE : (side + 1) * SIDE]
        rows = own.shape[0]
        total = own[...]
        for ref in got:
            total += ref[...].astype(F32)
        hidden = jnp.dot(total.astype(BF16), weight_ref[...], preferred_element_type=F32)
        hidden = jnp.maximum(hidden + bias_ref[...], 0.0)
        out_ref[side * rows : (side + 1) * rows, :] = hidden.astype(BF16)


def dense(terms, weight, bias):
    return pl.pallas_call(
        dense_kernel,
        out_shape=jax.ShapeDtypeStruct((2 * terms[0].shape[0], weight.shape[1]), BF16),
        in_specs=[VMEM] * (len(terms) + 2),
        out_specs=VMEM,
        compiler_params=params(32),
        name="dense",
    )(*terms, weight, bias.reshape(1, -1))


def swap(arrays, axis, first):
    return [
        lax.ppermute(array, axis, [(c, c ^ bit) for c in range(SIDE)])
        for array, bit in zip(arrays, (1, 3) if first else (3, 1))
    ]


def spread(sides):
    got = [list(side) for side in sides]
    for bit in (1, 2, 3):
        for side, axis in enumerate(("z", "x")):
            got[side][bit] = lax.ppermute(
                sides[side][bit], axis, [(c, c ^ bit) for c in range(SIDE)]
            )
    return got[0] + got[1]


def body(features, new_index, tile_values, tile_index, tile_count, weight, bias):
    grid_rows = lax.axis_size("y") * lax.axis_size("core")
    grid_cols = lax.axis_size("x") * lax.axis_size("z")
    local_rows = features.shape[0]
    everyone = ("core", "y", "x", "z")
    capacity = 2 * local_rows // (grid_rows * grid_cols)
    tiles = tile_values[0, 0]
    row_tiles = local_rows * grid_cols // tiles.shape[1]
    assert row_tiles == 256 and grid_cols == SIDE * SIDE

    codes = tile_codes(tile_index[0, 0], lax.axis_index("x"), lax.axis_index("z"))
    packed = pack_rows(new_index, features, grid_rows, grid_cols, capacity)
    got = lax.all_to_all(packed, everyone, split_axis=0, concat_axis=0, tiled=True)
    table = plan_tiles(tile_count.reshape(1), codes)
    got, table = lax.optimization_barrier((got, table))
    moved_rows = place_rows(got, local_rows)
    x = lax.all_gather(moved_rows, ("y", "core"), axis=0, tiled=True)

    rows = local_rows * grid_cols // 16
    axes = ("x", "z")
    pairs = (slice(0, PAIR), slice(PAIR, STREAMS))
    sent_on = tile_products(0, STREAMS, table, x, tiles, rows)
    got_on = [swap(sent_on[pair], axis, True) for pair, axis in zip(pairs, axes)]
    both = tile_products(1, 2 * STREAMS, table, x, tiles, rows)
    got_own = [swap(both[pair], axis, True) for pair, axis in zip(pairs, axes)]
    hand = forward_sums(both[STREAMS:], got_on[0] + got_on[1])
    got_last = [swap(hand[pair], axis, False) for pair, axis in zip(pairs, axes)]
    hand, table = lax.optimization_barrier((hand, table))
    kept = tile_products(2, STREAMS, table, x, tiles, rows)
    sides = turn_sums(kept, got_own[0] + got_own[1], got_last[0] + got_last[1])
    return dense(spread(sides), weight, bias)


def solution(mesh):
    fine = Mesh(mesh.devices.reshape(-1, 2, SIDE, SIDE), ("y", "core", "x", "z"))
    grid = (("y", "core"), ("x", "z"))
    flat = ("y", "core", "x", "z")
    in_specs = (
        P(flat, None),
        P(flat),
        P(*grid, None, None, None),
        P(*grid, None, None),
        P(*grid),
        P(),
        P(),
    )
    return jax.shard_map(
        body, mesh=fine, in_specs=in_specs, out_specs=P(flat, None), check_vma=False
    )
```

time: 178 us -> 165 us (0.927); the launches traced: 177 us -> 162 us
  blocking collectives: 32.7 us -> 0 us
  Pallas kernels: 31.3 us -> 44.3 us
  starting transfers between devices: 27.9 us -> 35.1 us
  local copies, waits for them, and re-layouts: 6.67 us -> 2.91 us
    all_to_all x1 -> x0, blocking collectives: 32.7 us -> none  [body(): lax.all_to_all(packed, everyone, split_axis=0, concat_axis=0, tiled=True)]
    ppermute x16 -> x18, waiting for transfers between devices: 42.4 us -> 23.5 us  [the longest x12 14.8 us: swap(): lax.ppermute(array, axis, [(c, c ^ bit) for c in range(SIDE)])]
    pallas_call x7, Pallas kernels: 14.4 us -> 30.6 us  [the longest x3 21.1 us: tile_products(): pl.pallas_call(functools.partial(tile_kernel, group, arrays), out_shape=[...]
    all_to_all x0 -> x1, waiting for transfers between devices: none -> 12.1 us  [body(): lax.all_to_all(packed, everyone, split_axis=0, concat_axis=0, tiled=True)]
    all_to_all x0 -> x1, starting transfers between devices: none -> 11.2 us  [body(): lax.all_to_all(packed, everyone, split_axis=0, concat_axis=0, tiled=True)]
    all_gather x1, waiting for transfers between devices: 21.5 us -> 29.5 us  [body(): x = lax.all_gather(moved_rows, ('y', 'core'), axis=0, tiled=True)]
    ppermute x16 -> x18, starting transfers between devices: 27.9 us -> 23.9 us  [the longest x12 13.2 us: swap(): lax.ppermute(array, axis, [(c, c ^ bit) for c in range(SIDE)])]
    unnamed x18 -> x12, local copies, waits for them, and re-layouts: 6.67 us -> 2.91 us
  transfers between devices with their start and end apart: 17 -> 20, of which waited for: 16 -> 10; matrix products, arithmetic and copies ran while one was open for 0% -> 0% of each run, Pallas kernels for 5% -> 14%
where the time goes in v3:
time: 165 us; the launch traced here: 162 us
  waiting for transfers between devices  65.2 us (40%)
  Pallas kernels  44.3 us (27%)
  starting transfers between devices  35.1 us (21%)
  between operations  14.2 us (9%)
  local copies, waits for them, and re-layouts  2.91 us (2%)
    all_gather x1, waiting for transfers between devices, body(): x = lax.all_gather(moved_rows, ('y', 'core'), axis=0, tiled=True)  29.5 us
    pallas_call x3, Pallas kernels, tile_products(): pl.pallas_call(functools.partial(tile_kernel, group, arrays), out_shape=[...  21.1 us
    ppermute x12, waiting for transfers between devices, swap(): lax.ppermute(array, axis, [(c, c ^ bit) for c in range(SIDE)])  14.8 us
    ppermute x12, starting transfers between devices, swap(): lax.ppermute(array, axis, [(c, c ^ bit) for c in range(SIDE)])  13.2 us
    all_to_all x1, waiting for transfers between devices, body(): lax.all_to_all(packed, everyone, split_axis=0, concat_axis=0, tiled=True)  12.1 us
    all_to_all x1, starting transfers between devices, body(): lax.all_to_all(packed, everyone, split_axis=0, concat_axis=0, tiled=True)  11.2 us
    ppermute x6, starting transfers between devices, spread(): lax.ppermute(sides[side][bit], axis, [(c, c ^ bit) for c in range(SIDE)])  10.8 us
    ppermute x6, waiting for transfers between devices, spread(): lax.ppermute(sides[side][bit], axis, [(c, c ^ bit) for c in range(SIDE)])  8.74 us
  transfers between devices with their start and end apart: 20, of which 10 were waited for; matrix products, arithmetic and copies ran while one was open for 0% of the time, Pallas kernels for 14%

profile of v3, /device:TPU:0, one launch (start us, length us, event | category | flops | bytes accessed | tf_op | source)
XLA Modules:
  0.0 162.4 jit_solution(10994890425125298205)
XLA Ops:
  6.5 7.9 %pack_rows.1 = bf16[128,40,128]{2,1,0:T(8,128)(2,1)} custom-call(s32[16,128]{1,0:T(8,128)} %bitcast.6, bf16[2048,128]{1,0:T(8,128)(2,1)} %rows_hbm.1), custom_call_target="tpu_custom_call" | custom-call | tf_op jit(solution)/shard_map/pack_rows/pallas_call | solution.py:112
  14.5 11.2 %all-to-all-start = ((bf16[128,40,128]{2,1,0:T(8,128)(2,1)}), bf16[128,40,128]{2,1,0:T(8,128)(2,1)S(1)}, u32[]{:S(2)}, u32[]{:S(2)}) async-start(bf16[128,40,128]{2,1,0:T(8,128)(2,1)} %pack_rows.1), calls=%async_computation | async-start | bytes 2621440 | tf_op jit(solution)/shard_map/all_to_all | solution.py:395
  25.6 0.0 all-gather.2.cloned.1.call-start
  26.4 0.6 or_or_fusion.code_ref
  27.0 6.8 %plan_tiles.1.table_ref = s32[4,656]{1,0:T(4,128)} custom-call(s32[1]{0:T(128)} %bitcast.4.count_ref, s32[640]{0:T(1024)} %or_or_fusion.code_ref), custom_call_target="tpu_custom_call" | custom-call | tf_op jit(solution)/shard_map/plan_tiles/pallas_call | solution.py:217
  33.8 12.1 %all-to-all-done.in_ref = bf16[128,40,128]{2,1,0:T(8,128)(2,1)S(1)} async-done(((bf16[128,40,128]{2,1,0:T(8,128)(2,1)}), bf16[128,40,128]{2,1,0:T(8,128)(2,1)S(1)}, u32[]{:S(2)}, u32[]{:S(2)}) %all-to-all-start) | async-done | bytes 1310752 | tf_op jit(solution)/shard_map/all_to_all | solution.py:395
  45.9 5.7 %place_rows.1 = bf16[2048,128]{1,0:T(8,128)(2,1)} custom-call(bf16[128,40,128]{2,1,0:T(8,128)(2,1)S(1)} %all-to-all-done.in_ref), custom_call_target="tpu_custom_call" | custom-call | tf_op jit(solution)/shard_map/place_rows/pallas_call | solution.py:156
  51.7 0.0 all-gather.2.cloned.1.call-update
  51.7 29.5 %all-gather.2.cloned.1.call-done.x_ref = bf16[16384,128]{1,0:T(8,128)(2,1)} async-done(((bf16[2048,128]{1,0:T(8,128)(2,1)}), bf16[16384,128]{1,0:T(8,128)(2,1)}) %all-gather.2.cloned.1.call-update) | async-done | bytes 4194320 | tf_op jit(solution)/shard_map/all_gather | solution.py:399
  81.2 0.7 copy-done.1
  81.9 2.2 %copy-done.3 = bf16[16384,128]{1,0:T(8,128)(2,1)S(1)} copy-done((bf16[16384,128]{1,0:T(8,128)(2,1)S(1)}, bf16[16384,128]{1,0:T(8,128)(2,1)}, u32[]{:S(2)}) %copy-start.3) | copy-done | bytes 4194328
  84.1 5.4 %tile_products.4 = (bf16[2048,128]{1,0:T(8,128)(2,1)S(1)}, bf16[2048,128]{1,0:T(8,128)(2,1)S(1)}, bf16[2048,128]{1,0:T(8,128)(2,1)S(1)}, bf16[2048,128]{1,0:T(8,128)(2,1)S(1)}) custom-call(s32[4,656]{1,0:T(4,128)S(1)} %copy-done.1, bf16[16384,128]{1,0:T(8,128)(2,1)S(1)} %copy-done.3, bf16[640,128,128]{2,1,0:T(8,128)(2,1)} %bitcast.7), custom_call_target="tpu_custom_call" | custom-call | flops 20000000000 | bytes 20000000 | tf_op jit(solution)/shard_map/tile_products/pallas_call | solution.py:273
  89.6 1.9 %collective-permute-start = (bf16[2048,128]{1,0:T(8,128)(2,1)S(1)}, bf16[2048,128]{1,0:T(8,128)(2,1)S(1)}, u32[]{:S(2)}, u32[]{:S(2)}) collective-permute-start(bf16[2048,128]{1,0:T(8,128)(2,1)S(1)} %get-tuple-element.39), channel_id=1, source_target_pairs={{0,4},{4,0},{8,12},{12,8},{1,5},{5,1},{9,13},{13,9},{2,6},{6,2},{1... | collective-permute-start | bytes 1572872 | tf_op jit(solution)/shard_map/ppermute | solution.py:368
  91.5 0.0 collective-permute-start.1
  91.5 1.7 %collective-permute-start.2 = (bf16[2048,128]{1,0:T(8,128)(2,1)S(1)}, bf16[2048,128]{1,0:T(8,128)(2,1)S(1)}, u32[]{:S(2)}, u32[]{:S(2)}) collective-permute-start(bf16[2048,128]{1,0:T(8,128)(2,1)S(1)} %get-tuple-element.43), channel_id=1, source_target_pairs={{0,1},{1,0},{2,3},{3,2},{4,5},{5,4},{6,7},{7,6},{8,9},{9,8},{10,11... | collective-permute-start | bytes 1572872 | tf_op jit(solution)/shard_map/ppermute | solution.py:368
  93.2 3.7 %collective-permute-start.3 = (bf16[2048,128]{1,0:T(8,128)(2,1)S(1)}, bf16[2048,128]{1,0:T(8,128)(2,1)S(1)}, u32[]{:S(2)}, u32[]{:S(2)}) collective-permute-start(bf16[2048,128]{1,0:T(8,128)(2,1)S(1)} %get-tuple-element.45), channel_id=1, source_target_pairs={{0,3},{1,2},{2,1},{3,0},{4,7},{5,6},{6,5},{7,4},{8,11},{9,10},{10,... | collective-permute-start | bytes 1572872 | tf_op jit(solution)/shard_map/ppermute | solution.py:368
  96.9 10.3 %tile_products.3 = (bf16[2048,128]{1,0:T(8,128)(2,1)S(1)}, bf16[2048,128]{1,0:T(8,128)(2,1)S(1)}, bf16[2048,128]{1,0:T(8,128)(2,1)S(1)}, bf16[2048,128]{1,0:T(8,...) custom-call(s32[4,656]{1,0:T(4,128)S(1)} %copy-done.1, ...), custom_call_target="tpu_custom_call" | custom-call | flops 40000000000 | bytes 40000000 | tf_op jit(solution)/shard_map/tile_products/pallas_call | solution.py:273
  107.2 0.1 collective-permute-start.4
  107.3 0.0 collective-permute-done.refs_1_
  107.3 0.1 collective-permute-start.6
  107.4 0.0 collective-permute-done.1.refs_3_
  107.4 0.8 collective-permute-start.8
  108.2 0.0 collective-permute-done.2.refs_5_
  108.2 1.6 %collective-permute-start.10 = (bf16[2048,128]{1,0:T(8,128)(2,1)S(1)}, bf16[2048,128]{1,0:T(8,128)(2,1)S(1)}, u32[]{:S(2)}, u32[]{:S(2)}) collective-permute-start(bf16[2048,128]{1,0:T(8,128)(2,1)S(1)} %get-tuple-element.58), channel_id=1, source_target_pairs={{0,3},{1,2},{2,1},{3,0},{4,7},{5,6},{6,5},{7,4},{8,11},{9,10},{10,... | collective-permute-start | bytes 1572872 | tf_op jit(solution)/shard_map/ppermute | solution.py:368
  109.8 0.0 collective-permute-done.3.refs_7_
  109.8 0.5 forward_sums.1
  110.3 2.2 %collective-permute-start.5 = (bf16[2048,128]{1,0:T(8,128)(2,1)S(1)}, bf16[2048,128]{1,0:T(8,128)(2,1)S(1)}, u32[]{:S(2)}, u32[]{:S(2)}) collective-permute-start(bf16[2048,128]{1,0:T(8,128)(2,1)S(1)} %get-tuple-element.46), channel_id=1, source_target_pairs={{0,12},{4,8},{8,4},{12,0},{1,13},{5,9},{9,5},{13,1},{2,14},{6,10},... | collective-permute-start | bytes 1572872 | tf_op jit(solution)/shard_map/ppermute | solution.py:368
  112.5 6.8 %collective-permute-done.4.refs_1_ = bf16[2048,128]{1,0:T(8,128)(2,1)S(1)} collective-permute-done((bf16[2048,128]{1,0:T(8,128)(2,1)S(1)}, bf16[2048,128]{1,0:T(8,128)(2,1)S(1)}, u32[]{:S(2)}, u32[]{:S(2)}) %collective-permute-start.4) | collective-permute-done | bytes 524320 | tf_op jit(solution)/shard_map/ppermute | solution.py:368
  119.3 0.3 collective-permute-start.7
  119.6 3.8 %collective-permute-done.6.refs_4_ = bf16[2048,128]{1,0:T(8,128)(2,1)S(1)} collective-permute-done((bf16[2048,128]{1,0:T(8,128)(2,1)S(1)}, bf16[2048,128]{1,0:T(8,128)(2,1)S(1)}, u32[]{:S(2)}, u32[]{:S(2)}) %collective-permute-start.6) | collective-permute-done | bytes 524320 | tf_op jit(solution)/shard_map/ppermute | solution.py:368
  123.4 0.7 collective-permute-start.11
  124.2 5.4 %tile_products.5 = (bf16[2048,128]{1,0:T(8,128)(2,1)S(1)}, bf16[2048,128]{1,0:T(8,128)(2,1)S(1)}, bf16[2048,128]{1,0:T(8,128)(2,1)S(1)}, bf16[2048,128]{1,0:T(8,128)(2,1)S(1)}) custom-call(s32[4,656]{1,0:T(4,128)S(1)} %copy-done.1, bf16[16384,128]{1,0:T(8,128)(2,1)S(1)} %copy-done.4, bf16[640,128,128]{2,1,0:T(8,128)(2,1)} %bitcast.9), custom_call_target="tpu_custom_call" | custom-call | flops 20000000000 | bytes 20000000 | tf_op jit(solution)/shard_map/tile_products/pallas_call | solution.py:273
  129.6 0.0 copy-start
  129.7 0.0 copy-start.2
  129.7 2.2 %collective-permute-done.5.refs_2_ = bf16[2048,128]{1,0:T(8,128)(2,1)S(1)} collective-permute-done((bf16[2048,128]{1,0:T(8,128)(2,1)S(1)}, bf16[2048,128]{1,0:T(8,128)(2,1)S(1)}, u32[]{:S(2)}, u32[]{:S(2)}) %collective-permute-start.5) | collective-permute-done | bytes 524320 | tf_op jit(solution)/shard_map/ppermute | solution.py:368
  131.9 1.9 %collective-permute-done.9.refs_8_ = bf16[2048,128]{1,0:T(8,128)(2,1)S(1)} collective-permute-done((bf16[2048,128]{1,0:T(8,128)(2,1)S(1)}, bf16[2048,128]{1,0:T(8,128)(2,1)S(1)}, u32[]{:S(2)}, u32[]{:S(2)}) %collective-permute-start.9) | collective-permute-done | bytes 524320 | tf_op jit(solution)/shard_map/ppermute | solution.py:368
  133.8 0.7 turn_sums.1
  134.6 0.3 collective-permute-start.12
  134.9 3.8 %collective-permute-start.13 = (bf16[1024,128]{1,0:T(8,128)(2,1)S(1)}, bf16[1024,128]{1,0:T(8,128)(2,1)S(1)}, u32[]{:S(2)}, u32[]{:S(2)}) collective-permute-start(bf16[1024,128]{1,0:T(8,128)(2,1)S(1)} %get-tuple-element.61), channel_id=1, source_target_pairs={{0,2},{1,3},{2,0},{3,1},{4,6},{5,7},{6,4},{7,5},{8,10},{9,11},{10,... | collective-permute-start | bytes 786440 | tf_op jit(solution)/shard_map/ppermute | solution.py:377
  138.7 0.6 collective-permute-start.14
  139.3 0.8 collective-permute-start.15
  140.1 3.3 %collective-permute-start.16 = (bf16[1024,128]{1,0:T(8,128)(2,1)S(1)}, bf16[1024,128]{1,0:T(8,128)(2,1)S(1)}, u32[]{:S(2)}, u32[]{:S(2)}) collective-permute-start(bf16[1024,128]{1,0:T(8,128)(2,1)S(1)} %get-tuple-element.65), channel_id=1, source_target_pairs={{0,8},{4,12},{8,0},{12,4},{1,9},{5,13},{9,1},{13,5},{2,10},{6,14},... | collective-permute-start | bytes 786440 | tf_op jit(solution)/shard_map/ppermute | solution.py:377
  143.4 2.0 %collective-permute-start.17 = (bf16[1024,128]{1,0:T(8,128)(2,1)S(1)}, bf16[1024,128]{1,0:T(8,128)(2,1)S(1)}, u32[]{:S(2)}, u32[]{:S(2)}) collective-permute-start(bf16[1024,128]{1,0:T(8,128)(2,1)S(1)} %get-tuple-element.66), channel_id=1, source_target_pairs={{0,12},{4,8},{8,4},{12,0},{1,13},{5,9},{9,5},{13,1},{2,14},{6,10},... | collective-permute-start | bytes 786440 | tf_op jit(solution)/shard_map/ppermute | solution.py:377
  145.3 1.3 collective-permute-done.13.refs_2_
  146.7 2.4 %collective-permute-done.14.refs_3_ = bf16[1024,128]{1,0:T(8,128)(2,1)S(1)} collective-permute-done((bf16[1024,128]{1,0:T(8,128)(2,1)S(1)}, bf16[1024,128]{1,0:T(8,128)(2,1)S(1)}, u32[]{:S(2)}, u32[]{:S(2)}) %collective-permute-start.14) | collective-permute-done | bytes 262176 | tf_op jit(solution)/shard_map/ppermute | solution.py:377
  149.1 2.4 %collective-permute-done.16.refs_6_ = bf16[1024,128]{1,0:T(8,128)(2,1)S(1)} collective-permute-done((bf16[1024,128]{1,0:T(8,128)(2,1)S(1)}, bf16[1024,128]{1,0:T(8,128)(2,1)S(1)}, u32[]{:S(2)}, u32[]{:S(2)}) %collective-permute-start.16) | collective-permute-done | bytes 262176 | tf_op jit(solution)/shard_map/ppermute | solution.py:377
  151.6 2.5 %collective-permute-done.17.refs_7_ = bf16[1024,128]{1,0:T(8,128)(2,1)S(1)} collective-permute-done((bf16[1024,128]{1,0:T(8,128)(2,1)S(1)}, bf16[1024,128]{1,0:T(8,128)(2,1)S(1)}, u32[]{:S(2)}, u32[]{:S(2)}) %collective-permute-start.17) | collective-permute-done | bytes 262176 | tf_op jit(solution)/shard_map/ppermute | solution.py:377
  154.1 1.5 dense.1
  (16 shorter events, 0.1 us)
Async XLA Ops:
  6.5 19.8 %copy-start.5 = (s32[1,1,2,640]{3,2,1,0:T(2,128)S(1)}, s32[1,1,2,640]{3,2,1,0:T(2,128)}, u32[]{:S(2)}) copy-start(s32[1,1,2,640]{3,2,1,0:T(2,128)} %param.10) | copy-start | bytes 15364
  14.5 31.5 %all-to-all-start = ((bf16[128,40,128]{2,1,0:T(8,128)(2,1)}), bf16[128,40,128]{2,1,0:T(8,128)(2,1)S(1)}, u32[]{:S(2)}, u32[]{:S(2)}) async-start(bf16[128,40,128]{2,1,0:T(8,128)(2,1)} %pack_rows.1), calls=%async_computation | async-start | bytes 2621440 | tf_op jit(solution)/shard_map/all_to_all | solution.py:395
  25.6 55.6 %all-gather.2.cloned.1.call-start = ((), (), s32[]{:S(2)}) async-start(), calls=%async_computation.1 | async-start | bytes 4718592 | tf_op jit(solution)/shard_map/all_gather | solution.py:399
  81.2 0.7 copy-start.1
  81.9 2.2 %copy-start.3 = (bf16[16384,128]{1,0:T(8,128)(2,1)S(1)}, bf16[16384,128]{1,0:T(8,128)(2,1)}, u32[]{:S(2)}) copy-start(bf16[16384,128]{1,0:T(8,128)(2,1)} %all-gather.2.cloned.1.call-done.x_ref) | copy-start | bytes 12582916
  89.6 17.7 %collective-permute-start = (bf16[2048,128]{1,0:T(8,128)(2,1)S(1)}, bf16[2048,128]{1,0:T(8,128)(2,1)S(1)}, u32[]{:S(2)}, u32[]{:S(2)}) collective-permute-start(bf16[2048,128]{1,0:T(8,128)(2,1)S(1)} %get-tuple-element.39), channel_id=1, source_target_pairs={{0,4},{4,0},{8,12},{12,8},{1,5},{5,1},{9,13},{13,9},{2,6},{6,2},{1... | collective-permute-start | bytes 1572872 | tf_op jit(solution)/shard_map/ppermute | solution.py:368
  91.5 15.9 %collective-permute-start.1 = (bf16[2048,128]{1,0:T(8,128)(2,1)S(1)}, bf16[2048,128]{1,0:T(8,128)(2,1)S(1)}, u32[]{:S(2)}, u32[]{:S(2)}) collective-permute-start(bf16[2048,128]{1,0:T(8,128)(2,1)S(1)} %get-tuple-element.41), channel_id=1, source_target_pairs={{0,12},{4,8},{8,4},{12,0},{1,13},{5,9},{9,5},{13,1},{2,14},{6,10},... | collective-permute-start | bytes 1572872 | tf_op jit(solution)/shard_map/ppermute | solution.py:368
  91.5 16.7 %collective-permute-start.2 = (bf16[2048,128]{1,0:T(8,128)(2,1)S(1)}, bf16[2048,128]{1,0:T(8,128)(2,1)S(1)}, u32[]{:S(2)}, u32[]{:S(2)}) collective-permute-start(bf16[2048,128]{1,0:T(8,128)(2,1)S(1)} %get-tuple-element.43), channel_id=1, source_target_pairs={{0,1},{1,0},{2,3},{3,2},{4,5},{5,4},{6,7},{7,6},{8,9},{9,8},{10,11... | collective-permute-start | bytes 1572872 | tf_op jit(solution)/shard_map/ppermute | solution.py:368
  93.2 16.6 %collective-permute-start.3 = (bf16[2048,128]{1,0:T(8,128)(2,1)S(1)}, bf16[2048,128]{1,0:T(8,128)(2,1)S(1)}, u32[]{:S(2)}, u32[]{:S(2)}) collective-permute-start(bf16[2048,128]{1,0:T(8,128)(2,1)S(1)} %get-tuple-element.45), channel_id=1, source_target_pairs={{0,3},{1,2},{2,1},{3,0},{4,7},{5,6},{6,5},{7,4},{8,11},{9,10},{10,... | collective-permute-start | bytes 1572872 | tf_op jit(solution)/shard_map/ppermute | solution.py:368
  107.2 17.0 %copy-start.4 = (bf16[16384,128]{1,0:T(8,128)(2,1)S(1)}, bf16[16384,128]{1,0:T(8,128)(2,1)}, u32[]{:S(2)}) copy-start(bf16[16384,128]{1,0:T(8,128)(2,1)} %all-gather.2.cloned.1.call-done.x_ref) | copy-start | bytes 12582916
  107.2 12.2 %collective-permute-start.4 = (bf16[2048,128]{1,0:T(8,128)(2,1)S(1)}, bf16[2048,128]{1,0:T(8,128)(2,1)S(1)}, u32[]{:S(2)}, u32[]{:S(2)}) collective-permute-start(bf16[2048,128]{1,0:T(8,128)(2,1)S(1)} %get-tuple-element.52), channel_id=1, source_target_pairs={{0,4},{4,0},{8,12},{12,8},{1,5},{5,1},{9,13},{13,9},{2,6},{6,2},{1... | collective-permute-start | bytes 1572872 | tf_op jit(solution)/shard_map/ppermute | solution.py:368
  107.3 16.1 %collective-permute-start.6 = (bf16[2048,128]{1,0:T(8,128)(2,1)S(1)}, bf16[2048,128]{1,0:T(8,128)(2,1)S(1)}, u32[]{:S(2)}, u32[]{:S(2)}) collective-permute-start(bf16[2048,128]{1,0:T(8,128)(2,1)S(1)} %get-tuple-element.54), channel_id=1, source_target_pairs={{0,12},{4,8},{8,4},{12,0},{1,13},{5,9},{9,5},{13,1},{2,14},{6,10},... | collective-permute-start | bytes 1572872 | tf_op jit(solution)/shard_map/ppermute | solution.py:368
  107.4 16.1 %collective-permute-start.8 = (bf16[2048,128]{1,0:T(8,128)(2,1)S(1)}, bf16[2048,128]{1,0:T(8,128)(2,1)S(1)}, u32[]{:S(2)}, u32[]{:S(2)}) collective-permute-start(bf16[2048,128]{1,0:T(8,128)(2,1)S(1)} %get-tuple-element.56), channel_id=1, source_target_pairs={{0,1},{1,0},{2,3},{3,2},{4,5},{5,4},{6,7},{7,6},{8,9},{9,8},{10,11... | collective-permute-start | bytes 1572872 | tf_op jit(solution)/shard_map/ppermute | solution.py:368
  108.2 21.5 %collective-permute-start.10 = (bf16[2048,128]{1,0:T(8,128)(2,1)S(1)}, bf16[2048,128]{1,0:T(8,128)(2,1)S(1)}, u32[]{:S(2)}, u32[]{:S(2)}) collective-permute-start(bf16[2048,128]{1,0:T(8,128)(2,1)S(1)} %get-tuple-element.58), channel_id=1, source_target_pairs={{0,3},{1,2},{2,1},{3,0},{4,7},{5,6},{6,5},{7,4},{8,11},{9,10},{10,... | collective-permute-start | bytes 1572872 | tf_op jit(solution)/shard_map/ppermute | solution.py:368
  110.3 21.6 %collective-permute-start.5 = (bf16[2048,128]{1,0:T(8,128)(2,1)S(1)}, bf16[2048,128]{1,0:T(8,128)(2,1)S(1)}, u32[]{:S(2)}, u32[]{:S(2)}) collective-permute-start(bf16[2048,128]{1,0:T(8,128)(2,1)S(1)} %get-tuple-element.46), channel_id=1, source_target_pairs={{0,12},{4,8},{8,4},{12,0},{1,13},{5,9},{9,5},{13,1},{2,14},{6,10},... | collective-permute-start | bytes 1572872 | tf_op jit(solution)/shard_map/ppermute | solution.py:368
  119.3 12.5 %collective-permute-start.7 = (bf16[2048,128]{1,0:T(8,128)(2,1)S(1)}, bf16[2048,128]{1,0:T(8,128)(2,1)S(1)}, u32[]{:S(2)}, u32[]{:S(2)}) collective-permute-start(bf16[2048,128]{1,0:T(8,128)(2,1)S(1)} %get-tuple-element.47), channel_id=1, source_target_pairs={{0,4},{4,0},{8,12},{12,8},{1,5},{5,1},{9,13},{13,9},{2,6},{6,2},{1... | collective-permute-start | bytes 1572872 | tf_op jit(solution)/shard_map/ppermute | solution.py:368
  123.4 10.4 %collective-permute-start.9 = (bf16[2048,128]{1,0:T(8,128)(2,1)S(1)}, bf16[2048,128]{1,0:T(8,128)(2,1)S(1)}, u32[]{:S(2)}, u32[]{:S(2)}) collective-permute-start(bf16[2048,128]{1,0:T(8,128)(2,1)S(1)} %get-tuple-element.48), channel_id=1, source_target_pairs={{0,3},{1,2},{2,1},{3,0},{4,7},{5,6},{6,5},{7,4},{8,11},{9,10},{10,... | collective-permute-start | bytes 1572872 | tf_op jit(solution)/shard_map/ppermute | solution.py:368
  123.4 10.4 %collective-permute-start.11 = (bf16[2048,128]{1,0:T(8,128)(2,1)S(1)}, bf16[2048,128]{1,0:T(8,128)(2,1)S(1)}, u32[]{:S(2)}, u32[]{:S(2)}) collective-permute-start(bf16[2048,128]{1,0:T(8,128)(2,1)S(1)} %get-tuple-element.49), channel_id=1, source_target_pairs={{0,1},{1,0},{2,3},{3,2},{4,5},{5,4},{6,7},{7,6},{8,9},{9,8},{10,11... | collective-permute-start | bytes 1572872 | tf_op jit(solution)/shard_map/ppermute | solution.py:368
  129.6 24.4 %copy-start = (bf16[128,256]{1,0:T(8,128)(2,1)S(1)}, bf16[128,256]{1,0:T(8,128)(2,1)}, u32[]{:S(2)}) copy-start(bf16[128,256]{1,0:T(8,128)(2,1)} %refs_8_.1) | copy-start | bytes 196612
  129.7 24.4 %copy-start.2 = (f32[256]{0:T(256)S(1)}, f32[256]{0:T(256)}, u32[]{:S(2)}) copy-start(f32[256]{0:T(256)} %param.13) | copy-start | bytes 3076
  134.6 8.8 %collective-permute-start.12 = (bf16[1024,128]{1,0:T(8,128)(2,1)S(1)}, bf16[1024,128]{1,0:T(8,128)(2,1)S(1)}, u32[]{:S(2)}, u32[]{:S(2)}) collective-permute-start(bf16[1024,128]{1,0:T(8,128)(2,1)S(1)} %get-tuple-element.60), channel_id=1, source_target_pairs={{0,1},{1,0},{2,3},{3,2},{4,5},{5,4},{6,7},{7,6},{8,9},{9,8},{10,11... | collective-permute-start | bytes 786440 | tf_op jit(solution)/shard_map/ppermute | solution.py:377
  134.9 11.8 %collective-permute-start.13 = (bf16[1024,128]{1,0:T(8,128)(2,1)S(1)}, bf16[1024,128]{1,0:T(8,128)(2,1)S(1)}, u32[]{:S(2)}, u32[]{:S(2)}) collective-permute-start(bf16[1024,128]{1,0:T(8,128)(2,1)S(1)} %get-tuple-element.61), channel_id=1, source_target_pairs={{0,2},{1,3},{2,0},{3,1},{4,6},{5,7},{6,4},{7,5},{8,10},{9,11},{10,... | collective-permute-start | bytes 786440 | tf_op jit(solution)/shard_map/ppermute | solution.py:377
  138.7 10.4 %collective-permute-start.14 = (bf16[1024,128]{1,0:T(8,128)(2,1)S(1)}, bf16[1024,128]{1,0:T(8,128)(2,1)S(1)}, u32[]{:S(2)}, u32[]{:S(2)}) collective-permute-start(bf16[1024,128]{1,0:T(8,128)(2,1)S(1)} %get-tuple-element.62), channel_id=1, source_target_pairs={{0,3},{1,2},{2,1},{3,0},{4,7},{5,6},{6,5},{7,4},{8,11},{9,10},{10,... | collective-permute-start | bytes 786440 | tf_op jit(solution)/shard_map/ppermute | solution.py:377
  139.3 9.8 %collective-permute-start.15 = (bf16[1024,128]{1,0:T(8,128)(2,1)S(1)}, bf16[1024,128]{1,0:T(8,128)(2,1)S(1)}, u32[]{:S(2)}, u32[]{:S(2)}) collective-permute-start(bf16[1024,128]{1,0:T(8,128)(2,1)S(1)} %get-tuple-element.64), channel_id=1, source_target_pairs={{0,4},{4,0},{8,12},{12,8},{1,5},{5,1},{9,13},{13,9},{2,6},{6,2},{1... | collective-permute-start | bytes 786440 | tf_op jit(solution)/shard_map/ppermute | solution.py:377
  140.1 11.4 %collective-permute-start.16 = (bf16[1024,128]{1,0:T(8,128)(2,1)S(1)}, bf16[1024,128]{1,0:T(8,128)(2,1)S(1)}, u32[]{:S(2)}, u32[]{:S(2)}) collective-permute-start(bf16[1024,128]{1,0:T(8,128)(2,1)S(1)} %get-tuple-element.65), channel_id=1, source_target_pairs={{0,8},{4,12},{8,0},{12,4},{1,9},{5,13},{9,1},{13,5},{2,10},{6,14},... | collective-permute-start | bytes 786440 | tf_op jit(solution)/shard_map/ppermute | solution.py:377
  143.4 10.7 %collective-permute-start.17 = (bf16[1024,128]{1,0:T(8,128)(2,1)S(1)}, bf16[1024,128]{1,0:T(8,128)(2,1)S(1)}, u32[]{:S(2)}, u32[]{:S(2)}) collective-permute-start(bf16[1024,128]{1,0:T(8,128)(2,1)S(1)} %get-tuple-element.66), channel_id=1, source_target_pairs={{0,12},{4,8},{8,4},{12,0},{1,13},{5,9},{9,5},{13,1},{2,14},{6,10},... | collective-permute-start | bytes 786440 | tf_op jit(solution)/shard_map/ppermute | solution.py:377
Sparse Core Ops, SparseCore 0:
  51.8 29.3 all-gather.1

commit v4 on v3

--- a/solution.py
+++ b/solution.py
@@ -167,8 +167,10 @@
     )(got)
 
 
-def tile_codes(index, me_x, me_z):
+def tile_codes(index, me_x, me_z, me_y, me_core):
     row, col = index[0], index[1]
+    d_y, d_core = (col >> 5) ^ me_y, ((col >> 4) & 1) ^ me_core
+    col = ((d_y ^ (d_y >> 1)) << 5) | (d_core << 4) | (col & 15)
     tile = jnp.arange(index.shape[1], dtype=jnp.int32)
     dest, inner = row >> 4, row & 15
     stream, sub = inner >> 2, inner & 3
@@ -223,8 +225,10 @@
     )(count, codes)
 
 
-def tile_kernel(group, arrays, table_ref, x_ref, tiles_ref, *refs):
-    out_refs, (held, totals, sems) = refs[:arrays], refs[arrays:]
+def tile_kernel(group, arrays, pieces, table_ref, *refs):
+    x_refs, tiles_ref, refs = refs[:pieces], refs[pieces], refs[pieces + 1 :]
+    out_refs, (held, totals, sems) = refs[:arrays], refs[-3:]
+    x_ref = x_refs[0] if pieces == 1 else refs[arrays]
     edge = held.shape[2]
     steps = (table_ref[3, group] + UNROLL - 1) // UNROLL
 
@@ -241,6 +245,11 @@
             fetch(ahead)
 
     totals[...] = jnp.zeros_like(totals)
+    if pieces > 1:
+        start = 0
+        for piece in x_refs:
+            x_ref[start : start + piece.shape[0], :] = piece[...]
+            start += piece.shape[0]
 
     def add_tiles(step, carry):
         @pl.when(step + SLOTS - 1 < steps)
@@ -267,14 +276,17 @@
         out_ref[...] = totals[array * rows : (array + 1) * rows, :].astype(BF16)
 
 
-def tile_products(group, arrays, table, x, tiles, rows):
+def tile_products(group, arrays, table, pieces, tiles, rows):
     _, edge, _ = tiles.shape
-    width = x.shape[1]
-    return pl.pallas_call(
-        functools.partial(tile_kernel, group, arrays),
-        out_shape=[jax.ShapeDtypeStruct((rows, width), BF16)] * arrays,
-        in_specs=[SMEM, VMEM, HBM],
-        out_specs=[VMEM] * arrays,
+    width = pieces[0].shape[1]
+    outs = [jax.ShapeDtypeStruct((rows, width), BF16)] * arrays
+    if len(pieces) > 1:
+        outs.append(jax.ShapeDtypeStruct((sum(p.shape[0] for p in pieces), width), BF16))
+    return pl.pallas_call(
+        functools.partial(tile_kernel, group, arrays, len(pieces)),
+        out_shape=outs,
+        in_specs=[SMEM] + [VMEM] * len(pieces) + [HBM],
+        out_specs=[VMEM] * len(outs),
         scratch_shapes=[
             pltpu.VMEM((SLOTS, UNROLL, edge, edge), BF16),
             pltpu.VMEM((arrays * rows + edge, width), F32),
@@ -285,7 +297,7 @@
             flops=5_000_000_000 * arrays, bytes_accessed=5_000_000 * arrays, transcendentals=0
         ),
         name="tile_products",
-    )(table, x, tiles)
+    )(table, *pieces, tiles)
 
 
 def wide(ref, start, rows):
@@ -363,6 +375,19 @@
     )(*terms, weight, bias.reshape(1, -1))
 
 
+def gather_pieces(own):
+    def over(array, axis, bit):
+        pairs = [(c, c ^ bit) for c in range(lax.axis_size(axis))]
+        return lax.ppermute(array, axis, pairs)
+
+    half = own.shape[0] // 2
+    one, three = over(own, "y", 1), over(own, "y", 3)
+    other = over(own, "core", 1)
+    far = [over(one[:half], "y", 3), over(three[half:], "y", 1)]
+    near = [over(piece, "core", 1) for piece in (one, three)]
+    return [own, other, one, near[0], three, near[1], *far, *(over(p, "core", 1) for p in far)]
+
+
 def swap(arrays, axis, first):
     return [
         lax.ppermute(array, axis, [(c, c ^ bit) for c in range(SIDE)])
@@ -390,25 +415,27 @@
     row_tiles = local_rows * grid_cols // tiles.shape[1]
     assert row_tiles == 256 and grid_cols == SIDE * SIDE
 
-    codes = tile_codes(tile_index[0, 0], lax.axis_index("x"), lax.axis_index("z"))
+    codes = tile_codes(
+        tile_index[0, 0], *(lax.axis_index(axis) for axis in ("x", "z", "y", "core"))
+    )
     packed = pack_rows(new_index, features, grid_rows, grid_cols, capacity)
     got = lax.all_to_all(packed, everyone, split_axis=0, concat_axis=0, tiled=True)
     table = plan_tiles(tile_count.reshape(1), codes)
     got, table = lax.optimization_barrier((got, table))
     moved_rows = place_rows(got, local_rows)
-    x = lax.all_gather(moved_rows, ("y", "core"), axis=0, tiled=True)
+    pieces = gather_pieces(moved_rows)
 
     rows = local_rows * grid_cols // 16
     axes = ("x", "z")
     pairs = (slice(0, PAIR), slice(PAIR, STREAMS))
-    sent_on = tile_products(0, STREAMS, table, x, tiles, rows)
+    *sent_on, x = tile_products(0, STREAMS, table, pieces, tiles, rows)
     got_on = [swap(sent_on[pair], axis, True) for pair, axis in zip(pairs, axes)]
-    both = tile_products(1, 2 * STREAMS, table, x, tiles, rows)
+    both = tile_products(1, 2 * STREAMS, table, [x], tiles, rows)
     got_own = [swap(both[pair], axis, True) for pair, axis in zip(pairs, axes)]
     hand = forward_sums(both[STREAMS:], got_on[0] + got_on[1])
     got_last = [swap(hand[pair], axis, False) for pair, axis in zip(pairs, axes)]
     hand, table = lax.optimization_barrier((hand, table))
-    kept = tile_products(2, STREAMS, table, x, tiles, rows)
+    kept = tile_products(2, STREAMS, table, [x], tiles, rows)
     sides = turn_sums(kept, got_own[0] + got_own[1], got_last[0] + got_last[1])
     return dense(spread(sides), weight, bias)
 

time: 165 us -> 142 us (0.86)
  Pallas kernels: 44.3 us -> 25.8 us
  starting transfers between devices: 35.1 us -> 52.2 us
  between operations: 14.2 us -> 0.81 us
  waiting for transfers between devices: 65.2 us -> 59.8 us
  local copies, waits for them, and re-layouts: 2.91 us -> 0.76 us
    all_gather x1 -> x0, waiting for transfers between devices: 29.5 us -> none  [body(): x = lax.all_gather(moved_rows, ('y', 'core'), axis=0, tiled=True)]
    ppermute x0 -> x9, waiting for transfers between devices: none -> 19.9 us  [over(): return lax.ppermute(array, axis, pairs)]
    pallas_call x3, Pallas kernels: 21.1 us -> 7.78 us  [tile_products(): pl.pallas_call(functools.partial(tile_kernel, group, arrays, len(pieces))...]
    ppermute x12, starting transfers between devices: 13.2 us -> 26.5 us  [swap(): lax.ppermute(array, axis, [(c, c ^ bit) for c in range(SIDE)])]
    ppermute x0 -> x9, starting transfers between devices: none -> 4.72 us  [over(): return lax.ppermute(array, axis, pairs)]
    all_to_all x1, waiting for transfers between devices: 12.1 us -> 16.6 us  [body(): lax.all_to_all(packed, everyone, split_axis=0, concat_axis=0, tiled=True)]
    pallas_call x1, Pallas kernels: 6.79 us -> 2.37 us  [plan_tiles(): pl.pallas_call(plan_kernel, out_shape=jax.ShapeDtypeStruct((4, codes.shap...]
    unnamed x12 -> x8, local copies, waits for them, and re-layouts: 2.91 us -> 0.72 us
  transfers between devices with their start and end apart: 20 -> 28, of which waited for: 10 -> 17; matrix products, arithmetic and copies ran while one was open for 0% -> 0% of each run, Pallas kernels for 14% -> 6%
where the time goes in v4:
time: 142 us; the launch traced here: 140 us
  waiting for transfers between devices  59.8 us (42%)
  starting transfers between devices  52.2 us (37%)
  Pallas kernels  25.8 us (18%)
    ppermute x12, starting transfers between devices, swap(): lax.ppermute(array, axis, [(c, c ^ bit) for c in range(SIDE)])  26.5 us
    ppermute x9, waiting for transfers between devices, over(): return lax.ppermute(array, axis, pairs)  19.9 us
    all_to_all x1, waiting for transfers between devices, body(): lax.all_to_all(packed, everyone, split_axis=0, concat_axis=0, tiled=True)  16.6 us
    ppermute x12, waiting for transfers between devices, swap(): lax.ppermute(array, axis, [(c, c ^ bit) for c in range(SIDE)])  14.1 us
    all_to_all x1, starting transfers between devices, body(): lax.all_to_all(packed, everyone, split_axis=0, concat_axis=0, tiled=True)  11.2 us
    ppermute x6, starting transfers between devices, spread(): lax.ppermute(sides[side][bit], axis, [(c, c ^ bit) for c in range(SIDE)])  9.87 us
    ppermute x6, waiting for transfers between devices, spread(): lax.ppermute(sides[side][bit], axis, [(c, c ^ bit) for c in range(SIDE)])  9.33 us
    pallas_call x1, Pallas kernels, pack_rows(): pl.pallas_call(functools.partial(pack_kernel, grid_rows, grid_cols, capac...  7.91 us
  transfers between devices with their start and end apart: 28, of which 17 were waited for; matrix products, arithmetic and copies ran while one was open for 0% of the time, Pallas kernels for 6%

profile of v4, /device:TPU:0, one launch (start us, length us, event | category | flops | bytes accessed | tf_op | source)
XLA Modules:
  0.0 140.1 jit_solution(2207248557581902178)
XLA Ops:
  0.0 7.9 %pack_rows.1 = bf16[128,40,128]{2,1,0:T(8,128)(2,1)} custom-call(s32[16,128]{1,0:T(8,128)} %bitcast.6, bf16[2048,128]{1,0:T(8,128)(2,1)} %rows_hbm.1), custom_call_target="tpu_custom_call" | custom-call | tf_op jit(solution)/shard_map/pack_rows/pallas_call | solution.py:112
  7.9 11.2 %all-to-all-start = ((bf16[128,40,128]{2,1,0:T(8,128)(2,1)}), bf16[128,40,128]{2,1,0:T(8,128)(2,1)S(1)}, u32[]{:S(2)}, u32[]{:S(2)}) async-start(bf16[128,40,128]{2,1,0:T(8,128)(2,1)} %pack_rows.1), calls=%async_computation | async-start | bytes 2621440 | tf_op jit(solution)/shard_map/all_to_all | solution.py:422
  19.8 0.6 fusion.3.code_ref
  20.4 2.4 %plan_tiles.1.table_ref = s32[4,656]{1,0:T(4,128)} custom-call(s32[1]{0:T(128)} %bitcast.4.count_ref, s32[640]{0:T(1024)} %fusion.3.code_ref), custom_call_target="tpu_custom_call" | custom-call | tf_op jit(solution)/shard_map/plan_tiles/pallas_call | solution.py:219
  22.8 16.6 %all-to-all-done.in_ref = bf16[128,40,128]{2,1,0:T(8,128)(2,1)S(1)} async-done(((bf16[128,40,128]{2,1,0:T(8,128)(2,1)}), bf16[128,40,128]{2,1,0:T(8,128)(2,1)S(1)}, u32[]{:S(2)}, u32[]{:S(2)}) %all-to-all-start) | async-done | bytes 1310752 | tf_op jit(solution)/shard_map/all_to_all | solution.py:422
  39.4 4.9 %place_rows.1.refs_0_ = bf16[2048,128]{1,0:T(8,128)(2,1)S(1)} custom-call(bf16[128,40,128]{2,1,0:T(8,128)(2,1)S(1)} %all-to-all-done.in_ref), custom_call_target="tpu_custom_call" | custom-call | tf_op jit(solution)/shard_map/place_rows/pallas_call | solution.py:156
  44.3 2.2 %collective-permute-start.3 = (bf16[2048,128]{1,0:T(8,128)(2,1)S(1)}, bf16[2048,128]{1,0:T(8,128)(2,1)S(1)}, u32[]{:S(2)}, u32[]{:S(2)}) collective-permute-start(bf16[2048,128]{1,0:T(8,128)(2,1)S(1)} %place_rows.1.refs_0_), channel_id=1, source_target_pairs={{0,96},{32,64},{64,32},{96,0},{1,97},{33,65},{65,33},{97,1},{2,98}... | collective-permute-start | bytes 1572872 | tf_op jit(solution)/shard_map/ppermute | solution.py:381
  46.8 12.2 %collective-permute-done.3.refs_4_ = bf16[2048,128]{1,0:T(8,128)(2,1)S(1)} collective-permute-done((bf16[2048,128]{1,0:T(8,128)(2,1)S(1)}, bf16[2048,128]{1,0:T(8,128)(2,1)S(1)}, u32[]{:S(2)}, u32[]{:S(2)}) %collective-permute-start.3) | collective-permute-done | bytes 524320 | tf_op jit(solution)/shard_map/ppermute | solution.py:381
  59.1 0.5 collective-permute-done.1.refs_2_
  59.6 1.7 %collective-permute-start.5 = (bf16[1024,128]{1,0:T(8,128)(2,1)S(1)}, bf16[1024,128]{1,0:T(8,128)(2,1)S(1)}, u32[]{:S(2)}, u32[]{:S(2)}) collective-permute-start(bf16[1024,128]{1,0:T(8,128)(2,1)S(1)} %slice.18), channel_id=1, source_target_pairs={{0,96},{32,64},{64,32},{96,0},{1,97},{33,65},{65,33},{97,1},{2,98}... | collective-permute-start | bytes 786440 | tf_op jit(solution)/shard_map/ppermute | solution.py:381
  61.3 0.5 collective-permute-start.2
  61.8 4.0 %collective-permute-done.6.refs_7_ = bf16[1024,128]{1,0:T(8,128)(2,1)S(1)} collective-permute-done((bf16[1024,128]{1,0:T(8,128)(2,1)S(1)}, bf16[1024,128]{1,0:T(8,128)(2,1)S(1)}, u32[]{:S(2)}, u32[]{:S(2)}) %collective-permute-start.6) | collective-permute-done | bytes 262176 | tf_op jit(solution)/shard_map/ppermute | solution.py:381
  65.9 1.6 %collective-permute-done.5.refs_6_ = bf16[1024,128]{1,0:T(8,128)(2,1)S(1)} collective-permute-done((bf16[1024,128]{1,0:T(8,128)(2,1)S(1)}, bf16[1024,128]{1,0:T(8,128)(2,1)S(1)}, u32[]{:S(2)}, u32[]{:S(2)}) %collective-permute-start.5) | collective-permute-done | bytes 262176 | tf_op jit(solution)/shard_map/ppermute | solution.py:381
  67.4 1.5 %collective-permute-done.7.refs_8_ = bf16[1024,128]{1,0:T(8,128)(2,1)S(1)} collective-permute-done((bf16[1024,128]{1,0:T(8,128)(2,1)S(1)}, bf16[1024,128]{1,0:T(8,128)(2,1)S(1)}, u32[]{:S(2)}, u32[]{:S(2)}) %collective-permute-start.7) | collective-permute-done | bytes 262176 | tf_op jit(solution)/shard_map/ppermute | solution.py:381
  69.0 0.7 copy-done.1
  69.7 2.3 %tile_products.3 = (bf16[2048,128]{1,0:T(8,128)(2,1)S(1)}, bf16[2048,128]{1,0:T(8,128)(2,1)S(1)}, bf16[2048,128]{1,0:T(8,128)(2,1)S(1)}, bf16[2048,128]{1,0:T(8,128)(2,1)S(1)}, bf16[16384,128]{1,0:T(8,128)(2,1)S(1)}) custom-call(s32[4,656]{1,0:T(4,128)S(1)} %copy-done.1, bf16[2048,128]{1,0:T(8,128)(2,1)S(1)} %place_rows.1.refs_0_, ...), custom_call_target="tpu_custom_call" | custom-call | flops 20000000000 | bytes 20000000 | tf_op jit(solution)/shard_map/tile_products/pallas_call | solution.py:285
  72.0 2.4 %collective-permute-start.9 = (bf16[2048,128]{1,0:T(8,128)(2,1)S(1)}, bf16[2048,128]{1,0:T(8,128)(2,1)S(1)}, u32[]{:S(2)}, u32[]{:S(2)}) collective-permute-start(bf16[2048,128]{1,0:T(8,128)(2,1)S(1)} %get-tuple-element.41), channel_id=1, source_target_pairs={{0,4},{4,0},{8,12},{12,8},{1,5},{5,1},{9,13},{13,9},{2,6},{6,2},{1... | collective-permute-start | bytes 1572872 | tf_op jit(solution)/shard_map/ppermute | solution.py:393
  74.4 4.2 %collective-permute-start.10 = (bf16[2048,128]{1,0:T(8,128)(2,1)S(1)}, bf16[2048,128]{1,0:T(8,128)(2,1)S(1)}, u32[]{:S(2)}, u32[]{:S(2)}) collective-permute-start(bf16[2048,128]{1,0:T(8,128)(2,1)S(1)} %get-tuple-element.43), channel_id=1, source_target_pairs={{0,12},{4,8},{8,4},{12,0},{1,13},{5,9},{9,5},{13,1},{2,14},{6,10},... | collective-permute-start | bytes 1572872 | tf_op jit(solution)/shard_map/ppermute | solution.py:393
  78.6 1.8 %collective-permute-start.12 = (bf16[2048,128]{1,0:T(8,128)(2,1)S(1)}, bf16[2048,128]{1,0:T(8,128)(2,1)S(1)}, u32[]{:S(2)}, u32[]{:S(2)}) collective-permute-start(bf16[2048,128]{1,0:T(8,128)(2,1)S(1)} %get-tuple-element.47), channel_id=1, source_target_pairs={{0,3},{1,2},{2,1},{3,0},{4,7},{5,6},{6,5},{7,4},{8,11},{9,10},{10,... | collective-permute-start | bytes 1572872 | tf_op jit(solution)/shard_map/ppermute | solution.py:393
  80.4 3.2 %tile_products.4 = (bf16[2048,128]{1,0:T(8,128)(2,1)S(1)}, bf16[2048,128]{1,0:T(8,128)(2,1)S(1)}, bf16[2048,128]{1,0:T(8,128)(2,1)S(1)}, bf16[2048,128]{1,0:T(8,...) custom-call(s32[4,656]{1,0:T(4,128)S(1)} %copy-done.1, ...), custom_call_target="tpu_custom_call" | custom-call | flops 40000000000 | bytes 40000000 | tf_op jit(solution)/shard_map/tile_products/pallas_call | solution.py:285
  83.5 1.4 %collective-permute-start.13 = (bf16[2048,128]{1,0:T(8,128)(2,1)S(1)}, bf16[2048,128]{1,0:T(8,128)(2,1)S(1)}, u32[]{:S(2)}, u32[]{:S(2)}) collective-permute-start(bf16[2048,128]{1,0:T(8,128)(2,1)S(1)} %get-tuple-element.54), channel_id=1, source_target_pairs={{0,4},{4,0},{8,12},{12,8},{1,5},{5,1},{9,13},{13,9},{2,6},{6,2},{1... | collective-permute-start | bytes 1572872 | tf_op jit(solution)/shard_map/ppermute | solution.py:393
  85.0 1.9 %collective-permute-done.9.refs_1_ = bf16[2048,128]{1,0:T(8,128)(2,1)S(1)} collective-permute-done((bf16[2048,128]{1,0:T(8,128)(2,1)S(1)}, bf16[2048,128]{1,0:T(8,128)(2,1)S(1)}, u32[]{:S(2)}, u32[]{:S(2)}) %collective-permute-start.9) | collective-permute-done | bytes 524320 | tf_op jit(solution)/shard_map/ppermute | solution.py:393
  86.8 5.3 %collective-permute-start.15 = (bf16[2048,128]{1,0:T(8,128)(2,1)S(1)}, bf16[2048,128]{1,0:T(8,128)(2,1)S(1)}, u32[]{:S(2)}, u32[]{:S(2)}) collective-permute-start(bf16[2048,128]{1,0:T(8,128)(2,1)S(1)} %get-tuple-element.56), channel_id=1, source_target_pairs={{0,12},{4,8},{8,4},{12,0},{1,13},{5,9},{9,5},{13,1},{2,14},{6,10},... | collective-permute-start | bytes 1572872 | tf_op jit(solution)/shard_map/ppermute | solution.py:393
  92.1 0.7 collective-permute-done.11.refs_5_
  92.8 2.4 %collective-permute-start.19 = (bf16[2048,128]{1,0:T(8,128)(2,1)S(1)}, bf16[2048,128]{1,0:T(8,128)(2,1)S(1)}, u32[]{:S(2)}, u32[]{:S(2)}) collective-permute-start(bf16[2048,128]{1,0:T(8,128)(2,1)S(1)} %get-tuple-element.60), channel_id=1, source_target_pairs={{0,3},{1,2},{2,1},{3,0},{4,7},{5,6},{6,5},{7,4},{8,11},{9,10},{10,... | collective-permute-start | bytes 1572872 | tf_op jit(solution)/shard_map/ppermute | solution.py:393
  95.1 0.5 forward_sums.1
  95.7 2.3 %collective-permute-start.14 = (bf16[2048,128]{1,0:T(8,128)(2,1)S(1)}, bf16[2048,128]{1,0:T(8,128)(2,1)S(1)}, u32[]{:S(2)}, u32[]{:S(2)}) collective-permute-start(bf16[2048,128]{1,0:T(8,128)(2,1)S(1)} %get-tuple-element.48), channel_id=1, source_target_pairs={{0,12},{4,8},{8,4},{12,0},{1,13},{5,9},{9,5},{13,1},{2,14},{6,10},... | collective-permute-start | bytes 1572872 | tf_op jit(solution)/shard_map/ppermute | solution.py:393
  98.0 0.2 collective-permute-done.13.refs_1_
  98.2 2.0 %collective-permute-start.16 = (bf16[2048,128]{1,0:T(8,128)(2,1)S(1)}, bf16[2048,128]{1,0:T(8,128)(2,1)S(1)}, u32[]{:S(2)}, u32[]{:S(2)}) collective-permute-start(bf16[2048,128]{1,0:T(8,128)(2,1)S(1)} %get-tuple-element.49), channel_id=1, source_target_pairs={{0,4},{4,0},{8,12},{12,8},{1,5},{5,1},{9,13},{13,9},{2,6},{6,2},{1... | collective-permute-start | bytes 1572872 | tf_op jit(solution)/shard_map/ppermute | solution.py:393
  100.3 4.6 %collective-permute-done.15.refs_4_ = bf16[2048,128]{1,0:T(8,128)(2,1)S(1)} collective-permute-done((bf16[2048,128]{1,0:T(8,128)(2,1)S(1)}, bf16[2048,128]{1,0:T(8,128)(2,1)S(1)}, u32[]{:S(2)}, u32[]{:S(2)}) %collective-permute-start.15) | collective-permute-done | bytes 524320 | tf_op jit(solution)/shard_map/ppermute | solution.py:393
  104.9 1.6 %collective-permute-start.18 = (bf16[2048,128]{1,0:T(8,128)(2,1)S(1)}, bf16[2048,128]{1,0:T(8,128)(2,1)S(1)}, u32[]{:S(2)}, u32[]{:S(2)}) collective-permute-start(bf16[2048,128]{1,0:T(8,128)(2,1)S(1)} %get-tuple-element.50), channel_id=1, source_target_pairs={{0,3},{1,2},{2,1},{3,0},{4,7},{5,6},{6,5},{7,4},{8,11},{9,10},{10,... | collective-permute-start | bytes 1572872 | tf_op jit(solution)/shard_map/ppermute | solution.py:393
  106.5 3.1 %collective-permute-start.20 = (bf16[2048,128]{1,0:T(8,128)(2,1)S(1)}, bf16[2048,128]{1,0:T(8,128)(2,1)S(1)}, u32[]{:S(2)}, u32[]{:S(2)}) collective-permute-start(bf16[2048,128]{1,0:T(8,128)(2,1)S(1)} %get-tuple-element.51), channel_id=1, source_target_pairs={{0,1},{1,0},{2,3},{3,2},{4,5},{5,4},{6,7},{7,6},{8,9},{9,8},{10,11... | collective-permute-start | bytes 1572872 | tf_op jit(solution)/shard_map/ppermute | solution.py:393
  109.6 2.3 %tile_products.5 = (bf16[2048,128]{1,0:T(8,128)(2,1)S(1)}, bf16[2048,128]{1,0:T(8,128)(2,1)S(1)}, bf16[2048,128]{1,0:T(8,128)(2,1)S(1)}, bf16[2048,128]{1,0:T(8,128)(2,1)S(1)}) custom-call(s32[4,656]{1,0:T(4,128)S(1)} %copy-done.1, bf16[16384,128]{1,0:T(8,128)(2,1)S(1)} %get-tuple-element.39.refs_0_, bf16[640,128,128]{2,1,0:T(8,128)(2,1)} %bitcast.9), custom_call_target="tpu_custom_call" | custom-call | flops 20000000000 | bytes 20000000 | tf_op jit(solution)/shard_map/tile_products/pallas_call | solution.py:285
  112.0 2.3 %collective-permute-done.14.refs_2_ = bf16[2048,128]{1,0:T(8,128)(2,1)S(1)} collective-permute-done((bf16[2048,128]{1,0:T(8,128)(2,1)S(1)}, bf16[2048,128]{1,0:T(8,128)(2,1)S(1)}, u32[]{:S(2)}, u32[]{:S(2)}) %collective-permute-start.14) | collective-permute-done | bytes 524320 | tf_op jit(solution)/shard_map/ppermute | solution.py:393
  114.3 4.3 %collective-permute-done.18.refs_8_ = bf16[2048,128]{1,0:T(8,128)(2,1)S(1)} collective-permute-done((bf16[2048,128]{1,0:T(8,128)(2,1)S(1)}, bf16[2048,128]{1,0:T(8,128)(2,1)S(1)}, u32[]{:S(2)}, u32[]{:S(2)}) %collective-permute-start.18) | collective-permute-done | bytes 524320 | tf_op jit(solution)/shard_map/ppermute | solution.py:393
  118.6 0.8 turn_sums.1
  119.4 0.3 collective-permute-start.21
  119.7 1.6 %collective-permute-start.22 = (bf16[1024,128]{1,0:T(8,128)(2,1)S(1)}, bf16[1024,128]{1,0:T(8,128)(2,1)S(1)}, u32[]{:S(2)}, u32[]{:S(2)}) collective-permute-start(bf16[1024,128]{1,0:T(8,128)(2,1)S(1)} %get-tuple-element.63), channel_id=1, source_target_pairs={{0,2},{1,3},{2,0},{3,1},{4,6},{5,7},{6,4},{7,5},{8,10},{9,11},{10,... | collective-permute-start | bytes 786440 | tf_op jit(solution)/shard_map/ppermute | solution.py:402
  121.2 3.0 %collective-permute-start.23 = (bf16[1024,128]{1,0:T(8,128)(2,1)S(1)}, bf16[1024,128]{1,0:T(8,128)(2,1)S(1)}, u32[]{:S(2)}, u32[]{:S(2)}) collective-permute-start(bf16[1024,128]{1,0:T(8,128)(2,1)S(1)} %get-tuple-element.64), channel_id=1, source_target_pairs={{0,3},{1,2},{2,1},{3,0},{4,7},{5,6},{6,5},{7,4},{8,11},{9,10},{10,... | collective-permute-start | bytes 786440 | tf_op jit(solution)/shard_map/ppermute | solution.py:402
  124.2 0.4 collective-permute-start.24
  124.6 3.1 %collective-permute-start.25 = (bf16[1024,128]{1,0:T(8,128)(2,1)S(1)}, bf16[1024,128]{1,0:T(8,128)(2,1)S(1)}, u32[]{:S(2)}, u32[]{:S(2)}) collective-permute-start(bf16[1024,128]{1,0:T(8,128)(2,1)S(1)} %get-tuple-element.67), channel_id=1, source_target_pairs={{0,8},{4,12},{8,0},{12,4},{1,9},{5,13},{9,1},{13,5},{2,10},{6,14},... | collective-permute-start | bytes 786440 | tf_op jit(solution)/shard_map/ppermute | solution.py:402
  127.7 0.5 collective-permute-done.21.refs_1_
  128.2 1.6 %collective-permute-start.26 = (bf16[1024,128]{1,0:T(8,128)(2,1)S(1)}, bf16[1024,128]{1,0:T(8,128)(2,1)S(1)}, u32[]{:S(2)}, u32[]{:S(2)}) collective-permute-start(bf16[1024,128]{1,0:T(8,128)(2,1)S(1)} %get-tuple-element.68), channel_id=1, source_target_pairs={{0,12},{4,8},{8,4},{12,0},{1,13},{5,9},{9,5},{13,1},{2,14},{6,10},... | collective-permute-start | bytes 786440 | tf_op jit(solution)/shard_map/ppermute | solution.py:402
  129.8 0.3 collective-permute-done.22.refs_2_
  130.1 2.7 %collective-permute-done.23.refs_3_ = bf16[1024,128]{1,0:T(8,128)(2,1)S(1)} collective-permute-done((bf16[1024,128]{1,0:T(8,128)(2,1)S(1)}, bf16[1024,128]{1,0:T(8,128)(2,1)S(1)}, u32[]{:S(2)}, u32[]{:S(2)}) %collective-permute-start.23) | collective-permute-done | bytes 262176 | tf_op jit(solution)/shard_map/ppermute | solution.py:402
  132.8 3.3 %collective-permute-done.25.refs_6_ = bf16[1024,128]{1,0:T(8,128)(2,1)S(1)} collective-permute-done((bf16[1024,128]{1,0:T(8,128)(2,1)S(1)}, bf16[1024,128]{1,0:T(8,128)(2,1)S(1)}, u32[]{:S(2)}, u32[]{:S(2)}) %collective-permute-start.25) | collective-permute-done | bytes 262176 | tf_op jit(solution)/shard_map/ppermute | solution.py:402
  136.1 2.5 %collective-permute-done.26.refs_7_ = bf16[1024,128]{1,0:T(8,128)(2,1)S(1)} collective-permute-done((bf16[1024,128]{1,0:T(8,128)(2,1)S(1)}, bf16[1024,128]{1,0:T(8,128)(2,1)S(1)}, u32[]{:S(2)}, u32[]{:S(2)}) %collective-permute-start.26) | collective-permute-done | bytes 262176 | tf_op jit(solution)/shard_map/ppermute | solution.py:402
  138.6 1.5 %dense.1 = bf16[2048,256]{1,0:T(8,128)(2,1)} custom-call(f32[1024,128]{1,0:T(8,128)S(1)} %get-tuple-element.61.refs_0_, bf16[1024,128]{1,0:T(8,128)(2,1)S(1)} %collective-permute-done.21.refs_1_, bf16[1024,128]{1,0:T(8,128)(2,1)S(1)} %collective-permute-done.22.refs_2_, bf16[1024,128]{1,0:T(8,128)(2,1)S(1)} %collective-permute-done.23.refs_3_, ...), custom_call_target="tpu_custom_call" | custom-call | tf_op jit(solution)/shard_map/dense/pallas_call | solution.py:368
  (29 shorter events, 0.5 us)
Async XLA Ops:
  0.0 19.7 %copy-start.3 = (s32[1,1,2,640]{3,2,1,0:T(2,128)S(1)}, s32[1,1,2,640]{3,2,1,0:T(2,128)}, u32[]{:S(2)}) copy-start(s32[1,1,2,640]{3,2,1,0:T(2,128)} %param.10) | copy-start | bytes 15364
  7.9 31.5 %all-to-all-start = ((bf16[128,40,128]{2,1,0:T(8,128)(2,1)}), bf16[128,40,128]{2,1,0:T(8,128)(2,1)S(1)}, u32[]{:S(2)}, u32[]{:S(2)}) async-start(bf16[128,40,128]{2,1,0:T(8,128)(2,1)} %pack_rows.1), calls=%async_computation | async-start | bytes 2621440 | tf_op jit(solution)/shard_map/all_to_all | solution.py:422
  44.3 14.6 %collective-permute-start.3 = (bf16[2048,128]{1,0:T(8,128)(2,1)S(1)}, bf16[2048,128]{1,0:T(8,128)(2,1)S(1)}, u32[]{:S(2)}, u32[]{:S(2)}) collective-permute-start(bf16[2048,128]{1,0:T(8,128)(2,1)S(1)} %place_rows.1.refs_0_), channel_id=1, source_target_pairs={{0,96},{32,64},{64,32},{96,0},{1,97},{33,65},{65,33},{97,1},{2,98}... | collective-permute-start | bytes 1572872 | tf_op jit(solution)/shard_map/ppermute | solution.py:381
  46.5 13.1 %collective-permute-start.1 = (bf16[2048,128]{1,0:T(8,128)(2,1)S(1)}, bf16[2048,128]{1,0:T(8,128)(2,1)S(1)}, u32[]{:S(2)}, u32[]{:S(2)}) collective-permute-start(bf16[2048,128]{1,0:T(8,128)(2,1)S(1)} %place_rows.1.refs_0_), channel_id=1, source_target_pairs={{0,32},{32,0},{64,96},{96,64},{1,33},{33,1},{65,97},{97,65},{2,34}... | collective-permute-start | bytes 1572872 | tf_op jit(solution)/shard_map/ppermute | solution.py:381
  46.8 20.7 %collective-permute-start = (bf16[2048,128]{1,0:T(8,128)(2,1)S(1)}, bf16[2048,128]{1,0:T(8,128)(2,1)S(1)}, u32[]{:S(2)}, u32[]{:S(2)}) collective-permute-start(bf16[2048,128]{1,0:T(8,128)(2,1)S(1)} %place_rows.1.refs_0_), channel_id=1, source_target_pairs={{0,16},{16,0},{1,17},{17,1},{2,18},{18,2},{3,19},{19,3},{4,20},{20... | collective-permute-start | bytes 1572872 | tf_op jit(solution)/shard_map/ppermute | solution.py:381
  59.0 6.9 %collective-permute-start.6 = (bf16[1024,128]{1,0:T(8,128)(2,1)S(1)}, bf16[1024,128]{1,0:T(8,128)(2,1)S(1)}, u32[]{:S(2)}, u32[]{:S(2)}) collective-permute-start(bf16[1024,128]{1,0:T(8,128)(2,1)S(1)} %slice.19), channel_id=1, source_target_pairs={{0,32},{32,0},{64,96},{96,64},{1,33},{33,1},{65,97},{97,65},{2,34}... | collective-permute-start | bytes 786440 | tf_op jit(solution)/shard_map/ppermute | solution.py:381
  59.6 7.8 %collective-permute-start.5 = (bf16[1024,128]{1,0:T(8,128)(2,1)S(1)}, bf16[1024,128]{1,0:T(8,128)(2,1)S(1)}, u32[]{:S(2)}, u32[]{:S(2)}) collective-permute-start(bf16[1024,128]{1,0:T(8,128)(2,1)S(1)} %slice.18), channel_id=1, source_target_pairs={{0,96},{32,64},{64,32},{96,0},{1,97},{33,65},{65,33},{97,1},{2,98}... | collective-permute-start | bytes 786440 | tf_op jit(solution)/shard_map/ppermute | solution.py:381
  61.3 7.6 %collective-permute-start.4 = (bf16[2048,128]{1,0:T(8,128)(2,1)S(1)}, bf16[2048,128]{1,0:T(8,128)(2,1)S(1)}, u32[]{:S(2)}, u32[]{:S(2)}) collective-permute-start(bf16[2048,128]{1,0:T(8,128)(2,1)S(1)} %collective-permute-done.3.refs_4_), channel_id=1, source_target_pairs={{0,16},{16,0},{1,17},{17,1},{2,18},{18,2},{3,19},{19,3},{4,20},{20... | collective-permute-start | bytes 1572872 | tf_op jit(solution)/shard_map/ppermute | solution.py:381
  61.3 7.6 %collective-permute-start.2 = (bf16[2048,128]{1,0:T(8,128)(2,1)S(1)}, bf16[2048,128]{1,0:T(8,128)(2,1)S(1)}, u32[]{:S(2)}, u32[]{:S(2)}) collective-permute-start(bf16[2048,128]{1,0:T(8,128)(2,1)S(1)} %collective-permute-done.1.refs_2_), channel_id=1, source_target_pairs={{0,16},{16,0},{1,17},{17,1},{2,18},{18,2},{3,19},{19,3},{4,20},{20... | collective-permute-start | bytes 1572872 | tf_op jit(solution)/shard_map/ppermute | solution.py:381
  65.9 1.6 %collective-permute-start.8 = (bf16[1024,128]{1,0:T(8,128)(2,1)S(1)}, bf16[1024,128]{1,0:T(8,128)(2,1)S(1)}, u32[]{:S(2)}, u32[]{:S(2)}) collective-permute-start(bf16[1024,128]{1,0:T(8,128)(2,1)S(1)} %collective-permute-done.6.refs_7_), channel_id=1, source_target_pairs={{0,16},{16,0},{1,17},{17,1},{2,18},{18,2},{3,19},{19,3},{4,20},{20... | collective-permute-start | bytes 786440 | tf_op jit(solution)/shard_map/ppermute | solution.py:381
  67.4 1.5 %collective-permute-start.7 = (bf16[1024,128]{1,0:T(8,128)(2,1)S(1)}, bf16[1024,128]{1,0:T(8,128)(2,1)S(1)}, u32[]{:S(2)}, u32[]{:S(2)}) collective-permute-start(bf16[1024,128]{1,0:T(8,128)(2,1)S(1)} %collective-permute-done.5.refs_6_), channel_id=1, source_target_pairs={{0,16},{16,0},{1,17},{17,1},{2,18},{18,2},{3,19},{19,3},{4,20},{20... | collective-permute-start | bytes 786440 | tf_op jit(solution)/shard_map/ppermute | solution.py:381
  69.0 0.7 copy-start.1
  72.0 14.8 %collective-permute-start.9 = (bf16[2048,128]{1,0:T(8,128)(2,1)S(1)}, bf16[2048,128]{1,0:T(8,128)(2,1)S(1)}, u32[]{:S(2)}, u32[]{:S(2)}) collective-permute-start(bf16[2048,128]{1,0:T(8,128)(2,1)S(1)} %get-tuple-element.41), channel_id=1, source_target_pairs={{0,4},{4,0},{8,12},{12,8},{1,5},{5,1},{9,13},{13,9},{2,6},{6,2},{1... | collective-permute-start | bytes 1572872 | tf_op jit(solution)/shard_map/ppermute | solution.py:393
  74.4 17.7 %collective-permute-start.10 = (bf16[2048,128]{1,0:T(8,128)(2,1)S(1)}, bf16[2048,128]{1,0:T(8,128)(2,1)S(1)}, u32[]{:S(2)}, u32[]{:S(2)}) collective-permute-start(bf16[2048,128]{1,0:T(8,128)(2,1)S(1)} %get-tuple-element.43), channel_id=1, source_target_pairs={{0,12},{4,8},{8,4},{12,0},{1,13},{5,9},{9,5},{13,1},{2,14},{6,10},... | collective-permute-start | bytes 1572872 | tf_op jit(solution)/shard_map/ppermute | solution.py:393
  78.6 14.2 %collective-permute-start.11 = (bf16[2048,128]{1,0:T(8,128)(2,1)S(1)}, bf16[2048,128]{1,0:T(8,128)(2,1)S(1)}, u32[]{:S(2)}, u32[]{:S(2)}) collective-permute-start(bf16[2048,128]{1,0:T(8,128)(2,1)S(1)} %get-tuple-element.45), channel_id=1, source_target_pairs={{0,1},{1,0},{2,3},{3,2},{4,5},{5,4},{6,7},{7,6},{8,9},{9,8},{10,11... | collective-permute-start | bytes 1572872 | tf_op jit(solution)/shard_map/ppermute | solution.py:393
  78.6 16.6 %collective-permute-start.12 = (bf16[2048,128]{1,0:T(8,128)(2,1)S(1)}, bf16[2048,128]{1,0:T(8,128)(2,1)S(1)}, u32[]{:S(2)}, u32[]{:S(2)}) collective-permute-start(bf16[2048,128]{1,0:T(8,128)(2,1)S(1)} %get-tuple-element.47), channel_id=1, source_target_pairs={{0,3},{1,2},{2,1},{3,0},{4,7},{5,6},{6,5},{7,4},{8,11},{9,10},{10,... | collective-permute-start | bytes 1572872 | tf_op jit(solution)/shard_map/ppermute | solution.py:393
  83.5 14.7 %collective-permute-start.13 = (bf16[2048,128]{1,0:T(8,128)(2,1)S(1)}, bf16[2048,128]{1,0:T(8,128)(2,1)S(1)}, u32[]{:S(2)}, u32[]{:S(2)}) collective-permute-start(bf16[2048,128]{1,0:T(8,128)(2,1)S(1)} %get-tuple-element.54), channel_id=1, source_target_pairs={{0,4},{4,0},{8,12},{12,8},{1,5},{5,1},{9,13},{13,9},{2,6},{6,2},{1... | collective-permute-start | bytes 1572872 | tf_op jit(solution)/shard_map/ppermute | solution.py:393
  86.8 18.1 %collective-permute-start.15 = (bf16[2048,128]{1,0:T(8,128)(2,1)S(1)}, bf16[2048,128]{1,0:T(8,128)(2,1)S(1)}, u32[]{:S(2)}, u32[]{:S(2)}) collective-permute-start(bf16[2048,128]{1,0:T(8,128)(2,1)S(1)} %get-tuple-element.56), channel_id=1, source_target_pairs={{0,12},{4,8},{8,4},{12,0},{1,13},{5,9},{9,5},{13,1},{2,14},{6,10},... | collective-permute-start | bytes 1572872 | tf_op jit(solution)/shard_map/ppermute | solution.py:393
  92.1 14.4 %collective-permute-start.17 = (bf16[2048,128]{1,0:T(8,128)(2,1)S(1)}, bf16[2048,128]{1,0:T(8,128)(2,1)S(1)}, u32[]{:S(2)}, u32[]{:S(2)}) collective-permute-start(bf16[2048,128]{1,0:T(8,128)(2,1)S(1)} %get-tuple-element.58), channel_id=1, source_target_pairs={{0,1},{1,0},{2,3},{3,2},{4,5},{5,4},{6,7},{7,6},{8,9},{9,8},{10,11... | collective-permute-start | bytes 1572872 | tf_op jit(solution)/shard_map/ppermute | solution.py:393
  92.8 19.2 %collective-permute-start.19 = (bf16[2048,128]{1,0:T(8,128)(2,1)S(1)}, bf16[2048,128]{1,0:T(8,128)(2,1)S(1)}, u32[]{:S(2)}, u32[]{:S(2)}) collective-permute-start(bf16[2048,128]{1,0:T(8,128)(2,1)S(1)} %get-tuple-element.60), channel_id=1, source_target_pairs={{0,3},{1,2},{2,1},{3,0},{4,7},{5,6},{6,5},{7,4},{8,11},{9,10},{10,... | collective-permute-start | bytes 1572872 | tf_op jit(solution)/shard_map/ppermute | solution.py:393
  95.7 18.6 %collective-permute-start.14 = (bf16[2048,128]{1,0:T(8,128)(2,1)S(1)}, bf16[2048,128]{1,0:T(8,128)(2,1)S(1)}, u32[]{:S(2)}, u32[]{:S(2)}) collective-permute-start(bf16[2048,128]{1,0:T(8,128)(2,1)S(1)} %get-tuple-element.48), channel_id=1, source_target_pairs={{0,12},{4,8},{8,4},{12,0},{1,13},{5,9},{9,5},{13,1},{2,14},{6,10},... | collective-permute-start | bytes 1572872 | tf_op jit(solution)/shard_map/ppermute | solution.py:393
  98.2 16.1 %collective-permute-start.16 = (bf16[2048,128]{1,0:T(8,128)(2,1)S(1)}, bf16[2048,128]{1,0:T(8,128)(2,1)S(1)}, u32[]{:S(2)}, u32[]{:S(2)}) collective-permute-start(bf16[2048,128]{1,0:T(8,128)(2,1)S(1)} %get-tuple-element.49), channel_id=1, source_target_pairs={{0,4},{4,0},{8,12},{12,8},{1,5},{5,1},{9,13},{13,9},{2,6},{6,2},{1... | collective-permute-start | bytes 1572872 | tf_op jit(solution)/shard_map/ppermute | solution.py:393
  104.9 13.7 %collective-permute-start.18 = (bf16[2048,128]{1,0:T(8,128)(2,1)S(1)}, bf16[2048,128]{1,0:T(8,128)(2,1)S(1)}, u32[]{:S(2)}, u32[]{:S(2)}) collective-permute-start(bf16[2048,128]{1,0:T(8,128)(2,1)S(1)} %get-tuple-element.50), channel_id=1, source_target_pairs={{0,3},{1,2},{2,1},{3,0},{4,7},{5,6},{6,5},{7,4},{8,11},{9,10},{10,... | collective-permute-start | bytes 1572872 | tf_op jit(solution)/shard_map/ppermute | solution.py:393
  106.5 12.1 %collective-permute-start.20 = (bf16[2048,128]{1,0:T(8,128)(2,1)S(1)}, bf16[2048,128]{1,0:T(8,128)(2,1)S(1)}, u32[]{:S(2)}, u32[]{:S(2)}) collective-permute-start(bf16[2048,128]{1,0:T(8,128)(2,1)S(1)} %get-tuple-element.51), channel_id=1, source_target_pairs={{0,1},{1,0},{2,3},{3,2},{4,5},{5,4},{6,7},{7,6},{8,9},{9,8},{10,11... | collective-permute-start | bytes 1572872 | tf_op jit(solution)/shard_map/ppermute | solution.py:393
  111.9 26.7 %copy-start = (bf16[128,256]{1,0:T(8,128)(2,1)S(1)}, bf16[128,256]{1,0:T(8,128)(2,1)}, u32[]{:S(2)}) copy-start(bf16[128,256]{1,0:T(8,128)(2,1)} %refs_8_.1) | copy-start | bytes 196612
  111.9 26.7 %copy-start.2 = (f32[256]{0:T(256)S(1)}, f32[256]{0:T(256)}, u32[]{:S(2)}) copy-start(f32[256]{0:T(256)} %param.13) | copy-start | bytes 3076
  119.4 8.8 %collective-permute-start.21 = (bf16[1024,128]{1,0:T(8,128)(2,1)S(1)}, bf16[1024,128]{1,0:T(8,128)(2,1)S(1)}, u32[]{:S(2)}, u32[]{:S(2)}) collective-permute-start(bf16[1024,128]{1,0:T(8,128)(2,1)S(1)} %get-tuple-element.62), channel_id=1, source_target_pairs={{0,1},{1,0},{2,3},{3,2},{4,5},{5,4},{6,7},{7,6},{8,9},{9,8},{10,11... | collective-permute-start | bytes 786440 | tf_op jit(solution)/shard_map/ppermute | solution.py:402
  119.7 10.4 %collective-permute-start.22 = (bf16[1024,128]{1,0:T(8,128)(2,1)S(1)}, bf16[1024,128]{1,0:T(8,128)(2,1)S(1)}, u32[]{:S(2)}, u32[]{:S(2)}) collective-permute-start(bf16[1024,128]{1,0:T(8,128)(2,1)S(1)} %get-tuple-element.63), channel_id=1, source_target_pairs={{0,2},{1,3},{2,0},{3,1},{4,6},{5,7},{6,4},{7,5},{8,10},{9,11},{10,... | collective-permute-start | bytes 786440 | tf_op jit(solution)/shard_map/ppermute | solution.py:402
  121.2 11.6 %collective-permute-start.23 = (bf16[1024,128]{1,0:T(8,128)(2,1)S(1)}, bf16[1024,128]{1,0:T(8,128)(2,1)S(1)}, u32[]{:S(2)}, u32[]{:S(2)}) collective-permute-start(bf16[1024,128]{1,0:T(8,128)(2,1)S(1)} %get-tuple-element.64), channel_id=1, source_target_pairs={{0,3},{1,2},{2,1},{3,0},{4,7},{5,6},{6,5},{7,4},{8,11},{9,10},{10,... | collective-permute-start | bytes 786440 | tf_op jit(solution)/shard_map/ppermute | solution.py:402
  124.2 8.6 %collective-permute-start.24 = (bf16[1024,128]{1,0:T(8,128)(2,1)S(1)}, bf16[1024,128]{1,0:T(8,128)(2,1)S(1)}, u32[]{:S(2)}, u32[]{:S(2)}) collective-permute-start(bf16[1024,128]{1,0:T(8,128)(2,1)S(1)} %get-tuple-element.66), channel_id=1, source_target_pairs={{0,4},{4,0},{8,12},{12,8},{1,5},{5,1},{9,13},{13,9},{2,6},{6,2},{1... | collective-permute-start | bytes 786440 | tf_op jit(solution)/shard_map/ppermute | solution.py:402
  124.6 11.5 %collective-permute-start.25 = (bf16[1024,128]{1,0:T(8,128)(2,1)S(1)}, bf16[1024,128]{1,0:T(8,128)(2,1)S(1)}, u32[]{:S(2)}, u32[]{:S(2)}) collective-permute-start(bf16[1024,128]{1,0:T(8,128)(2,1)S(1)} %get-tuple-element.67), channel_id=1, source_target_pairs={{0,8},{4,12},{8,0},{12,4},{1,9},{5,13},{9,1},{13,5},{2,10},{6,14},... | collective-permute-start | bytes 786440 | tf_op jit(solution)/shard_map/ppermute | solution.py:402
  128.2 10.4 %collective-permute-start.26 = (bf16[1024,128]{1,0:T(8,128)(2,1)S(1)}, bf16[1024,128]{1,0:T(8,128)(2,1)S(1)}, u32[]{:S(2)}, u32[]{:S(2)}) collective-permute-start(bf16[1024,128]{1,0:T(8,128)(2,1)S(1)} %get-tuple-element.68), channel_id=1, source_target_pairs={{0,12},{4,8},{8,4},{12,0},{1,13},{5,9},{9,5},{13,1},{2,14},{6,10},... | collective-permute-start | bytes 786440 | tf_op jit(solution)/shard_map/ppermute | solution.py:402

commit v5 on v3

--- a/solution.py
+++ b/solution.py
@@ -167,8 +167,11 @@
     )(got)
 
 
-def tile_codes(index, me_x, me_z):
+def tile_codes(index, me_x, me_z, me_y, me_core):
     row, col = index[0], index[1]
+    owner = (((col >> 5) ^ me_y) << 1) | (((col >> 4) & 1) ^ me_core)
+    block = (0x53764210 >> (4 * owner)) & 7
+    col = (block << 4) | (col & 15)
     tile = jnp.arange(index.shape[1], dtype=jnp.int32)
     dest, inner = row >> 4, row & 15
     stream, sub = inner >> 2, inner & 3
@@ -179,20 +182,21 @@
     place = stream * 16 + second * 4 + sub
     group = jnp.where(first == 0, 2, jnp.where(first == 2, 0, 1))
     place = place + jnp.where((group == 1) & (first != near), 64, 0)
+    group = jnp.where((group == 0) & (block >= 6), 3, group)
     return (group << 25) | (tile << 15) | (place << 7) | col
 
 
 def plan_kernel(count_ref, code_ref, table_ref):
-    for group in range(3):
-        table_ref[3, group] = 0
+    for group in range(4):
+        table_ref[4, group] = 0
 
     def visit(step, carry):
         for sub in range(8):
             code = code_ref[step * 8 + sub]
             group = code >> 25
-            at = table_ref[3, group]
+            at = table_ref[4, group]
             table_ref[group, at] = code
-            table_ref[3, group] = at + 1
+            table_ref[4, group] = at + 1
         return carry
 
     count = count_ref[0]
@@ -202,31 +206,30 @@
     def visit_one(tile, carry):
         code = code_ref[tile]
         group = code >> 25
-        at = table_ref[3, group]
+        at = table_ref[4, group]
         table_ref[group, at] = code
-        table_ref[3, group] = at + 1
+        table_ref[4, group] = at + 1
         return carry
 
     lax.fori_loop(full * 8, count, visit_one, 0)
-    for group in range(3):
+    for group in range(4):
         for step in range(UNROLL):
-            table_ref[group, table_ref[3, group] + step] = 128 << 7
+            table_ref[group, table_ref[4, group] + step] = 128 << 7
 
 
 def plan_tiles(count, codes):
     return pl.pallas_call(
         plan_kernel,
-        out_shape=jax.ShapeDtypeStruct((4, codes.shape[0] + UNROLL), jnp.int32),
+        out_shape=jax.ShapeDtypeStruct((5, codes.shape[0] + UNROLL), jnp.int32),
         in_specs=[SMEM] * 2,
         out_specs=SMEM,
         name="plan_tiles",
     )(count, codes)
 
 
-def tile_kernel(group, arrays, table_ref, x_ref, tiles_ref, *refs):
-    out_refs, (held, totals, sems) = refs[:arrays], refs[arrays:]
+def add_list(group, table_ref, x_ref, tiles_ref, held, totals, sems, prepare):
     edge = held.shape[2]
-    steps = (table_ref[3, group] + UNROLL - 1) // UNROLL
+    steps = (table_ref[4, group] + UNROLL - 1) // UNROLL
 
     def fetch(step):
         lane = lax.rem(step, SLOTS)
@@ -240,7 +243,7 @@
         def _():
             fetch(ahead)
 
-    totals[...] = jnp.zeros_like(totals)
+    prepare()
 
     def add_tiles(step, carry):
         @pl.when(step + SLOTS - 1 < steps)
@@ -262,30 +265,116 @@
         return carry
 
     lax.fori_loop(0, steps, add_tiles, 0)
+
+
+def write_totals(totals, out_refs):
     rows = out_refs[0].shape[0]
     for array, out_ref in enumerate(out_refs):
         out_ref[...] = totals[array * rows : (array + 1) * rows, :].astype(BF16)
 
 
+def join(pieces, out_ref, start):
+    for piece in pieces:
+        out_ref[start : start + piece.shape[0], :] = piece[...]
+        start += piece.shape[0]
+
+
+def early_kernel(group, pieces, table_ref, *refs):
+    x_refs, (tiles_ref, x_out, totals, held, sems) = refs[:pieces], refs[pieces:]
+
+    def prepare():
+        totals[...] = jnp.zeros_like(totals)
+        join(x_refs, x_out, 0)
+
+    add_list(group, table_ref, x_out, tiles_ref, held, totals, sems, prepare)
+
+
+def late_kernel(group, arrays, pieces, table_ref, *refs):
+    x_refs, (tiles_ref, x_in, totals_in, x_out, totals), refs = (
+        refs[:pieces],
+        refs[pieces : pieces + 5],
+        refs[pieces + 5 :],
+    )
+    out_refs, (held, sems) = refs[:arrays], refs[arrays:]
+    rows = sum(piece.shape[0] for piece in x_refs)
+
+    def prepare():
+        join(x_refs, x_out, x_out.shape[0] - rows)
+
+    add_list(group, table_ref, x_out, tiles_ref, held, totals, sems, prepare)
+    write_totals(totals, out_refs)
+
+
+def tile_kernel(group, arrays, table_ref, x_ref, tiles_ref, *refs):
+    out_refs, (totals, held, sems) = refs[:arrays], refs[arrays:]
+
+    def prepare():
+        totals[...] = jnp.zeros_like(totals)
+
+    add_list(group, table_ref, x_ref, tiles_ref, held, totals, sems, prepare)
+    write_totals(totals, out_refs)
+
+
+def tile_scratch(tiles):
+    _, edge, _ = tiles.shape
+    return [pltpu.VMEM((SLOTS, UNROLL, edge, edge), BF16), pltpu.SemaphoreType.DMA((SLOTS,))]
+
+
+def work(arrays):
+    return pl.CostEstimate(
+        flops=5_000_000_000 * arrays, bytes_accessed=5_000_000 * arrays, transcendentals=0
+    )
+
+
 def tile_products(group, arrays, table, x, tiles, rows):
-    _, edge, _ = tiles.shape
-    width = x.shape[1]
+    edge, width = tiles.shape[1], x.shape[1]
     return pl.pallas_call(
         functools.partial(tile_kernel, group, arrays),
         out_shape=[jax.ShapeDtypeStruct((rows, width), BF16)] * arrays,
         in_specs=[SMEM, VMEM, HBM],
         out_specs=[VMEM] * arrays,
-        scratch_shapes=[
-            pltpu.VMEM((SLOTS, UNROLL, edge, edge), BF16),
-            pltpu.VMEM((arrays * rows + edge, width), F32),
-            pltpu.SemaphoreType.DMA((SLOTS,)),
-        ],
-        compiler_params=params(32),
-        cost_estimate=pl.CostEstimate(
-            flops=5_000_000_000 * arrays, bytes_accessed=5_000_000 * arrays, transcendentals=0
-        ),
+        scratch_shapes=[pltpu.VMEM((arrays * rows + edge, width), F32), *tile_scratch(tiles)],
+        compiler_params=params(32),
+        cost_estimate=work(arrays),
         name="tile_products",
     )(table, x, tiles)
+
+
+def early_products(group, arrays, table, pieces, x_rows, tiles, rows):
+    edge, width = tiles.shape[1], pieces[0].shape[1]
+    return pl.pallas_call(
+        functools.partial(early_kernel, group, len(pieces)),
+        out_shape=[
+            jax.ShapeDtypeStruct((x_rows, width), BF16),
+            jax.ShapeDtypeStruct((arrays * rows + edge, width), F32),
+        ],
+        in_specs=[SMEM] + [VMEM] * len(pieces) + [HBM],
+        out_specs=[VMEM] * 2,
+        scratch_shapes=tile_scratch(tiles),
+        compiler_params=params(32),
+        cost_estimate=work(1),
+        name="early_products",
+    )(table, *pieces, tiles)
+
+
+def late_products(group, arrays, table, pieces, x, totals, tiles, rows):
+    width = x.shape[1]
+    at = len(pieces) + 2
+    return pl.pallas_call(
+        functools.partial(late_kernel, group, arrays, len(pieces)),
+        out_shape=[
+            jax.ShapeDtypeStruct(x.shape, x.dtype),
+            jax.ShapeDtypeStruct(totals.shape, totals.dtype),
+        ]
+        + [jax.ShapeDtypeStruct((rows, width), BF16)] * arrays,
+        in_specs=[SMEM] + [VMEM] * len(pieces) + [HBM, VMEM, VMEM],
+        out_specs=[VMEM] * (2 + arrays),
+        scratch_shapes=tile_scratch(tiles),
+        input_output_aliases={at: 0, at + 1: 1},
+        compiler_params=params(32),
+        cost_estimate=work(1),
+        name="late_products",
+    )(table, *pieces, tiles, x, totals)
 
 
 def wide(ref, start, rows):
@@ -311,15 +400,15 @@
 
 
 def turn_kernel(*refs):
-    outs = refs[3 * STREAMS :]
-    for stream in range(STREAMS):
+    outs = refs[3 * PAIR :]
+    for stream in range(PAIR):
         kept, got, last = refs[3 * stream : 3 * stream + 3]
         rows = last.shape[0] // SIDE
-        at = stream % PAIR * rows
+        at = stream * rows
         for delta in range(SIDE):
             start = delta * rows
             total = wide(kept, start, rows) + wide(got, start, rows) + wide(last, start, rows)
-            out = outs[stream // PAIR * SIDE + delta]
+            out = outs[delta]
             out[at : at + rows, :] = total.astype(out.dtype)
 
 
@@ -328,15 +417,14 @@
     rows, width = last[0].shape
     shape = (PAIR * rows // SIDE, width)
     outs = [jax.ShapeDtypeStruct(shape, F32)] + [jax.ShapeDtypeStruct(shape, BF16)] * (SIDE - 1)
-    done = pl.pallas_call(
+    return pl.pallas_call(
         turn_kernel,
-        out_shape=outs * 2,
+        out_shape=outs,
         in_specs=[VMEM] * len(ins),
-        out_specs=[VMEM] * (2 * SIDE),
+        out_specs=[VMEM] * SIDE,
         compiler_params=params(32),
         name="turn_sums",
     )(*ins)
-    return done[:SIDE], done[SIDE:]
 
 
 def dense_kernel(*refs):
@@ -363,6 +451,20 @@
     )(*terms, weight, bias.reshape(1, -1))
 
 
+def over(array, axis, bit):
+    pairs = [(c, c ^ bit) for c in range(lax.axis_size(axis))]
+    return lax.ppermute(array, axis, pairs)
+
+
+def gather_first(own):
+    half = own.shape[0] // 2
+    one, three = over(own, "y", 1), over(own, "y", 3)
+    other = over(own, "core", 1)
+    far = [over(one[:half], "y", 3), over(three[half:], "y", 1)]
+    near = [over(piece, "core", 1) for piece in (one, three)]
+    return [own, other, one, three, *near], far
+
+
 def swap(arrays, axis, first):
     return [
         lax.ppermute(array, axis, [(c, c ^ bit) for c in range(SIDE)])
@@ -370,14 +472,13 @@
     ]
 
 
-def spread(sides):
-    got = [list(side) for side in sides]
-    for bit in (1, 2, 3):
-        for side, axis in enumerate(("z", "x")):
-            got[side][bit] = lax.ppermute(
-                sides[side][bit], axis, [(c, c ^ bit) for c in range(SIDE)]
-            )
-    return got[0] + got[1]
+def spread(sums, axis):
+    mine, *send = sums
+    got = [
+        lax.ppermute(array, axis, [(c, c ^ bit) for c in range(SIDE)])
+        for bit, array in enumerate(send, 1)
+    ]
+    return [mine, *got]
 
 
 def body(features, new_index, tile_values, tile_index, tile_count, weight, bias):
@@ -390,27 +491,34 @@
     row_tiles = local_rows * grid_cols // tiles.shape[1]
     assert row_tiles == 256 and grid_cols == SIDE * SIDE
 
-    codes = tile_codes(tile_index[0, 0], lax.axis_index("x"), lax.axis_index("z"))
+    codes = tile_codes(
+        tile_index[0, 0], *(lax.axis_index(axis) for axis in ("x", "z", "y", "core"))
+    )
     packed = pack_rows(new_index, features, grid_rows, grid_cols, capacity)
     got = lax.all_to_all(packed, everyone, split_axis=0, concat_axis=0, tiled=True)
     table = plan_tiles(tile_count.reshape(1), codes)
     got, table = lax.optimization_barrier((got, table))
     moved_rows = place_rows(got, local_rows)
-    x = lax.all_gather(moved_rows, ("y", "core"), axis=0, tiled=True)
+    early, far = gather_first(moved_rows)
 
     rows = local_rows * grid_cols // 16
     axes = ("x", "z")
     pairs = (slice(0, PAIR), slice(PAIR, STREAMS))
-    sent_on = tile_products(0, STREAMS, table, x, tiles, rows)
+    x_rows = local_rows * grid_rows
+    x, totals = early_products(0, STREAMS, table, early, x_rows, tiles, rows)
+    far, x, totals = lax.optimization_barrier((far, x, totals))
+    late = [*far, *(over(piece, "core", 1) for piece in far)]
+    x, _, *sent_on = late_products(3, STREAMS, table, late, x, totals, tiles, rows)
     got_on = [swap(sent_on[pair], axis, True) for pair, axis in zip(pairs, axes)]
     both = tile_products(1, 2 * STREAMS, table, x, tiles, rows)
     got_own = [swap(both[pair], axis, True) for pair, axis in zip(pairs, axes)]
     hand = forward_sums(both[STREAMS:], got_on[0] + got_on[1])
     got_last = [swap(hand[pair], axis, False) for pair, axis in zip(pairs, axes)]
-    hand, table = lax.optimization_barrier((hand, table))
+    hand, table, got_own = lax.optimization_barrier((hand, table, got_own))
     kept = tile_products(2, STREAMS, table, x, tiles, rows)
-    sides = turn_sums(kept, got_own[0] + got_own[1], got_last[0] + got_last[1])
-    return dense(spread(sides), weight, bias)
+    first = spread(turn_sums(kept[pairs[0]], got_own[0], got_last[0]), "z")
+    second = spread(turn_sums(kept[pairs[1]], got_own[1], got_last[1]), "x")
+    return dense(first + second, weight, bias)
 
 
 def solution(mesh):

time: 165 us -> 138 us (0.84)
  Pallas kernels: 44.3 us -> 29.7 us
  between operations: 14.2 us -> 0.82 us
  starting transfers between devices: 35.1 us -> 45.6 us
  waiting for transfers between devices: 65.2 us -> 59.2 us
  local copies, waits for them, and re-layouts: 2.91 us -> 0.78 us
    all_gather x1 -> x0, waiting for transfers between devices: 29.5 us -> none  [body(): x = lax.all_gather(moved_rows, ('y', 'core'), axis=0, tiled=True)]
    ppermute x6 -> x15, waiting for transfers between devices: 8.74 us -> 26.3 us  [the longest x9 19.1 us: over(): return lax.ppermute(array, axis, pairs)]
    pallas_call x3 -> x2, Pallas kernels: 21.1 us -> 6.37 us  [tile_products(): pl.pallas_call(functools.partial(tile_kernel, group, arrays), out_shape=[...]
    ppermute x6 -> x15, starting transfers between devices: 10.8 us -> 17.7 us  [the longest x6 12.5 us: spread(): lax.ppermute(array, axis, [(c, c ^ bit) for c in range(SIDE)])]
    all_to_all x1, waiting for transfers between devices: 12.1 us -> 16.2 us  [body(): lax.all_to_all(packed, everyone, split_axis=0, concat_axis=0, tiled=True)]
    ppermute x12, starting transfers between devices: 13.2 us -> 16.8 us  [swap(): lax.ppermute(array, axis, [(c, c ^ bit) for c in range(SIDE)])]
    unnamed x12 -> x8, local copies, waits for them, and re-layouts: 2.91 us -> 0.75 us
    ppermute x12, waiting for transfers between devices: 14.8 us -> 16.7 us  [swap(): lax.ppermute(array, axis, [(c, c ^ bit) for c in range(SIDE)])]
  transfers between devices with their start and end apart: 20 -> 28, of which waited for: 10 -> 15; matrix products, arithmetic and copies ran while one was open for 0% -> 1% of each run, Pallas kernels for 14% -> 9%
where the time goes in v5:
time: 138 us; the launch traced here: 137 us
  waiting for transfers between devices  59.2 us (43%)
  starting transfers between devices  45.6 us (33%)
  Pallas kernels  29.7 us (22%)
    ppermute x9, waiting for transfers between devices, over(): return lax.ppermute(array, axis, pairs)  19.1 us
    ppermute x12, starting transfers between devices, swap(): lax.ppermute(array, axis, [(c, c ^ bit) for c in range(SIDE)])  16.8 us
    ppermute x12, waiting for transfers between devices, swap(): lax.ppermute(array, axis, [(c, c ^ bit) for c in range(SIDE)])  16.7 us
    all_to_all x1, waiting for transfers between devices, body(): lax.all_to_all(packed, everyone, split_axis=0, concat_axis=0, tiled=True)  16.2 us
    ppermute x6, starting transfers between devices, spread(): lax.ppermute(array, axis, [(c, c ^ bit) for c in range(SIDE)])  12.5 us
    all_to_all x1, starting transfers between devices, body(): lax.all_to_all(packed, everyone, split_axis=0, concat_axis=0, tiled=True)  11.2 us
    pallas_call x1, Pallas kernels, pack_rows(): pl.pallas_call(functools.partial(pack_kernel, grid_rows, grid_cols, capac...  7.91 us
    ppermute x6, waiting for transfers between devices, spread(): lax.ppermute(array, axis, [(c, c ^ bit) for c in range(SIDE)])  7.16 us
  transfers between devices with their start and end apart: 28, of which 15 were waited for; matrix products, arithmetic and copies ran while one was open for 1% of the time, Pallas kernels for 9%

profile of v5, /device:TPU:0, one launch (start us, length us, event | category | flops | bytes accessed | tf_op | source)
XLA Modules:
  0.0 136.8 jit_solution(11224358342660731911)
XLA Ops:
  0.0 7.9 %pack_rows.1 = bf16[128,40,128]{2,1,0:T(8,128)(2,1)} custom-call(s32[16,128]{1,0:T(8,128)} %bitcast.10, bf16[2048,128]{1,0:T(8,128)(2,1)} %rows_hbm.1), custom_call_target="tpu_custom_call" | custom-call | tf_op jit(solution)/shard_map/pack_rows/pallas_call | solution.py:112
  7.9 11.2 %all-to-all-start = ((bf16[128,40,128]{2,1,0:T(8,128)(2,1)}), bf16[128,40,128]{2,1,0:T(8,128)(2,1)S(1)}, u32[]{:S(2)}, u32[]{:S(2)}) async-start(bf16[128,40,128]{2,1,0:T(8,128)(2,1)} %pack_rows.1), calls=%async_computation | async-start | bytes 2621440 | tf_op jit(solution)/shard_map/all_to_all | solution.py:498
  19.9 0.6 or_or_fusion.code_ref
  20.5 2.7 %plan_tiles.1.table_ref = s32[5,656]{1,0:T(8,128)} custom-call(s32[1]{0:T(128)} %bitcast.4.count_ref, s32[640]{0:T(1024)} %or_or_fusion.code_ref), custom_call_target="tpu_custom_call" | custom-call | tf_op jit(solution)/shard_map/plan_tiles/pallas_call | solution.py:221
  23.1 16.2 %all-to-all-done.in_ref = bf16[128,40,128]{2,1,0:T(8,128)(2,1)S(1)} async-done(((bf16[128,40,128]{2,1,0:T(8,128)(2,1)}), bf16[128,40,128]{2,1,0:T(8,128)(2,1)S(1)}, u32[]{:S(2)}, u32[]{:S(2)}) %all-to-all-start) | async-done | bytes 1310752 | tf_op jit(solution)/shard_map/all_to_all | solution.py:498
  39.4 4.9 %place_rows.1.refs_0_ = bf16[2048,128]{1,0:T(8,128)(2,1)S(1)} custom-call(bf16[128,40,128]{2,1,0:T(8,128)(2,1)S(1)} %all-to-all-done.in_ref), custom_call_target="tpu_custom_call" | custom-call | tf_op jit(solution)/shard_map/place_rows/pallas_call | solution.py:156
  44.3 2.2 %collective-permute-start.2 = (bf16[2048,128]{1,0:T(8,128)(2,1)S(1)}, bf16[2048,128]{1,0:T(8,128)(2,1)S(1)}, u32[]{:S(2)}, u32[]{:S(2)}) collective-permute-start(bf16[2048,128]{1,0:T(8,128)(2,1)S(1)} %place_rows.1.refs_0_), channel_id=1, source_target_pairs={{0,96},{32,64},{64,32},{96,0},{1,97},{33,65},{65,33},{97,1},{2,98}... | collective-permute-start | bytes 1572872 | tf_op jit(solution)/shard_map/ppermute | solution.py:456
  46.5 0.2 collective-permute-start
  46.8 12.2 %collective-permute-done.2.refs_3_ = bf16[2048,128]{1,0:T(8,128)(2,1)S(1)} collective-permute-done((bf16[2048,128]{1,0:T(8,128)(2,1)S(1)}, bf16[2048,128]{1,0:T(8,128)(2,1)S(1)}, u32[]{:S(2)}, u32[]{:S(2)}) %collective-permute-start.2) | collective-permute-done | bytes 524320 | tf_op jit(solution)/shard_map/ppermute | solution.py:456
  59.0 0.6 collective-permute-done.refs_2_
  59.6 0.4 collective-permute-start.3
  60.0 1.8 %collective-permute-start.1 = (bf16[1024,128]{1,0:T(8,128)(2,1)S(1)}, bf16[1024,128]{1,0:T(8,128)(2,1)S(1)}, u32[]{:S(2)}, u32[]{:S(2)}) collective-permute-start(bf16[1024,128]{1,0:T(8,128)(2,1)S(1)} %slice.18), channel_id=1, source_target_pairs={{0,96},{32,64},{64,32},{96,0},{1,97},{33,65},{65,33},{97,1},{2,98}... | collective-permute-start | bytes 786440 | tf_op jit(solution)/shard_map/ppermute | solution.py:456
  61.9 0.7 copy-done
  62.6 2.3 %early_products.1 = (bf16[16384,128]{1,0:T(8,128)(2,1)S(1)}, f32[8320,128]{1,0:T(8,128)S(1)}) custom-call(s32[5,656]{1,0:T(8,128)S(1)} %copy-done, bf16[2048,128]{1,0:T(8,128)(2,1)S(1)} %place_rows.1.refs_0_, bf16[2048,128]{1,0:T(8,128)(2,1)S(1)} %collective-permute-done.4.refs_1_, bf16[2048,128]{1,0:T(8,128)(2,1)S(1)} %collective-permute-done.refs_2_, ...), custom_call_target="tpu_custom_call" | custom-call | flops 5000000000 | bytes 5000000 | tf_op jit(solution)/shard_map/early_products/pallas_call | solution.py:345
  64.9 3.5 %collective-permute-done.3.refs_1_ = bf16[1024,128]{1,0:T(8,128)(2,1)S(1)} collective-permute-done((bf16[1024,128]{1,0:T(8,128)(2,1)S(1)}, bf16[1024,128]{1,0:T(8,128)(2,1)S(1)}, u32[]{:S(2)}, u32[]{:S(2)}) %collective-permute-start.3) | collective-permute-done | bytes 262176 | tf_op jit(solution)/shard_map/ppermute | solution.py:456
  68.4 1.3 collective-permute-done.1.refs_0_
  69.8 0.5 collective-permute-start.8
  70.3 1.0 collective-permute-done.7.refs_2_
  71.3 0.4 collective-permute-done.8.refs_3_
  71.7 2.8 %late_products.1 = (bf16[16384,128]{1,0:T(8,128)(2,1)S(1)}, f32[8320,128]{1,0:T(8,128)S(1)}, bf16[2048,128]{1,0:T(8,128)(2,1)S(1)}, bf16[2048,128]{1,0:T(8,128)(...) custom-call(s32[5,656]{1,0:T(8,128)S(1)} %copy-done, ...), custom_call_target="tpu_custom_call", output_to_operand_aliasing={{0}: (6, {}), {1}: (7, {})} | custom-call | flops 5000000000 | bytes 5000000 | tf_op jit(solution)/shard_map/late_products/pallas_call | solution.py:363
  74.5 0.8 collective-permute-start.9
  75.3 2.2 %collective-permute-start.10 = (bf16[2048,128]{1,0:T(8,128)(2,1)S(1)}, bf16[2048,128]{1,0:T(8,128)(2,1)S(1)}, u32[]{:S(2)}, u32[]{:S(2)}) collective-permute-start(bf16[2048,128]{1,0:T(8,128)(2,1)S(1)} %get-tuple-element.59), channel_id=1, source_target_pairs={{0,12},{4,8},{8,4},{12,0},{1,13},{5,9},{9,5},{13,1},{2,14},{6,10},... | collective-permute-start | bytes 1572872 | tf_op jit(solution)/shard_map/ppermute | solution.py:470
  77.4 1.3 collective-permute-start.11
  78.9 3.5 %tile_products.2 = (bf16[2048,128]{1,0:T(8,128)(2,1)S(1)}, bf16[2048,128]{1,0:T(8,128)(2,1)S(1)}, bf16[2048,128]{1,0:T(8,128)(2,1)S(1)}, bf16[2048,128]{1,0:T(8,...) custom-call(s32[5,656]{1,0:T(8,128)S(1)} %copy-done, ...), custom_call_target="tpu_custom_call" | custom-call | flops 40000000000 | bytes 40000000 | tf_op jit(solution)/shard_map/tile_products/pallas_call | solution.py:331
  82.4 0.7 collective-permute-start.13
  83.2 5.7 %collective-permute-done.9.refs_1_ = bf16[2048,128]{1,0:T(8,128)(2,1)S(1)} collective-permute-done((bf16[2048,128]{1,0:T(8,128)(2,1)S(1)}, bf16[2048,128]{1,0:T(8,128)(2,1)S(1)}, u32[]{:S(2)}, u32[]{:S(2)}) %collective-permute-start.9) | collective-permute-done | bytes 524320 | tf_op jit(solution)/shard_map/ppermute | solution.py:470
  88.9 2.2 %collective-permute-start.14 = (bf16[2048,128]{1,0:T(8,128)(2,1)S(1)}, bf16[2048,128]{1,0:T(8,128)(2,1)S(1)}, u32[]{:S(2)}, u32[]{:S(2)}) collective-permute-start(bf16[2048,128]{1,0:T(8,128)(2,1)S(1)} %get-tuple-element.69), channel_id=1, source_target_pairs={{0,12},{4,8},{8,4},{12,0},{1,13},{5,9},{9,5},{13,1},{2,14},{6,10},... | collective-permute-start | bytes 1572872 | tf_op jit(solution)/shard_map/ppermute | solution.py:470
  91.1 2.0 %collective-permute-start.15 = (bf16[2048,128]{1,0:T(8,128)(2,1)S(1)}, bf16[2048,128]{1,0:T(8,128)(2,1)S(1)}, u32[]{:S(2)}, u32[]{:S(2)}) collective-permute-start(bf16[2048,128]{1,0:T(8,128)(2,1)S(1)} %get-tuple-element.70), channel_id=1, source_target_pairs={{0,1},{1,0},{2,3},{3,2},{4,5},{5,4},{6,7},{7,6},{8,9},{9,8},{10,11... | collective-permute-start | bytes 1572872 | tf_op jit(solution)/shard_map/ppermute | solution.py:470
  93.1 0.5 forward_sums.1
  93.6 2.7 %collective-permute-start.17 = (bf16[2048,128]{1,0:T(8,128)(2,1)S(1)}, bf16[2048,128]{1,0:T(8,128)(2,1)S(1)}, u32[]{:S(2)}, u32[]{:S(2)}) collective-permute-start(bf16[2048,128]{1,0:T(8,128)(2,1)S(1)} %get-tuple-element.64), channel_id=1, source_target_pairs={{0,12},{4,8},{8,4},{12,0},{1,13},{5,9},{9,5},{13,1},{2,14},{6,10},... | collective-permute-start | bytes 1572872 | tf_op jit(solution)/shard_map/ppermute | solution.py:470
  96.3 1.8 %collective-permute-done.13.refs_1_ = bf16[2048,128]{1,0:T(8,128)(2,1)S(1)} collective-permute-done((bf16[2048,128]{1,0:T(8,128)(2,1)S(1)}, bf16[2048,128]{1,0:T(8,128)(2,1)S(1)}, u32[]{:S(2)}, u32[]{:S(2)}) %collective-permute-start.13) | collective-permute-done | bytes 524320 | tf_op jit(solution)/shard_map/ppermute | solution.py:470
  98.2 1.1 collective-permute-start.18
  99.3 5.6 %collective-permute-done.14.refs_4_ = bf16[2048,128]{1,0:T(8,128)(2,1)S(1)} collective-permute-done((bf16[2048,128]{1,0:T(8,128)(2,1)S(1)}, bf16[2048,128]{1,0:T(8,128)(2,1)S(1)}, u32[]{:S(2)}, u32[]{:S(2)}) %collective-permute-start.14) | collective-permute-done | bytes 524320 | tf_op jit(solution)/shard_map/ppermute | solution.py:470
  104.9 3.5 %collective-permute-start.22 = (bf16[2048,128]{1,0:T(8,128)(2,1)S(1)}, bf16[2048,128]{1,0:T(8,128)(2,1)S(1)}, u32[]{:S(2)}, u32[]{:S(2)}) collective-permute-start(bf16[2048,128]{1,0:T(8,128)(2,1)S(1)} %get-tuple-element.66), channel_id=1, source_target_pairs={{0,3},{1,2},{2,1},{3,0},{4,7},{5,6},{6,5},{7,4},{8,11},{9,10},{10,... | collective-permute-start | bytes 1572872 | tf_op jit(solution)/shard_map/ppermute | solution.py:470
  108.5 2.8 %tile_products.3 = (bf16[2048,128]{1,0:T(8,128)(2,1)S(1)}, bf16[2048,128]{1,0:T(8,128)(2,1)S(1)}, bf16[2048,128]{1,0:T(8,128)(2,1)S(1)}, bf16[2048,128]{1,0:T(8,128)(2,1)S(1)}) custom-call(s32[5,656]{1,0:T(8,128)S(1)} %copy-done, bf16[16384,128]{1,0:T(8,128)(2,1)S(1)} %get-tuple-element.55.x_ref, bf16[640,128,128]{2,1,0:T(8,128)(2,1)} %bitcast.9), custom_call_target="tpu_custom_call" | custom-call | flops 20000000000 | bytes 20000000 | tf_op jit(solution)/shard_map/tile_products/pallas_call | solution.py:331
  111.3 3.5 %collective-permute-done.17.refs_2_ = bf16[2048,128]{1,0:T(8,128)(2,1)S(1)} collective-permute-done((bf16[2048,128]{1,0:T(8,128)(2,1)S(1)}, bf16[2048,128]{1,0:T(8,128)(2,1)S(1)}, u32[]{:S(2)}, u32[]{:S(2)}) %collective-permute-start.17) | collective-permute-done | bytes 524320 | tf_op jit(solution)/shard_map/ppermute | solution.py:470
  114.9 0.4 turn_sums.2
  115.3 1.6 %collective-permute-start.19 = (bf16[1024,128]{1,0:T(8,128)(2,1)S(1)}, bf16[1024,128]{1,0:T(8,128)(2,1)S(1)}, u32[]{:S(2)}, u32[]{:S(2)}) collective-permute-start(bf16[1024,128]{1,0:T(8,128)(2,1)S(1)} %get-tuple-element.78), channel_id=1, source_target_pairs={{0,1},{1,0},{2,3},{3,2},{4,5},{5,4},{6,7},{7,6},{8,9},{9,8},{10,11... | collective-permute-start | bytes 786440 | tf_op jit(solution)/shard_map/ppermute | solution.py:478
  116.8 2.7 %collective-permute-start.20 = (bf16[1024,128]{1,0:T(8,128)(2,1)S(1)}, bf16[1024,128]{1,0:T(8,128)(2,1)S(1)}, u32[]{:S(2)}, u32[]{:S(2)}) collective-permute-start(bf16[1024,128]{1,0:T(8,128)(2,1)S(1)} %get-tuple-element.79), channel_id=1, source_target_pairs={{0,2},{1,3},{2,0},{3,1},{4,6},{5,7},{6,4},{7,5},{8,10},{9,11},{10,... | collective-permute-start | bytes 786440 | tf_op jit(solution)/shard_map/ppermute | solution.py:478
  119.5 0.6 collective-permute-start.21
  120.1 0.4 turn_sums.3
  120.6 4.2 %collective-permute-start.25 = (bf16[1024,128]{1,0:T(8,128)(2,1)S(1)}, bf16[1024,128]{1,0:T(8,128)(2,1)S(1)}, u32[]{:S(2)}, u32[]{:S(2)}) collective-permute-start(bf16[1024,128]{1,0:T(8,128)(2,1)S(1)} %get-tuple-element.87), channel_id=1, source_target_pairs={{0,8},{4,12},{8,0},{12,4},{1,9},{5,13},{9,1},{13,5},{2,10},{6,14},... | collective-permute-start | bytes 786440 | tf_op jit(solution)/shard_map/ppermute | solution.py:478
  124.8 3.4 %collective-permute-start.26 = (bf16[1024,128]{1,0:T(8,128)(2,1)S(1)}, bf16[1024,128]{1,0:T(8,128)(2,1)S(1)}, u32[]{:S(2)}, u32[]{:S(2)}) collective-permute-start(bf16[1024,128]{1,0:T(8,128)(2,1)S(1)} %get-tuple-element.88), channel_id=1, source_target_pairs={{0,12},{4,8},{8,4},{12,0},{1,13},{5,9},{9,5},{13,1},{2,14},{6,10},... | collective-permute-start | bytes 786440 | tf_op jit(solution)/shard_map/ppermute | solution.py:478
  128.2 1.9 %collective-permute-done.20.refs_2_ = bf16[1024,128]{1,0:T(8,128)(2,1)S(1)} collective-permute-done((bf16[1024,128]{1,0:T(8,128)(2,1)S(1)}, bf16[1024,128]{1,0:T(8,128)(2,1)S(1)}, u32[]{:S(2)}, u32[]{:S(2)}) %collective-permute-start.20) | collective-permute-done | bytes 262176 | tf_op jit(solution)/shard_map/ppermute | solution.py:478
  130.1 1.9 %collective-permute-done.21.refs_3_ = bf16[1024,128]{1,0:T(8,128)(2,1)S(1)} collective-permute-done((bf16[1024,128]{1,0:T(8,128)(2,1)S(1)}, bf16[1024,128]{1,0:T(8,128)(2,1)S(1)}, u32[]{:S(2)}, u32[]{:S(2)}) %collective-permute-start.21) | collective-permute-done | bytes 262176 | tf_op jit(solution)/shard_map/ppermute | solution.py:478
  132.0 0.7 collective-permute-done.25.refs_6_
  132.6 2.7 %collective-permute-done.26.refs_7_ = bf16[1024,128]{1,0:T(8,128)(2,1)S(1)} collective-permute-done((bf16[1024,128]{1,0:T(8,128)(2,1)S(1)}, bf16[1024,128]{1,0:T(8,128)(2,1)S(1)}, u32[]{:S(2)}, u32[]{:S(2)}) %collective-permute-start.26) | collective-permute-done | bytes 262176 | tf_op jit(solution)/shard_map/ppermute | solution.py:478
  135.4 1.5 %dense.1 = bf16[2048,256]{1,0:T(8,128)(2,1)} custom-call(f32[1024,128]{1,0:T(8,128)S(1)} %get-tuple-element.77.refs_0_, bf16[1024,128]{1,0:T(8,128)(2,1)S(1)} %collective-permute-done.19.refs_1_, bf16[1024,128]{1,0:T(8,128)(2,1)S(1)} %collective-permute-done.20.refs_2_, bf16[1024,128]{1,0:T(8,128)(2,1)S(1)} %collective-permute-done.21.refs_3_, ...), custom_call_target="tpu_custom_call" | custom-call | tf_op jit(solution)/shard_map/dense/pallas_call | solution.py:444
  (32 shorter events, 0.6 us)
Async XLA Ops:
  0.0 19.7 %copy-start.3 = (s32[1,1,2,640]{3,2,1,0:T(2,128)S(1)}, s32[1,1,2,640]{3,2,1,0:T(2,128)}, u32[]{:S(2)}) copy-start(s32[1,1,2,640]{3,2,1,0:T(2,128)} %param.10) | copy-start | bytes 15364
  7.9 31.5 %all-to-all-start = ((bf16[128,40,128]{2,1,0:T(8,128)(2,1)}), bf16[128,40,128]{2,1,0:T(8,128)(2,1)S(1)}, u32[]{:S(2)}, u32[]{:S(2)}) async-start(bf16[128,40,128]{2,1,0:T(8,128)(2,1)} %pack_rows.1), calls=%async_computation | async-start | bytes 2621440 | tf_op jit(solution)/shard_map/all_to_all | solution.py:498
  44.3 14.6 %collective-permute-start.2 = (bf16[2048,128]{1,0:T(8,128)(2,1)S(1)}, bf16[2048,128]{1,0:T(8,128)(2,1)S(1)}, u32[]{:S(2)}, u32[]{:S(2)}) collective-permute-start(bf16[2048,128]{1,0:T(8,128)(2,1)S(1)} %place_rows.1.refs_0_), channel_id=1, source_target_pairs={{0,96},{32,64},{64,32},{96,0},{1,97},{33,65},{65,33},{97,1},{2,98}... | collective-permute-start | bytes 1572872 | tf_op jit(solution)/shard_map/ppermute | solution.py:456
  46.5 13.1 %collective-permute-start = (bf16[2048,128]{1,0:T(8,128)(2,1)S(1)}, bf16[2048,128]{1,0:T(8,128)(2,1)S(1)}, u32[]{:S(2)}, u32[]{:S(2)}) collective-permute-start(bf16[2048,128]{1,0:T(8,128)(2,1)S(1)} %place_rows.1.refs_0_), channel_id=1, source_target_pairs={{0,32},{32,0},{64,96},{96,64},{1,33},{33,1},{65,97},{97,65},{2,34}... | collective-permute-start | bytes 1572872 | tf_op jit(solution)/shard_map/ppermute | solution.py:456
  46.8 15.1 %collective-permute-start.4 = (bf16[2048,128]{1,0:T(8,128)(2,1)S(1)}, bf16[2048,128]{1,0:T(8,128)(2,1)S(1)}, u32[]{:S(2)}, u32[]{:S(2)}) collective-permute-start(bf16[2048,128]{1,0:T(8,128)(2,1)S(1)} %place_rows.1.refs_0_), channel_id=1, source_target_pairs={{0,16},{16,0},{1,17},{17,1},{2,18},{18,2},{3,19},{19,3},{4,20},{20... | collective-permute-start | bytes 1572872 | tf_op jit(solution)/shard_map/ppermute | solution.py:456
  59.0 2.9 %collective-permute-start.6 = (bf16[2048,128]{1,0:T(8,128)(2,1)S(1)}, bf16[2048,128]{1,0:T(8,128)(2,1)S(1)}, u32[]{:S(2)}, u32[]{:S(2)}) collective-permute-start(bf16[2048,128]{1,0:T(8,128)(2,1)S(1)} %collective-permute-done.2.refs_3_), channel_id=1, source_target_pairs={{0,16},{16,0},{1,17},{17,1},{2,18},{18,2},{3,19},{19,3},{4,20},{20... | collective-permute-start | bytes 1572872 | tf_op jit(solution)/shard_map/ppermute | solution.py:456
  59.6 2.2 %collective-permute-start.5 = (bf16[2048,128]{1,0:T(8,128)(2,1)S(1)}, bf16[2048,128]{1,0:T(8,128)(2,1)S(1)}, u32[]{:S(2)}, u32[]{:S(2)}) collective-permute-start(bf16[2048,128]{1,0:T(8,128)(2,1)S(1)} %collective-permute-done.refs_2_), channel_id=1, source_target_pairs={{0,16},{16,0},{1,17},{17,1},{2,18},{18,2},{3,19},{19,3},{4,20},{20... | collective-permute-start | bytes 1572872 | tf_op jit(solution)/shard_map/ppermute | solution.py:456
  59.6 8.8 %collective-permute-start.3 = (bf16[1024,128]{1,0:T(8,128)(2,1)S(1)}, bf16[1024,128]{1,0:T(8,128)(2,1)S(1)}, u32[]{:S(2)}, u32[]{:S(2)}) collective-permute-start(bf16[1024,128]{1,0:T(8,128)(2,1)S(1)} %slice.19), channel_id=1, source_target_pairs={{0,32},{32,0},{64,96},{96,64},{1,33},{33,1},{65,97},{97,65},{2,34}... | collective-permute-start | bytes 786440 | tf_op jit(solution)/shard_map/ppermute | solution.py:456
  60.0 9.7 %collective-permute-start.1 = (bf16[1024,128]{1,0:T(8,128)(2,1)S(1)}, bf16[1024,128]{1,0:T(8,128)(2,1)S(1)}, u32[]{:S(2)}, u32[]{:S(2)}) collective-permute-start(bf16[1024,128]{1,0:T(8,128)(2,1)S(1)} %slice.18), channel_id=1, source_target_pairs={{0,96},{32,64},{64,32},{96,0},{1,97},{33,65},{65,33},{97,1},{2,98}... | collective-permute-start | bytes 786440 | tf_op jit(solution)/shard_map/ppermute | solution.py:456
  61.8 0.7 copy-start
  69.8 1.5 %collective-permute-start.7 = (bf16[1024,128]{1,0:T(8,128)(2,1)S(1)}, bf16[1024,128]{1,0:T(8,128)(2,1)S(1)}, u32[]{:S(2)}, u32[]{:S(2)}) collective-permute-start(bf16[1024,128]{1,0:T(8,128)(2,1)S(1)} %collective-permute-done.1.refs_0_), channel_id=1, source_target_pairs={{0,16},{16,0},{1,17},{17,1},{2,18},{18,2},{3,19},{19,3},{4,20},{20... | collective-permute-start | bytes 786440 | tf_op jit(solution)/shard_map/ppermute | solution.py:456
  69.8 1.9 %collective-permute-start.8 = (bf16[1024,128]{1,0:T(8,128)(2,1)S(1)}, bf16[1024,128]{1,0:T(8,128)(2,1)S(1)}, u32[]{:S(2)}, u32[]{:S(2)}) collective-permute-start(bf16[1024,128]{1,0:T(8,128)(2,1)S(1)} %collective-permute-done.3.refs_1_), channel_id=1, source_target_pairs={{0,16},{16,0},{1,17},{17,1},{2,18},{18,2},{3,19},{19,3},{4,20},{20... | collective-permute-start | bytes 786440 | tf_op jit(solution)/shard_map/ppermute | solution.py:456
  74.5 14.4 %collective-permute-start.9 = (bf16[2048,128]{1,0:T(8,128)(2,1)S(1)}, bf16[2048,128]{1,0:T(8,128)(2,1)S(1)}, u32[]{:S(2)}, u32[]{:S(2)}) collective-permute-start(bf16[2048,128]{1,0:T(8,128)(2,1)S(1)} %get-tuple-element.57), channel_id=1, source_target_pairs={{0,4},{4,0},{8,12},{12,8},{1,5},{5,1},{9,13},{13,9},{2,6},{6,2},{1... | collective-permute-start | bytes 1572872 | tf_op jit(solution)/shard_map/ppermute | solution.py:470
  75.3 15.8 %collective-permute-start.10 = (bf16[2048,128]{1,0:T(8,128)(2,1)S(1)}, bf16[2048,128]{1,0:T(8,128)(2,1)S(1)}, u32[]{:S(2)}, u32[]{:S(2)}) collective-permute-start(bf16[2048,128]{1,0:T(8,128)(2,1)S(1)} %get-tuple-element.59), channel_id=1, source_target_pairs={{0,12},{4,8},{8,4},{12,0},{1,13},{5,9},{9,5},{13,1},{2,14},{6,10},... | collective-permute-start | bytes 1572872 | tf_op jit(solution)/shard_map/ppermute | solution.py:470
  77.4 15.7 %collective-permute-start.11 = (bf16[2048,128]{1,0:T(8,128)(2,1)S(1)}, bf16[2048,128]{1,0:T(8,128)(2,1)S(1)}, u32[]{:S(2)}, u32[]{:S(2)}) collective-permute-start(bf16[2048,128]{1,0:T(8,128)(2,1)S(1)} %get-tuple-element.61), channel_id=1, source_target_pairs={{0,1},{1,0},{2,3},{3,2},{4,5},{5,4},{6,7},{7,6},{8,9},{9,8},{10,11... | collective-permute-start | bytes 1572872 | tf_op jit(solution)/shard_map/ppermute | solution.py:470
  78.7 14.4 %collective-permute-start.12 = (bf16[2048,128]{1,0:T(8,128)(2,1)S(1)}, bf16[2048,128]{1,0:T(8,128)(2,1)S(1)}, u32[]{:S(2)}, u32[]{:S(2)}) collective-permute-start(bf16[2048,128]{1,0:T(8,128)(2,1)S(1)} %get-tuple-element.63), channel_id=1, source_target_pairs={{0,3},{1,2},{2,1},{3,0},{4,7},{5,6},{6,5},{7,4},{8,11},{9,10},{10,... | collective-permute-start | bytes 1572872 | tf_op jit(solution)/shard_map/ppermute | solution.py:470
  82.4 15.7 %collective-permute-start.13 = (bf16[2048,128]{1,0:T(8,128)(2,1)S(1)}, bf16[2048,128]{1,0:T(8,128)(2,1)S(1)}, u32[]{:S(2)}, u32[]{:S(2)}) collective-permute-start(bf16[2048,128]{1,0:T(8,128)(2,1)S(1)} %get-tuple-element.68), channel_id=1, source_target_pairs={{0,4},{4,0},{8,12},{12,8},{1,5},{5,1},{9,13},{13,9},{2,6},{6,2},{1... | collective-permute-start | bytes 1572872 | tf_op jit(solution)/shard_map/ppermute | solution.py:470
  88.9 16.0 %collective-permute-start.14 = (bf16[2048,128]{1,0:T(8,128)(2,1)S(1)}, bf16[2048,128]{1,0:T(8,128)(2,1)S(1)}, u32[]{:S(2)}, u32[]{:S(2)}) collective-permute-start(bf16[2048,128]{1,0:T(8,128)(2,1)S(1)} %get-tuple-element.69), channel_id=1, source_target_pairs={{0,12},{4,8},{8,4},{12,0},{1,13},{5,9},{9,5},{13,1},{2,14},{6,10},... | collective-permute-start | bytes 1572872 | tf_op jit(solution)/shard_map/ppermute | solution.py:470
  91.1 17.4 %collective-permute-start.15 = (bf16[2048,128]{1,0:T(8,128)(2,1)S(1)}, bf16[2048,128]{1,0:T(8,128)(2,1)S(1)}, u32[]{:S(2)}, u32[]{:S(2)}) collective-permute-start(bf16[2048,128]{1,0:T(8,128)(2,1)S(1)} %get-tuple-element.70), channel_id=1, source_target_pairs={{0,1},{1,0},{2,3},{3,2},{4,5},{5,4},{6,7},{7,6},{8,9},{9,8},{10,11... | collective-permute-start | bytes 1572872 | tf_op jit(solution)/shard_map/ppermute | solution.py:470
  93.1 15.4 %collective-permute-start.16 = (bf16[2048,128]{1,0:T(8,128)(2,1)S(1)}, bf16[2048,128]{1,0:T(8,128)(2,1)S(1)}, u32[]{:S(2)}, u32[]{:S(2)}) collective-permute-start(bf16[2048,128]{1,0:T(8,128)(2,1)S(1)} %get-tuple-element.71), channel_id=1, source_target_pairs={{0,3},{1,2},{2,1},{3,0},{4,7},{5,6},{6,5},{7,4},{8,11},{9,10},{10,... | collective-permute-start | bytes 1572872 | tf_op jit(solution)/shard_map/ppermute | solution.py:470
  93.6 21.3 %collective-permute-start.17 = (bf16[2048,128]{1,0:T(8,128)(2,1)S(1)}, bf16[2048,128]{1,0:T(8,128)(2,1)S(1)}, u32[]{:S(2)}, u32[]{:S(2)}) collective-permute-start(bf16[2048,128]{1,0:T(8,128)(2,1)S(1)} %get-tuple-element.64), channel_id=1, source_target_pairs={{0,12},{4,8},{8,4},{12,0},{1,13},{5,9},{9,5},{13,1},{2,14},{6,10},... | collective-permute-start | bytes 1572872 | tf_op jit(solution)/shard_map/ppermute | solution.py:470
  98.2 16.7 %collective-permute-start.18 = (bf16[2048,128]{1,0:T(8,128)(2,1)S(1)}, bf16[2048,128]{1,0:T(8,128)(2,1)S(1)}, u32[]{:S(2)}, u32[]{:S(2)}) collective-permute-start(bf16[2048,128]{1,0:T(8,128)(2,1)S(1)} %get-tuple-element.65), channel_id=1, source_target_pairs={{0,4},{4,0},{8,12},{12,8},{1,5},{5,1},{9,13},{13,9},{2,6},{6,2},{1... | collective-permute-start | bytes 1572872 | tf_op jit(solution)/shard_map/ppermute | solution.py:470
  104.9 15.1 %collective-permute-start.22 = (bf16[2048,128]{1,0:T(8,128)(2,1)S(1)}, bf16[2048,128]{1,0:T(8,128)(2,1)S(1)}, u32[]{:S(2)}, u32[]{:S(2)}) collective-permute-start(bf16[2048,128]{1,0:T(8,128)(2,1)S(1)} %get-tuple-element.66), channel_id=1, source_target_pairs={{0,3},{1,2},{2,1},{3,0},{4,7},{5,6},{6,5},{7,4},{8,11},{9,10},{10,... | collective-permute-start | bytes 1572872 | tf_op jit(solution)/shard_map/ppermute | solution.py:470
  108.5 11.6 %collective-permute-start.23 = (bf16[2048,128]{1,0:T(8,128)(2,1)S(1)}, bf16[2048,128]{1,0:T(8,128)(2,1)S(1)}, u32[]{:S(2)}, u32[]{:S(2)}) collective-permute-start(bf16[2048,128]{1,0:T(8,128)(2,1)S(1)} %get-tuple-element.67), channel_id=1, source_target_pairs={{0,1},{1,0},{2,3},{3,2},{4,5},{5,4},{6,7},{7,6},{8,9},{9,8},{10,11... | collective-permute-start | bytes 1572872 | tf_op jit(solution)/shard_map/ppermute | solution.py:470
  111.3 24.0 %copy-start.1 = (bf16[128,256]{1,0:T(8,128)(2,1)S(1)}, bf16[128,256]{1,0:T(8,128)(2,1)}, u32[]{:S(2)}) copy-start(bf16[128,256]{1,0:T(8,128)(2,1)} %refs_8_.1) | copy-start | bytes 196612
  111.3 24.0 %copy-start.2 = (f32[256]{0:T(256)S(1)}, f32[256]{0:T(256)}, u32[]{:S(2)}) copy-start(f32[256]{0:T(256)} %param.13) | copy-start | bytes 3076
  115.3 9.5 %collective-permute-start.19 = (bf16[1024,128]{1,0:T(8,128)(2,1)S(1)}, bf16[1024,128]{1,0:T(8,128)(2,1)S(1)}, u32[]{:S(2)}, u32[]{:S(2)}) collective-permute-start(bf16[1024,128]{1,0:T(8,128)(2,1)S(1)} %get-tuple-element.78), channel_id=1, source_target_pairs={{0,1},{1,0},{2,3},{3,2},{4,5},{5,4},{6,7},{7,6},{8,9},{9,8},{10,11... | collective-permute-start | bytes 786440 | tf_op jit(solution)/shard_map/ppermute | solution.py:478
  116.8 13.3 %collective-permute-start.20 = (bf16[1024,128]{1,0:T(8,128)(2,1)S(1)}, bf16[1024,128]{1,0:T(8,128)(2,1)S(1)}, u32[]{:S(2)}, u32[]{:S(2)}) collective-permute-start(bf16[1024,128]{1,0:T(8,128)(2,1)S(1)} %get-tuple-element.79), channel_id=1, source_target_pairs={{0,2},{1,3},{2,0},{3,1},{4,6},{5,7},{6,4},{7,5},{8,10},{9,11},{10,... | collective-permute-start | bytes 786440 | tf_op jit(solution)/shard_map/ppermute | solution.py:478
  119.5 12.5 %collective-permute-start.21 = (bf16[1024,128]{1,0:T(8,128)(2,1)S(1)}, bf16[1024,128]{1,0:T(8,128)(2,1)S(1)}, u32[]{:S(2)}, u32[]{:S(2)}) collective-permute-start(bf16[1024,128]{1,0:T(8,128)(2,1)S(1)} %get-tuple-element.80), channel_id=1, source_target_pairs={{0,3},{1,2},{2,1},{3,0},{4,7},{5,6},{6,5},{7,4},{8,11},{9,10},{10,... | collective-permute-start | bytes 786440 | tf_op jit(solution)/shard_map/ppermute | solution.py:478
  120.4 11.5 %collective-permute-start.24 = (bf16[1024,128]{1,0:T(8,128)(2,1)S(1)}, bf16[1024,128]{1,0:T(8,128)(2,1)S(1)}, u32[]{:S(2)}, u32[]{:S(2)}) collective-permute-start(bf16[1024,128]{1,0:T(8,128)(2,1)S(1)} %get-tuple-element.86), channel_id=1, source_target_pairs={{0,4},{4,0},{8,12},{12,8},{1,5},{5,1},{9,13},{13,9},{2,6},{6,2},{1... | collective-permute-start | bytes 786440 | tf_op jit(solution)/shard_map/ppermute | solution.py:478
  120.6 12.0 %collective-permute-start.25 = (bf16[1024,128]{1,0:T(8,128)(2,1)S(1)}, bf16[1024,128]{1,0:T(8,128)(2,1)S(1)}, u32[]{:S(2)}, u32[]{:S(2)}) collective-permute-start(bf16[1024,128]{1,0:T(8,128)(2,1)S(1)} %get-tuple-element.87), channel_id=1, source_target_pairs={{0,8},{4,12},{8,0},{12,4},{1,9},{5,13},{9,1},{13,5},{2,10},{6,14},... | collective-permute-start | bytes 786440 | tf_op jit(solution)/shard_map/ppermute | solution.py:478
  124.8 10.6 %collective-permute-start.26 = (bf16[1024,128]{1,0:T(8,128)(2,1)S(1)}, bf16[1024,128]{1,0:T(8,128)(2,1)S(1)}, u32[]{:S(2)}, u32[]{:S(2)}) collective-permute-start(bf16[1024,128]{1,0:T(8,128)(2,1)S(1)} %get-tuple-element.88), channel_id=1, source_target_pairs={{0,12},{4,8},{8,4},{12,0},{1,13},{5,9},{9,5},{13,1},{2,14},{6,10},... | collective-permute-start | bytes 786440 | tf_op jit(solution)/shard_map/ppermute | solution.py:478

commit v6 on v5

--- a/solution.py
+++ b/solution.py
@@ -10,8 +10,8 @@
 
 EXTRA = 8
 PICK = 1024
-UNROLL = 16
-SLOTS = 6
+UNROLL = 20
+SLOTS = 8
 STREAMS = 4
 PAIR = 2
 SIDE = 4
@@ -126,10 +126,9 @@
     )(index.reshape(-1, LANES), rows)
 
 
-def place_kernel(in_ref, out_ref, slot_ref, rows_ref):
+def place_kernel(first, in_ref, out_ref, slot_ref, rows_ref):
     peers, held, width = in_ref.shape
     capacity = held - EXTRA
-    local_rows = out_ref.shape[0]
     per = LANES // capacity
     extra = in_ref[:, capacity:, :].astype(F32)
     high, low = extra[:, 0, :], extra[:, 1, :]
@@ -143,19 +142,19 @@
     slot = jnp.concatenate([slot[q : q + 1, :] for q in range(peers // per)], axis=1)
 
     def place_rows(step, carry):
-        pick = (iota((PICK, peers * capacity), 0) + step * PICK == slot).astype(F32).astype(BF16)
+        pick = (iota((PICK, peers * capacity), 0) + (first + step * PICK) == slot).astype(F32).astype(BF16)
         rows = jnp.dot(pick, rows_ref[...], preferred_element_type=F32)
         out_ref[pl.ds(pl.multiple_of(step * PICK, PICK), PICK), :] = rows.astype(BF16)
         return carry
 
-    lax.fori_loop(0, local_rows // PICK, place_rows, 0)
-
-
-def place_rows(got, local_rows):
+    lax.fori_loop(0, out_ref.shape[0] // PICK, place_rows, 0)
+
+
+def place_rows(got, first, rows):
     peers, held, width = got.shape
     return pl.pallas_call(
-        place_kernel,
-        out_shape=jax.ShapeDtypeStruct((local_rows, width), BF16),
+        functools.partial(place_kernel, first),
+        out_shape=jax.ShapeDtypeStruct((rows, width), BF16),
         in_specs=[VMEM],
         out_specs=VMEM,
         scratch_shapes=[
@@ -456,13 +455,14 @@
     return lax.ppermute(array, axis, pairs)
 
 
-def gather_first(own):
-    half = own.shape[0] // 2
-    one, three = over(own, "y", 1), over(own, "y", 3)
-    other = over(own, "core", 1)
-    far = [over(one[:half], "y", 3), over(three[half:], "y", 1)]
-    near = [over(piece, "core", 1) for piece in (one, three)]
-    return [own, other, one, three, *near], far
+def gather_first(low, high):
+    one_low, three_low = over(low, "y", 1), over(low, "y", 3)
+    one_high, three_high = over(high, "y", 1), over(high, "y", 3)
+    other = [over(low, "core", 1), over(high, "core", 1)]
+    far = [over(one_low, "y", 3), over(three_high, "y", 1)]
+    halves = [one_low, one_high, three_low, three_high]
+    near = [over(piece, "core", 1) for piece in halves]
+    return [low, high, *other, *halves, *near], far
 
 
 def swap(arrays, axis, first):
@@ -498,8 +498,9 @@
     got = lax.all_to_all(packed, everyone, split_axis=0, concat_axis=0, tiled=True)
     table = plan_tiles(tile_count.reshape(1), codes)
     got, table = lax.optimization_barrier((got, table))
-    moved_rows = place_rows(got, local_rows)
-    early, far = gather_first(moved_rows)
+    half = local_rows // 2
+    low, high = (place_rows(got, first, half) for first in (0, half))
+    early, far = gather_first(low, high)
 
     rows = local_rows * grid_cols // 16
     axes = ("x", "z")

time: 138 us -> 136 us (0.986)
  waiting for transfers between devices: 59.2 us -> 42 us
  Pallas kernels: 29.7 us -> 45.2 us
    pallas_call x2, Pallas kernels: 6.37 us -> 14.2 us  [tile_products(): pl.pallas_call(functools.partial(tile_kernel, group, arrays), out_shape=[...]
    ppermute x9 -> x14, waiting for transfers between devices: 19.1 us -> 12.4 us  [over(): return lax.ppermute(array, axis, pairs)]
    ppermute x12, waiting for transfers between devices: 16.7 us -> 10.7 us  [swap(): lax.ppermute(array, axis, [(c, c ^ bit) for c in range(SIDE)])]
    pallas_call x1, Pallas kernels: 2.68 us -> 7.21 us  [plan_tiles(): pl.pallas_call(plan_kernel, out_shape=jax.ShapeDtypeStruct((5, codes.shap...]
    all_to_all x1, waiting for transfers between devices: 16.2 us -> 11.7 us  [body(): lax.all_to_all(packed, everyone, split_axis=0, concat_axis=0, tiled=True)]
    ppermute x12, starting transfers between devices: 16.8 us -> 13.4 us  [swap(): lax.ppermute(array, axis, [(c, c ^ bit) for c in range(SIDE)])]
    ppermute x9 -> x14, starting transfers between devices: 5.12 us -> 8.07 us  [over(): return lax.ppermute(array, axis, pairs)]
    pallas_call x1, Pallas kernels: 2.31 us -> 4.71 us  [early_products(): pl.pallas_call(functools.partial(early_kernel, group, len(pieces)), out_s...]
  transfers between devices with their start and end apart: 28 -> 33, of which waited for: 15 -> 17; matrix products, arithmetic and copies ran while one was open for 1% -> 1% of each run, Pallas kernels for 9% -> 22%
where the time goes in v6:
time: 136 us
  starting transfers between devices  46.3 us (34%)
  Pallas kernels  45.2 us (33%)
  waiting for transfers between devices  42 us (31%)
    pallas_call x2, Pallas kernels, tile_products(): pl.pallas_call(functools.partial(tile_kernel, group, arrays), out_shape=[...  14.2 us
    ppermute x6, starting transfers between devices, spread(): lax.ppermute(array, axis, [(c, c ^ bit) for c in range(SIDE)])  13.7 us
    ppermute x12, starting transfers between devices, swap(): lax.ppermute(array, axis, [(c, c ^ bit) for c in range(SIDE)])  13.4 us
    ppermute x14, waiting for transfers between devices, over(): return lax.ppermute(array, axis, pairs)  12.4 us
    all_to_all x1, waiting for transfers between devices, body(): lax.all_to_all(packed, everyone, split_axis=0, concat_axis=0, tiled=True)  11.7 us
    all_to_all x1, starting transfers between devices, body(): lax.all_to_all(packed, everyone, split_axis=0, concat_axis=0, tiled=True)  11.2 us
    ppermute x12, waiting for transfers between devices, swap(): lax.ppermute(array, axis, [(c, c ^ bit) for c in range(SIDE)])  10.7 us
    ppermute x14, starting transfers between devices, over(): return lax.ppermute(array, axis, pairs)  8.07 us
  transfers between devices with their start and end apart: 33, of which 17 were waited for; matrix products, arithmetic and copies ran while one was open for 1% of the time, Pallas kernels for 22%

profile of v6, /device:TPU:0, one launch (start us, length us, event | category | flops | bytes accessed | tf_op | source)
XLA Modules:
  0.0 135.8 jit_solution(11573388937070164845)
XLA Ops:
  0.0 7.9 %pack_rows.1 = bf16[128,40,128]{2,1,0:T(8,128)(2,1)} custom-call(s32[16,128]{1,0:T(8,128)} %bitcast.10, bf16[2048,128]{1,0:T(8,128)(2,1)} %rows_hbm.1), custom_call_target="tpu_custom_call" | custom-call | tf_op jit(solution)/shard_map/pack_rows/pallas_call | solution.py:112
  7.9 11.2 %all-to-all-start = ((bf16[128,40,128]{2,1,0:T(8,128)(2,1)}), bf16[128,40,128]{2,1,0:T(8,128)(2,1)S(1)}, u32[]{:S(2)}, u32[]{:S(2)}) async-start(bf16[128,40,128]{2,1,0:T(8,128)(2,1)} %pack_rows.1), calls=%async_computation | async-start | bytes 2621440 | tf_op jit(solution)/shard_map/all_to_all | solution.py:498
  19.9 0.6 or_or_fusion.code_ref
  20.5 7.2 %plan_tiles.1.table_ref = s32[5,660]{1,0:T(8,128)} custom-call(s32[1]{0:T(128)} %bitcast.4.count_ref, s32[640]{0:T(1024)} %or_or_fusion.code_ref), custom_call_target="tpu_custom_call" | custom-call | tf_op jit(solution)/shard_map/plan_tiles/pallas_call | solution.py:220
  27.7 11.7 %all-to-all-done.in_ref = bf16[128,40,128]{2,1,0:T(8,128)(2,1)S(1)} async-done(((bf16[128,40,128]{2,1,0:T(8,128)(2,1)}), bf16[128,40,128]{2,1,0:T(8,128)(2,1)S(1)}, u32[]{:S(2)}, u32[]{:S(2)}) %all-to-all-start) | async-done | bytes 1310752 | tf_op jit(solution)/shard_map/all_to_all | solution.py:498
  39.4 2.6 %place_rows.2.refs_0_ = bf16[1024,128]{1,0:T(8,128)(2,1)S(1)} custom-call(bf16[128,40,128]{2,1,0:T(8,128)(2,1)S(1)} %all-to-all-done.in_ref), custom_call_target="tpu_custom_call" | custom-call | tf_op jit(solution)/shard_map/place_rows/pallas_call | solution.py:155
  42.0 2.2 %collective-permute-start.7 = (bf16[1024,128]{1,0:T(8,128)(2,1)S(1)}, bf16[1024,128]{1,0:T(8,128)(2,1)S(1)}, u32[]{:S(2)}, u32[]{:S(2)}) collective-permute-start(bf16[1024,128]{1,0:T(8,128)(2,1)S(1)} %place_rows.2.refs_0_), channel_id=1, source_target_pairs={{0,96},{32,64},{64,32},{96,0},{1,97},{33,65},{65,33},{97,1},{2,98}... | collective-permute-start | bytes 786440 | tf_op jit(solution)/shard_map/ppermute | solution.py:455
  44.4 2.5 %place_rows.3.refs_1_ = bf16[1024,128]{1,0:T(8,128)(2,1)S(1)} custom-call(bf16[128,40,128]{2,1,0:T(8,128)(2,1)S(1)} %all-to-all-done.in_ref), custom_call_target="tpu_custom_call" | custom-call | tf_op jit(solution)/shard_map/place_rows/pallas_call | solution.py:155
  46.9 1.9 %collective-permute-start.6 = (bf16[1024,128]{1,0:T(8,128)(2,1)S(1)}, bf16[1024,128]{1,0:T(8,128)(2,1)S(1)}, u32[]{:S(2)}, u32[]{:S(2)}) collective-permute-start(bf16[1024,128]{1,0:T(8,128)(2,1)S(1)} %place_rows.3.refs_1_), channel_id=1, source_target_pairs={{0,32},{32,0},{64,96},{96,64},{1,33},{33,1},{65,97},{97,65},{2,34}... | collective-permute-start | bytes 786440 | tf_op jit(solution)/shard_map/ppermute | solution.py:455
  48.8 1.1 collective-permute-start.2
  49.9 1.1 collective-permute-done.7.refs_6_
  51.0 0.5 collective-permute-start.10
  51.5 1.8 %collective-permute-done.refs_4_ = bf16[1024,128]{1,0:T(8,128)(2,1)S(1)} collective-permute-done((bf16[1024,128]{1,0:T(8,128)(2,1)S(1)}, bf16[1024,128]{1,0:T(8,128)(2,1)S(1)}, u32[]{:S(2)}, u32[]{:S(2)}) %collective-permute-start) | collective-permute-done | bytes 262176 | tf_op jit(solution)/shard_map/ppermute | solution.py:455
  53.3 5.2 %collective-permute-done.6.refs_5_ = bf16[1024,128]{1,0:T(8,128)(2,1)S(1)} collective-permute-done((bf16[1024,128]{1,0:T(8,128)(2,1)S(1)}, bf16[1024,128]{1,0:T(8,128)(2,1)S(1)}, u32[]{:S(2)}, u32[]{:S(2)}) %collective-permute-start.6) | collective-permute-done | bytes 262176 | tf_op jit(solution)/shard_map/ppermute | solution.py:455
  58.5 0.5 collective-permute-start.11
  59.1 1.1 collective-permute-start.1
  60.5 0.7 copy-done
  61.2 4.7 %early_products.1 = (bf16[16384,128]{1,0:T(8,128)(2,1)S(1)}, f32[8320,128]{1,0:T(8,128)S(1)}) custom-call(s32[5,660]{1,0:T(8,128)S(1)} %copy-done, bf16[1024,128]{1,0:T(8,128)(2,1)S(1)} %place_rows.2.refs_0_, bf16[1024,128]{1,0:T(8,128)(2,1)S(1)} %place_rows.3.refs_1_, bf16[1024,128]{1,0:T(8,128)(2,1)S(1)} %collective-permute-done.4.refs_2_, ...), custom_call_target="tpu_custom_call" | custom-call | flops 5000000000 | bytes 5000000 | tf_op jit(solution)/shard_map/early_products/pallas_call | solution.py:344
  65.9 2.7 %collective-permute-done.1.refs_0_ = bf16[1024,128]{1,0:T(8,128)(2,1)S(1)} collective-permute-done((bf16[1024,128]{1,0:T(8,128)(2,1)S(1)}, bf16[1024,128]{1,0:T(8,128)(2,1)S(1)}, u32[]{:S(2)}, u32[]{:S(2)}) %collective-permute-start.1) | collective-permute-done | bytes 262176 | tf_op jit(solution)/shard_map/ppermute | solution.py:455
  68.6 0.5 collective-permute-start.13
  69.1 1.0 collective-permute-done.12.refs_2_
  70.5 3.3 %late_products.1 = (bf16[16384,128]{1,0:T(8,128)(2,1)S(1)}, f32[8320,128]{1,0:T(8,128)S(1)}, bf16[2048,128]{1,0:T(8,128)(2,1)S(1)}, bf16[2048,128]{1,0:T(8,128)(...) custom-call(s32[5,660]{1,0:T(8,128)S(1)} %copy-done, ...), custom_call_target="tpu_custom_call", output_to_operand_aliasing={{0}: (6, {}), {1}: (7, {})} | custom-call | flops 5000000000 | bytes 5000000 | tf_op jit(solution)/shard_map/late_products/pallas_call | solution.py:362
  74.2 1.0 collective-permute-start.15
  75.1 1.9 %collective-permute-start.16 = (bf16[2048,128]{1,0:T(8,128)(2,1)S(1)}, bf16[2048,128]{1,0:T(8,128)(2,1)S(1)}, u32[]{:S(2)}, u32[]{:S(2)}) collective-permute-start(bf16[2048,128]{1,0:T(8,128)(2,1)S(1)} %get-tuple-element.61), channel_id=1, source_target_pairs={{0,1},{1,0},{2,3},{3,2},{4,5},{5,4},{6,7},{7,6},{8,9},{9,8},{10,11... | collective-permute-start | bytes 1572872 | tf_op jit(solution)/shard_map/ppermute | solution.py:470
  77.4 9.2 %tile_products.2 = (bf16[2048,128]{1,0:T(8,128)(2,1)S(1)}, bf16[2048,128]{1,0:T(8,128)(2,1)S(1)}, bf16[2048,128]{1,0:T(8,128)(2,1)S(1)}, bf16[2048,128]{1,0:T(8,...) custom-call(s32[5,660]{1,0:T(8,128)S(1)} %copy-done, ...), custom_call_target="tpu_custom_call" | custom-call | flops 40000000000 | bytes 40000000 | tf_op jit(solution)/shard_map/tile_products/pallas_call | solution.py:330
  86.7 1.3 collective-permute-done.14.refs_1_
  88.0 1.4 %collective-permute-start.19 = (bf16[2048,128]{1,0:T(8,128)(2,1)S(1)}, bf16[2048,128]{1,0:T(8,128)(2,1)S(1)}, u32[]{:S(2)}, u32[]{:S(2)}) collective-permute-start(bf16[2048,128]{1,0:T(8,128)(2,1)S(1)} %get-tuple-element.69), channel_id=1, source_target_pairs={{0,12},{4,8},{8,4},{12,0},{1,13},{5,9},{9,5},{13,1},{2,14},{6,10},... | collective-permute-start | bytes 1572872 | tf_op jit(solution)/shard_map/ppermute | solution.py:470
  89.9 1.5 %collective-permute-start.21 = (bf16[2048,128]{1,0:T(8,128)(2,1)S(1)}, bf16[2048,128]{1,0:T(8,128)(2,1)S(1)}, u32[]{:S(2)}, u32[]{:S(2)}) collective-permute-start(bf16[2048,128]{1,0:T(8,128)(2,1)S(1)} %get-tuple-element.71), channel_id=1, source_target_pairs={{0,3},{1,2},{2,1},{3,0},{4,7},{5,6},{6,5},{7,4},{8,11},{9,10},{10,... | collective-permute-start | bytes 1572872 | tf_op jit(solution)/shard_map/ppermute | solution.py:470
  91.4 0.5 forward_sums.1
  91.9 2.9 %collective-permute-start.22 = (bf16[2048,128]{1,0:T(8,128)(2,1)S(1)}, bf16[2048,128]{1,0:T(8,128)(2,1)S(1)}, u32[]{:S(2)}, u32[]{:S(2)}) collective-permute-start(bf16[2048,128]{1,0:T(8,128)(2,1)S(1)} %get-tuple-element.64), channel_id=1, source_target_pairs={{0,12},{4,8},{8,4},{12,0},{1,13},{5,9},{9,5},{13,1},{2,14},{6,10},... | collective-permute-start | bytes 1572872 | tf_op jit(solution)/shard_map/ppermute | solution.py:470
  94.8 3.9 %collective-permute-done.18.refs_1_ = bf16[2048,128]{1,0:T(8,128)(2,1)S(1)} collective-permute-done((bf16[2048,128]{1,0:T(8,128)(2,1)S(1)}, bf16[2048,128]{1,0:T(8,128)(2,1)S(1)}, u32[]{:S(2)}, u32[]{:S(2)}) %collective-permute-start.18) | collective-permute-done | bytes 524320 | tf_op jit(solution)/shard_map/ppermute | solution.py:470
  98.8 1.2 collective-permute-start.23
  99.9 4.1 %collective-permute-done.19.refs_4_ = bf16[2048,128]{1,0:T(8,128)(2,1)S(1)} collective-permute-done((bf16[2048,128]{1,0:T(8,128)(2,1)S(1)}, bf16[2048,128]{1,0:T(8,128)(2,1)S(1)}, u32[]{:S(2)}, u32[]{:S(2)}) %collective-permute-start.19) | collective-permute-done | bytes 524320 | tf_op jit(solution)/shard_map/ppermute | solution.py:470
  104.1 0.5 collective-permute-start.27
  104.6 1.9 %collective-permute-start.28 = (bf16[2048,128]{1,0:T(8,128)(2,1)S(1)}, bf16[2048,128]{1,0:T(8,128)(2,1)S(1)}, u32[]{:S(2)}, u32[]{:S(2)}) collective-permute-start(bf16[2048,128]{1,0:T(8,128)(2,1)S(1)} %get-tuple-element.67), channel_id=1, source_target_pairs={{0,1},{1,0},{2,3},{3,2},{4,5},{5,4},{6,7},{7,6},{8,9},{9,8},{10,11... | collective-permute-start | bytes 1572872 | tf_op jit(solution)/shard_map/ppermute | solution.py:470
  106.5 5.1 %tile_products.3 = (bf16[2048,128]{1,0:T(8,128)(2,1)S(1)}, bf16[2048,128]{1,0:T(8,128)(2,1)S(1)}, bf16[2048,128]{1,0:T(8,128)(2,1)S(1)}, bf16[2048,128]{1,0:T(8,128)(2,1)S(1)}) custom-call(s32[5,660]{1,0:T(8,128)S(1)} %copy-done, bf16[16384,128]{1,0:T(8,128)(2,1)S(1)} %get-tuple-element.55.x_ref, bf16[640,128,128]{2,1,0:T(8,128)(2,1)} %bitcast.9), custom_call_target="tpu_custom_call" | custom-call | flops 20000000000 | bytes 20000000 | tf_op jit(solution)/shard_map/tile_products/pallas_call | solution.py:330
  111.6 1.1 collective-permute-done.22.refs_2_
  113.1 1.8 %collective-permute-start.24 = (bf16[1024,128]{1,0:T(8,128)(2,1)S(1)}, bf16[1024,128]{1,0:T(8,128)(2,1)S(1)}, u32[]{:S(2)}, u32[]{:S(2)}) collective-permute-start(bf16[1024,128]{1,0:T(8,128)(2,1)S(1)} %get-tuple-element.78), channel_id=1, source_target_pairs={{0,1},{1,0},{2,3},{3,2},{4,5},{5,4},{6,7},{7,6},{8,9},{9,8},{10,11... | collective-permute-start | bytes 786440 | tf_op jit(solution)/shard_map/ppermute | solution.py:478
  114.9 1.7 %collective-permute-start.25 = (bf16[1024,128]{1,0:T(8,128)(2,1)S(1)}, bf16[1024,128]{1,0:T(8,128)(2,1)S(1)}, u32[]{:S(2)}, u32[]{:S(2)}) collective-permute-start(bf16[1024,128]{1,0:T(8,128)(2,1)S(1)} %get-tuple-element.79), channel_id=1, source_target_pairs={{0,2},{1,3},{2,0},{3,1},{4,6},{5,7},{6,4},{7,5},{8,10},{9,11},{10,... | collective-permute-start | bytes 786440 | tf_op jit(solution)/shard_map/ppermute | solution.py:478
  116.6 1.3 collective-permute-start.26
  118.2 0.9 collective-permute-start.29
  119.2 4.6 %collective-permute-start.30 = (bf16[1024,128]{1,0:T(8,128)(2,1)S(1)}, bf16[1024,128]{1,0:T(8,128)(2,1)S(1)}, u32[]{:S(2)}, u32[]{:S(2)}) collective-permute-start(bf16[1024,128]{1,0:T(8,128)(2,1)S(1)} %get-tuple-element.87), channel_id=1, source_target_pairs={{0,8},{4,12},{8,0},{12,4},{1,9},{5,13},{9,1},{13,5},{2,10},{6,14},... | collective-permute-start | bytes 786440 | tf_op jit(solution)/shard_map/ppermute | solution.py:478
  123.8 3.4 %collective-permute-start.31 = (bf16[1024,128]{1,0:T(8,128)(2,1)S(1)}, bf16[1024,128]{1,0:T(8,128)(2,1)S(1)}, u32[]{:S(2)}, u32[]{:S(2)}) collective-permute-start(bf16[1024,128]{1,0:T(8,128)(2,1)S(1)} %get-tuple-element.88), channel_id=1, source_target_pairs={{0,12},{4,8},{8,4},{12,0},{1,13},{5,9},{9,5},{13,1},{2,14},{6,10},... | collective-permute-start | bytes 786440 | tf_op jit(solution)/shard_map/ppermute | solution.py:478
  127.1 0.8 collective-permute-done.25.refs_2_
  128.0 2.0 %collective-permute-done.26.refs_3_ = bf16[1024,128]{1,0:T(8,128)(2,1)S(1)} collective-permute-done((bf16[1024,128]{1,0:T(8,128)(2,1)S(1)}, bf16[1024,128]{1,0:T(8,128)(2,1)S(1)}, u32[]{:S(2)}, u32[]{:S(2)}) %collective-permute-start.26) | collective-permute-done | bytes 262176 | tf_op jit(solution)/shard_map/ppermute | solution.py:478
  129.9 1.7 %collective-permute-done.30.refs_6_ = bf16[1024,128]{1,0:T(8,128)(2,1)S(1)} collective-permute-done((bf16[1024,128]{1,0:T(8,128)(2,1)S(1)}, bf16[1024,128]{1,0:T(8,128)(2,1)S(1)}, u32[]{:S(2)}, u32[]{:S(2)}) %collective-permute-start.30) | collective-permute-done | bytes 262176 | tf_op jit(solution)/shard_map/ppermute | solution.py:478
  131.6 2.7 %collective-permute-done.31.refs_7_ = bf16[1024,128]{1,0:T(8,128)(2,1)S(1)} collective-permute-done((bf16[1024,128]{1,0:T(8,128)(2,1)S(1)}, bf16[1024,128]{1,0:T(8,128)(2,1)S(1)}, u32[]{:S(2)}, u32[]{:S(2)}) %collective-permute-start.31) | collective-permute-done | bytes 262176 | tf_op jit(solution)/shard_map/ppermute | solution.py:478
  134.3 1.5 %dense.1 = bf16[2048,256]{1,0:T(8,128)(2,1)} custom-call(f32[1024,128]{1,0:T(8,128)S(1)} %get-tuple-element.77.refs_0_, bf16[1024,128]{1,0:T(8,128)(2,1)S(1)} %collective-permute-done.24.refs_1_, bf16[1024,128]{1,0:T(8,128)(2,1)S(1)} %collective-permute-done.25.refs_2_, bf16[1024,128]{1,0:T(8,128)(2,1)S(1)} %collective-permute-done.26.refs_3_, ...), custom_call_target="tpu_custom_call" | custom-call | tf_op jit(solution)/shard_map/dense/pallas_call | solution.py:443
  (41 shorter events, 3.0 us)
Async XLA Ops:
  0.0 19.8 %copy-start.3 = (s32[1,1,2,640]{3,2,1,0:T(2,128)S(1)}, s32[1,1,2,640]{3,2,1,0:T(2,128)}, u32[]{:S(2)}) copy-start(s32[1,1,2,640]{3,2,1,0:T(2,128)} %param.10) | copy-start | bytes 15364
  7.9 31.5 %all-to-all-start = ((bf16[128,40,128]{2,1,0:T(8,128)(2,1)}), bf16[128,40,128]{2,1,0:T(8,128)(2,1)S(1)}, u32[]{:S(2)}, u32[]{:S(2)}) async-start(bf16[128,40,128]{2,1,0:T(8,128)(2,1)} %pack_rows.1), calls=%async_computation | async-start | bytes 2621440 | tf_op jit(solution)/shard_map/all_to_all | solution.py:498
  42.0 9.0 %collective-permute-start.7 = (bf16[1024,128]{1,0:T(8,128)(2,1)S(1)}, bf16[1024,128]{1,0:T(8,128)(2,1)S(1)}, u32[]{:S(2)}, u32[]{:S(2)}) collective-permute-start(bf16[1024,128]{1,0:T(8,128)(2,1)S(1)} %place_rows.2.refs_0_), channel_id=1, source_target_pairs={{0,96},{32,64},{64,32},{96,0},{1,97},{33,65},{65,33},{97,1},{2,98}... | collective-permute-start | bytes 786440 | tf_op jit(solution)/shard_map/ppermute | solution.py:455
  44.2 6.8 %collective-permute-start.4 = (bf16[1024,128]{1,0:T(8,128)(2,1)S(1)}, bf16[1024,128]{1,0:T(8,128)(2,1)S(1)}, u32[]{:S(2)}, u32[]{:S(2)}) collective-permute-start(bf16[1024,128]{1,0:T(8,128)(2,1)S(1)} %place_rows.2.refs_0_), channel_id=1, source_target_pairs={{0,16},{16,0},{1,17},{17,1},{2,18},{18,2},{3,19},{19,3},{4,20},{20... | collective-permute-start | bytes 786440 | tf_op jit(solution)/shard_map/ppermute | solution.py:455
  44.2 9.1 %collective-permute-start = (bf16[1024,128]{1,0:T(8,128)(2,1)S(1)}, bf16[1024,128]{1,0:T(8,128)(2,1)S(1)}, u32[]{:S(2)}, u32[]{:S(2)}) collective-permute-start(bf16[1024,128]{1,0:T(8,128)(2,1)S(1)} %place_rows.2.refs_0_), channel_id=1, source_target_pairs={{0,32},{32,0},{64,96},{96,64},{1,33},{33,1},{65,97},{97,65},{2,34}... | collective-permute-start | bytes 786440 | tf_op jit(solution)/shard_map/ppermute | solution.py:455
  46.9 11.6 %collective-permute-start.6 = (bf16[1024,128]{1,0:T(8,128)(2,1)S(1)}, bf16[1024,128]{1,0:T(8,128)(2,1)S(1)}, u32[]{:S(2)}, u32[]{:S(2)}) collective-permute-start(bf16[1024,128]{1,0:T(8,128)(2,1)S(1)} %place_rows.3.refs_1_), channel_id=1, source_target_pairs={{0,32},{32,0},{64,96},{96,64},{1,33},{33,1},{65,97},{97,65},{2,34}... | collective-permute-start | bytes 786440 | tf_op jit(solution)/shard_map/ppermute | solution.py:455
  48.8 9.7 %collective-permute-start.2 = (bf16[1024,128]{1,0:T(8,128)(2,1)S(1)}, bf16[1024,128]{1,0:T(8,128)(2,1)S(1)}, u32[]{:S(2)}, u32[]{:S(2)}) collective-permute-start(bf16[1024,128]{1,0:T(8,128)(2,1)S(1)} %place_rows.3.refs_1_), channel_id=1, source_target_pairs={{0,96},{32,64},{64,32},{96,0},{1,97},{33,65},{65,33},{97,1},{2,98}... | collective-permute-start | bytes 786440 | tf_op jit(solution)/shard_map/ppermute | solution.py:455
  51.0 8.1 %collective-permute-start.5 = (bf16[1024,128]{1,0:T(8,128)(2,1)S(1)}, bf16[1024,128]{1,0:T(8,128)(2,1)S(1)}, u32[]{:S(2)}, u32[]{:S(2)}) collective-permute-start(bf16[1024,128]{1,0:T(8,128)(2,1)S(1)} %place_rows.3.refs_1_), channel_id=1, source_target_pairs={{0,16},{16,0},{1,17},{17,1},{2,18},{18,2},{3,19},{19,3},{4,20},{20... | collective-permute-start | bytes 786440 | tf_op jit(solution)/shard_map/ppermute | solution.py:455
  51.0 9.2 %collective-permute-start.10 = (bf16[1024,128]{1,0:T(8,128)(2,1)S(1)}, bf16[1024,128]{1,0:T(8,128)(2,1)S(1)}, u32[]{:S(2)}, u32[]{:S(2)}) collective-permute-start(bf16[1024,128]{1,0:T(8,128)(2,1)S(1)} %collective-permute-done.7.refs_6_), channel_id=1, source_target_pairs={{0,16},{16,0},{1,17},{17,1},{2,18},{18,2},{3,19},{19,3},{4,20},{20... | collective-permute-start | bytes 786440 | tf_op jit(solution)/shard_map/ppermute | solution.py:455
  53.3 6.9 %collective-permute-start.8 = (bf16[1024,128]{1,0:T(8,128)(2,1)S(1)}, bf16[1024,128]{1,0:T(8,128)(2,1)S(1)}, u32[]{:S(2)}, u32[]{:S(2)}) collective-permute-start(bf16[1024,128]{1,0:T(8,128)(2,1)S(1)} %collective-permute-done.refs_4_), channel_id=1, source_target_pairs={{0,16},{16,0},{1,17},{17,1},{2,18},{18,2},{3,19},{19,3},{4,20},{20... | collective-permute-start | bytes 786440 | tf_op jit(solution)/shard_map/ppermute | solution.py:455
  58.5 1.6 %collective-permute-start.9 = (bf16[1024,128]{1,0:T(8,128)(2,1)S(1)}, bf16[1024,128]{1,0:T(8,128)(2,1)S(1)}, u32[]{:S(2)}, u32[]{:S(2)}) collective-permute-start(bf16[1024,128]{1,0:T(8,128)(2,1)S(1)} %collective-permute-done.6.refs_5_), channel_id=1, source_target_pairs={{0,16},{16,0},{1,17},{17,1},{2,18},{18,2},{3,19},{19,3},{4,20},{20... | collective-permute-start | bytes 786440 | tf_op jit(solution)/shard_map/ppermute | solution.py:455
  58.5 1.9 %collective-permute-start.11 = (bf16[1024,128]{1,0:T(8,128)(2,1)S(1)}, bf16[1024,128]{1,0:T(8,128)(2,1)S(1)}, u32[]{:S(2)}, u32[]{:S(2)}) collective-permute-start(bf16[1024,128]{1,0:T(8,128)(2,1)S(1)} %collective-permute-done.2.refs_7_), channel_id=1, source_target_pairs={{0,16},{16,0},{1,17},{17,1},{2,18},{18,2},{3,19},{19,3},{4,20},{20... | collective-permute-start | bytes 786440 | tf_op jit(solution)/shard_map/ppermute | solution.py:455
  59.1 9.5 %collective-permute-start.1 = (bf16[1024,128]{1,0:T(8,128)(2,1)S(1)}, bf16[1024,128]{1,0:T(8,128)(2,1)S(1)}, u32[]{:S(2)}, u32[]{:S(2)}) collective-permute-start(bf16[1024,128]{1,0:T(8,128)(2,1)S(1)} %collective-permute-done.refs_4_), channel_id=1, source_target_pairs={{0,96},{32,64},{64,32},{96,0},{1,97},{33,65},{65,33},{97,1},{2,98}... | collective-permute-start | bytes 786440 | tf_op jit(solution)/shard_map/ppermute | solution.py:455
  60.2 8.4 %collective-permute-start.3 = (bf16[1024,128]{1,0:T(8,128)(2,1)S(1)}, bf16[1024,128]{1,0:T(8,128)(2,1)S(1)}, u32[]{:S(2)}, u32[]{:S(2)}) collective-permute-start(bf16[1024,128]{1,0:T(8,128)(2,1)S(1)} %collective-permute-done.2.refs_7_), channel_id=1, source_target_pairs={{0,32},{32,0},{64,96},{96,64},{1,33},{33,1},{65,97},{97,65},{2,34}... | collective-permute-start | bytes 786440 | tf_op jit(solution)/shard_map/ppermute | solution.py:455
  60.5 0.7 copy-start
  68.6 1.5 %collective-permute-start.12 = (bf16[1024,128]{1,0:T(8,128)(2,1)S(1)}, bf16[1024,128]{1,0:T(8,128)(2,1)S(1)}, u32[]{:S(2)}, u32[]{:S(2)}) collective-permute-start(bf16[1024,128]{1,0:T(8,128)(2,1)S(1)} %collective-permute-done.1.refs_0_), channel_id=1, source_target_pairs={{0,16},{16,0},{1,17},{17,1},{2,18},{18,2},{3,19},{19,3},{4,20},{20... | collective-permute-start | bytes 786440 | tf_op jit(solution)/shard_map/ppermute | solution.py:455
  68.6 1.9 %collective-permute-start.13 = (bf16[1024,128]{1,0:T(8,128)(2,1)S(1)}, bf16[1024,128]{1,0:T(8,128)(2,1)S(1)}, u32[]{:S(2)}, u32[]{:S(2)}) collective-permute-start(bf16[1024,128]{1,0:T(8,128)(2,1)S(1)} %collective-permute-done.3.refs_1_), channel_id=1, source_target_pairs={{0,16},{16,0},{1,17},{17,1},{2,18},{18,2},{3,19},{19,3},{4,20},{20... | collective-permute-start | bytes 786440 | tf_op jit(solution)/shard_map/ppermute | solution.py:455
  73.8 14.2 %collective-permute-start.14 = (bf16[2048,128]{1,0:T(8,128)(2,1)S(1)}, bf16[2048,128]{1,0:T(8,128)(2,1)S(1)}, u32[]{:S(2)}, u32[]{:S(2)}) collective-permute-start(bf16[2048,128]{1,0:T(8,128)(2,1)S(1)} %get-tuple-element.57), channel_id=1, source_target_pairs={{0,4},{4,0},{8,12},{12,8},{1,5},{5,1},{9,13},{13,9},{2,6},{6,2},{1... | collective-permute-start | bytes 1572872 | tf_op jit(solution)/shard_map/ppermute | solution.py:470
  74.2 15.5 %collective-permute-start.15 = (bf16[2048,128]{1,0:T(8,128)(2,1)S(1)}, bf16[2048,128]{1,0:T(8,128)(2,1)S(1)}, u32[]{:S(2)}, u32[]{:S(2)}) collective-permute-start(bf16[2048,128]{1,0:T(8,128)(2,1)S(1)} %get-tuple-element.59), channel_id=1, source_target_pairs={{0,12},{4,8},{8,4},{12,0},{1,13},{5,9},{9,5},{13,1},{2,14},{6,10},... | collective-permute-start | bytes 1572872 | tf_op jit(solution)/shard_map/ppermute | solution.py:470
  75.1 14.7 %collective-permute-start.16 = (bf16[2048,128]{1,0:T(8,128)(2,1)S(1)}, bf16[2048,128]{1,0:T(8,128)(2,1)S(1)}, u32[]{:S(2)}, u32[]{:S(2)}) collective-permute-start(bf16[2048,128]{1,0:T(8,128)(2,1)S(1)} %get-tuple-element.61), channel_id=1, source_target_pairs={{0,1},{1,0},{2,3},{3,2},{4,5},{5,4},{6,7},{7,6},{8,9},{9,8},{10,11... | collective-permute-start | bytes 1572872 | tf_op jit(solution)/shard_map/ppermute | solution.py:470
  77.1 14.3 %collective-permute-start.17 = (bf16[2048,128]{1,0:T(8,128)(2,1)S(1)}, bf16[2048,128]{1,0:T(8,128)(2,1)S(1)}, u32[]{:S(2)}, u32[]{:S(2)}) collective-permute-start(bf16[2048,128]{1,0:T(8,128)(2,1)S(1)} %get-tuple-element.63), channel_id=1, source_target_pairs={{0,3},{1,2},{2,1},{3,0},{4,7},{5,6},{6,5},{7,4},{8,11},{9,10},{10,... | collective-permute-start | bytes 1572872 | tf_op jit(solution)/shard_map/ppermute | solution.py:470
  86.6 12.2 %collective-permute-start.18 = (bf16[2048,128]{1,0:T(8,128)(2,1)S(1)}, bf16[2048,128]{1,0:T(8,128)(2,1)S(1)}, u32[]{:S(2)}, u32[]{:S(2)}) collective-permute-start(bf16[2048,128]{1,0:T(8,128)(2,1)S(1)} %get-tuple-element.68), channel_id=1, source_target_pairs={{0,4},{4,0},{8,12},{12,8},{1,5},{5,1},{9,13},{13,9},{2,6},{6,2},{1... | collective-permute-start | bytes 1572872 | tf_op jit(solution)/shard_map/ppermute | solution.py:470
  88.0 16.1 %collective-permute-start.19 = (bf16[2048,128]{1,0:T(8,128)(2,1)S(1)}, bf16[2048,128]{1,0:T(8,128)(2,1)S(1)}, u32[]{:S(2)}, u32[]{:S(2)}) collective-permute-start(bf16[2048,128]{1,0:T(8,128)(2,1)S(1)} %get-tuple-element.69), channel_id=1, source_target_pairs={{0,12},{4,8},{8,4},{12,0},{1,13},{5,9},{9,5},{13,1},{2,14},{6,10},... | collective-permute-start | bytes 1572872 | tf_op jit(solution)/shard_map/ppermute | solution.py:470
  89.6 15.0 %collective-permute-start.20 = (bf16[2048,128]{1,0:T(8,128)(2,1)S(1)}, bf16[2048,128]{1,0:T(8,128)(2,1)S(1)}, u32[]{:S(2)}, u32[]{:S(2)}) collective-permute-start(bf16[2048,128]{1,0:T(8,128)(2,1)S(1)} %get-tuple-element.70), channel_id=1, source_target_pairs={{0,1},{1,0},{2,3},{3,2},{4,5},{5,4},{6,7},{7,6},{8,9},{9,8},{10,11... | collective-permute-start | bytes 1572872 | tf_op jit(solution)/shard_map/ppermute | solution.py:470
  89.9 16.6 %collective-permute-start.21 = (bf16[2048,128]{1,0:T(8,128)(2,1)S(1)}, bf16[2048,128]{1,0:T(8,128)(2,1)S(1)}, u32[]{:S(2)}, u32[]{:S(2)}) collective-permute-start(bf16[2048,128]{1,0:T(8,128)(2,1)S(1)} %get-tuple-element.71), channel_id=1, source_target_pairs={{0,3},{1,2},{2,1},{3,0},{4,7},{5,6},{6,5},{7,4},{8,11},{9,10},{10,... | collective-permute-start | bytes 1572872 | tf_op jit(solution)/shard_map/ppermute | solution.py:470
  91.9 20.8 %collective-permute-start.22 = (bf16[2048,128]{1,0:T(8,128)(2,1)S(1)}, bf16[2048,128]{1,0:T(8,128)(2,1)S(1)}, u32[]{:S(2)}, u32[]{:S(2)}) collective-permute-start(bf16[2048,128]{1,0:T(8,128)(2,1)S(1)} %get-tuple-element.64), channel_id=1, source_target_pairs={{0,12},{4,8},{8,4},{12,0},{1,13},{5,9},{9,5},{13,1},{2,14},{6,10},... | collective-permute-start | bytes 1572872 | tf_op jit(solution)/shard_map/ppermute | solution.py:470
  98.8 14.0 %collective-permute-start.23 = (bf16[2048,128]{1,0:T(8,128)(2,1)S(1)}, bf16[2048,128]{1,0:T(8,128)(2,1)S(1)}, u32[]{:S(2)}, u32[]{:S(2)}) collective-permute-start(bf16[2048,128]{1,0:T(8,128)(2,1)S(1)} %get-tuple-element.65), channel_id=1, source_target_pairs={{0,4},{4,0},{8,12},{12,8},{1,5},{5,1},{9,13},{13,9},{2,6},{6,2},{1... | collective-permute-start | bytes 1572872 | tf_op jit(solution)/shard_map/ppermute | solution.py:470
  104.1 13.8 %collective-permute-start.27 = (bf16[2048,128]{1,0:T(8,128)(2,1)S(1)}, bf16[2048,128]{1,0:T(8,128)(2,1)S(1)}, u32[]{:S(2)}, u32[]{:S(2)}) collective-permute-start(bf16[2048,128]{1,0:T(8,128)(2,1)S(1)} %get-tuple-element.66), channel_id=1, source_target_pairs={{0,3},{1,2},{2,1},{3,0},{4,7},{5,6},{6,5},{7,4},{8,11},{9,10},{10,... | collective-permute-start | bytes 1572872 | tf_op jit(solution)/shard_map/ppermute | solution.py:470
  104.6 13.2 %collective-permute-start.28 = (bf16[2048,128]{1,0:T(8,128)(2,1)S(1)}, bf16[2048,128]{1,0:T(8,128)(2,1)S(1)}, u32[]{:S(2)}, u32[]{:S(2)}) collective-permute-start(bf16[2048,128]{1,0:T(8,128)(2,1)S(1)} %get-tuple-element.67), channel_id=1, source_target_pairs={{0,1},{1,0},{2,3},{3,2},{4,5},{5,4},{6,7},{7,6},{8,9},{9,8},{10,11... | collective-permute-start | bytes 1572872 | tf_op jit(solution)/shard_map/ppermute | solution.py:470
  111.6 22.7 %copy-start.1 = (bf16[128,256]{1,0:T(8,128)(2,1)S(1)}, bf16[128,256]{1,0:T(8,128)(2,1)}, u32[]{:S(2)}) copy-start(bf16[128,256]{1,0:T(8,128)(2,1)} %refs_8_.1) | copy-start | bytes 196612
  111.6 22.7 %copy-start.2 = (f32[256]{0:T(256)S(1)}, f32[256]{0:T(256)}, u32[]{:S(2)}) copy-start(f32[256]{0:T(256)} %param.13) | copy-start | bytes 3076
  113.1 10.7 %collective-permute-start.24 = (bf16[1024,128]{1,0:T(8,128)(2,1)S(1)}, bf16[1024,128]{1,0:T(8,128)(2,1)S(1)}, u32[]{:S(2)}, u32[]{:S(2)}) collective-permute-start(bf16[1024,128]{1,0:T(8,128)(2,1)S(1)} %get-tuple-element.78), channel_id=1, source_target_pairs={{0,1},{1,0},{2,3},{3,2},{4,5},{5,4},{6,7},{7,6},{8,9},{9,8},{10,11... | collective-permute-start | bytes 786440 | tf_op jit(solution)/shard_map/ppermute | solution.py:478
  114.9 13.1 %collective-permute-start.25 = (bf16[1024,128]{1,0:T(8,128)(2,1)S(1)}, bf16[1024,128]{1,0:T(8,128)(2,1)S(1)}, u32[]{:S(2)}, u32[]{:S(2)}) collective-permute-start(bf16[1024,128]{1,0:T(8,128)(2,1)S(1)} %get-tuple-element.79), channel_id=1, source_target_pairs={{0,2},{1,3},{2,0},{3,1},{4,6},{5,7},{6,4},{7,5},{8,10},{9,11},{10,... | collective-permute-start | bytes 786440 | tf_op jit(solution)/shard_map/ppermute | solution.py:478
  116.6 13.4 %collective-permute-start.26 = (bf16[1024,128]{1,0:T(8,128)(2,1)S(1)}, bf16[1024,128]{1,0:T(8,128)(2,1)S(1)}, u32[]{:S(2)}, u32[]{:S(2)}) collective-permute-start(bf16[1024,128]{1,0:T(8,128)(2,1)S(1)} %get-tuple-element.80), channel_id=1, source_target_pairs={{0,3},{1,2},{2,1},{3,0},{4,7},{5,6},{6,5},{7,4},{8,11},{9,10},{10,... | collective-permute-start | bytes 786440 | tf_op jit(solution)/shard_map/ppermute | solution.py:478
  118.2 11.7 %collective-permute-start.29 = (bf16[1024,128]{1,0:T(8,128)(2,1)S(1)}, bf16[1024,128]{1,0:T(8,128)(2,1)S(1)}, u32[]{:S(2)}, u32[]{:S(2)}) collective-permute-start(bf16[1024,128]{1,0:T(8,128)(2,1)S(1)} %get-tuple-element.86), channel_id=1, source_target_pairs={{0,4},{4,0},{8,12},{12,8},{1,5},{5,1},{9,13},{13,9},{2,6},{6,2},{1... | collective-permute-start | bytes 786440 | tf_op jit(solution)/shard_map/ppermute | solution.py:478
  119.2 12.5 %collective-permute-start.30 = (bf16[1024,128]{1,0:T(8,128)(2,1)S(1)}, bf16[1024,128]{1,0:T(8,128)(2,1)S(1)}, u32[]{:S(2)}, u32[]{:S(2)}) collective-permute-start(bf16[1024,128]{1,0:T(8,128)(2,1)S(1)} %get-tuple-element.87), channel_id=1, source_target_pairs={{0,8},{4,12},{8,0},{12,4},{1,9},{5,13},{9,1},{13,5},{2,10},{6,14},... | collective-permute-start | bytes 786440 | tf_op jit(solution)/shard_map/ppermute | solution.py:478
  123.8 10.5 %collective-permute-start.31 = (bf16[1024,128]{1,0:T(8,128)(2,1)S(1)}, bf16[1024,128]{1,0:T(8,128)(2,1)S(1)}, u32[]{:S(2)}, u32[]{:S(2)}) collective-permute-start(bf16[1024,128]{1,0:T(8,128)(2,1)S(1)} %get-tuple-element.88), channel_id=1, source_target_pairs={{0,12},{4,8},{8,4},{12,0},{1,13},{5,9},{9,5},{13,1},{2,14},{6,10},... | collective-permute-start | bytes 786440 | tf_op jit(solution)/shard_map/ppermute | solution.py:478

commit v7 on v6

--- a/solution.py
+++ b/solution.py
@@ -426,28 +426,27 @@
     )(*ins)
 
 
-def dense_kernel(*refs):
-    weight_ref, bias_ref, out_ref = refs[2 * SIDE :]
-    for side in range(2):
-        own, *got = refs[side * SIDE : (side + 1) * SIDE]
-        rows = own.shape[0]
-        total = own[...]
-        for ref in got:
-            total += ref[...].astype(F32)
-        hidden = jnp.dot(total.astype(BF16), weight_ref[...], preferred_element_type=F32)
-        hidden = jnp.maximum(hidden + bias_ref[...], 0.0)
-        out_ref[side * rows : (side + 1) * rows, :] = hidden.astype(BF16)
-
-
-def dense(terms, weight, bias):
+def dense_kernel(own, *refs):
+    got, (weight_ref, bias_ref), out_ref = refs[: SIDE - 1], refs[SIDE - 1 : SIDE + 1], refs[-1]
+    total = own[...]
+    for ref in got:
+        total += ref[...].astype(F32)
+    hidden = jnp.dot(total.astype(BF16), weight_ref[...], preferred_element_type=F32)
+    out_ref[...] = jnp.maximum(hidden + bias_ref[...], 0.0).astype(BF16)
+
+
+def dense(side, terms, weight, bias, *done):
+    rows, hidden = terms[0].shape[0], weight.shape[1]
     return pl.pallas_call(
         dense_kernel,
-        out_shape=jax.ShapeDtypeStruct((2 * terms[0].shape[0], weight.shape[1]), BF16),
-        in_specs=[VMEM] * (len(terms) + 2),
-        out_specs=VMEM,
+        grid=(1,),
+        out_shape=jax.ShapeDtypeStruct((2 * rows, hidden), BF16),
+        in_specs=[VMEM] * (SIDE + 2) + [pl.BlockSpec(memory_space=pl.ANY)] * len(done),
+        out_specs=pl.BlockSpec((rows, hidden), lambda step: (side, 0)),
+        input_output_aliases={SIDE + 2: 0} if done else {},
         compiler_params=params(32),
         name="dense",
-    )(*terms, weight, bias.reshape(1, -1))
+    )(*terms, weight, bias.reshape(1, -1), *done)
 
 
 def over(array, axis, bit):
@@ -519,7 +518,8 @@
     kept = tile_products(2, STREAMS, table, x, tiles, rows)
     first = spread(turn_sums(kept[pairs[0]], got_own[0], got_last[0]), "z")
     second = spread(turn_sums(kept[pairs[1]], got_own[1], got_last[1]), "x")
-    return dense(first + second, weight, bias)
+    hidden = dense(0, first, weight, bias)
+    return dense(1, second, weight, bias, hidden)
 
 
 def solution(mesh):

time: 136 us -> 135 us (level)
    ppermute x6, starting transfers between devices: 13.7 us -> 11.2 us  [spread(): lax.ppermute(array, axis, [(c, c ^ bit) for c in range(SIDE)])]
    ppermute x12, starting transfers between devices: 13.4 us -> 15 us  [swap(): lax.ppermute(array, axis, [(c, c ^ bit) for c in range(SIDE)])]
  transfers between devices with their start and end apart: 33 -> 33, of which waited for: 17 -> 17; matrix products, arithmetic and copies ran while one was open for 1% -> 1% of each run, Pallas kernels for 22% -> 23%
where the time goes in v7:
time: 135 us; the launch traced here: 134 us
  Pallas kernels  45.5 us (34%)
  starting transfers between devices  45.4 us (34%)
  waiting for transfers between devices  41.1 us (30%)
    ppermute x12, starting transfers between devices, swap(): lax.ppermute(array, axis, [(c, c ^ bit) for c in range(SIDE)])  15 us
    pallas_call x2, Pallas kernels, tile_products(): pl.pallas_call(functools.partial(tile_kernel, group, arrays), out_shape=[...  13.8 us
    ppermute x14, waiting for transfers between devices, over(): return lax.ppermute(array, axis, pairs)  12.4 us
    all_to_all x1, waiting for transfers between devices, body(): lax.all_to_all(packed, everyone, split_axis=0, concat_axis=0, tiled=True)  11.7 us
    ppermute x6, starting transfers between devices, spread(): lax.ppermute(array, axis, [(c, c ^ bit) for c in range(SIDE)])  11.2 us
    all_to_all x1, starting transfers between devices, body(): lax.all_to_all(packed, everyone, split_axis=0, concat_axis=0, tiled=True)  11.2 us
    ppermute x12, waiting for transfers between devices, swap(): lax.ppermute(array, axis, [(c, c ^ bit) for c in range(SIDE)])  9.47 us
    ppermute x14, starting transfers between devices, over(): return lax.ppermute(array, axis, pairs)  8.07 us
  transfers between devices with their start and end apart: 33, of which 17 were waited for; matrix products, arithmetic and copies ran while one was open for 1% of the time, Pallas kernels for 23%

profile of v7, /device:TPU:0, one launch (start us, length us, event | category | flops | bytes accessed | tf_op | source)
XLA Modules:
  0.0 134.3 jit_solution(5525831599533068638)
XLA Ops:
  0.0 7.9 %pack_rows.1 = bf16[128,40,128]{2,1,0:T(8,128)(2,1)} custom-call(s32[16,128]{1,0:T(8,128)} %bitcast.11, bf16[2048,128]{1,0:T(8,128)(2,1)} %rows_hbm.1), custom_call_target="tpu_custom_call" | custom-call | tf_op jit(solution)/shard_map/pack_rows/pallas_call | solution.py:112
  7.9 11.2 %all-to-all-start = ((bf16[128,40,128]{2,1,0:T(8,128)(2,1)}), bf16[128,40,128]{2,1,0:T(8,128)(2,1)S(1)}, u32[]{:S(2)}, u32[]{:S(2)}) async-start(bf16[128,40,128]{2,1,0:T(8,128)(2,1)} %pack_rows.1), calls=%async_computation | async-start | bytes 2621440 | tf_op jit(solution)/shard_map/all_to_all | solution.py:497
  19.9 0.6 or_or_fusion.code_ref
  20.5 7.2 %plan_tiles.1.table_ref = s32[5,660]{1,0:T(8,128)} custom-call(s32[1]{0:T(128)} %bitcast.4.count_ref, s32[640]{0:T(1024)} %or_or_fusion.code_ref), custom_call_target="tpu_custom_call" | custom-call | tf_op jit(solution)/shard_map/plan_tiles/pallas_call | solution.py:220
  27.7 11.7 %all-to-all-done.in_ref = bf16[128,40,128]{2,1,0:T(8,128)(2,1)S(1)} async-done(((bf16[128,40,128]{2,1,0:T(8,128)(2,1)}), bf16[128,40,128]{2,1,0:T(8,128)(2,1)S(1)}, u32[]{:S(2)}, u32[]{:S(2)}) %all-to-all-start) | async-done | bytes 1310752 | tf_op jit(solution)/shard_map/all_to_all | solution.py:497
  39.4 2.6 %place_rows.2.refs_0_ = bf16[1024,128]{1,0:T(8,128)(2,1)S(1)} custom-call(bf16[128,40,128]{2,1,0:T(8,128)(2,1)S(1)} %all-to-all-done.in_ref), custom_call_target="tpu_custom_call" | custom-call | tf_op jit(solution)/shard_map/place_rows/pallas_call | solution.py:155
  42.0 2.2 %collective-permute-start.7 = (bf16[1024,128]{1,0:T(8,128)(2,1)S(1)}, bf16[1024,128]{1,0:T(8,128)(2,1)S(1)}, u32[]{:S(2)}, u32[]{:S(2)}) collective-permute-start(bf16[1024,128]{1,0:T(8,128)(2,1)S(1)} %place_rows.2.refs_0_), channel_id=1, source_target_pairs={{0,96},{32,64},{64,32},{96,0},{1,97},{33,65},{65,33},{97,1},{2,98}... | collective-permute-start | bytes 786440 | tf_op jit(solution)/shard_map/ppermute | solution.py:454
  44.4 2.5 %place_rows.3.refs_1_ = bf16[1024,128]{1,0:T(8,128)(2,1)S(1)} custom-call(bf16[128,40,128]{2,1,0:T(8,128)(2,1)S(1)} %all-to-all-done.in_ref), custom_call_target="tpu_custom_call" | custom-call | tf_op jit(solution)/shard_map/place_rows/pallas_call | solution.py:155
  46.9 1.9 %collective-permute-start.6 = (bf16[1024,128]{1,0:T(8,128)(2,1)S(1)}, bf16[1024,128]{1,0:T(8,128)(2,1)S(1)}, u32[]{:S(2)}, u32[]{:S(2)}) collective-permute-start(bf16[1024,128]{1,0:T(8,128)(2,1)S(1)} %place_rows.3.refs_1_), channel_id=1, source_target_pairs={{0,32},{32,0},{64,96},{96,64},{1,33},{33,1},{65,97},{97,65},{2,34}... | collective-permute-start | bytes 786440 | tf_op jit(solution)/shard_map/ppermute | solution.py:454
  48.8 1.1 collective-permute-start.2
  49.9 1.1 collective-permute-done.7.refs_6_
  51.0 0.5 collective-permute-start.10
  51.5 1.8 %collective-permute-done.refs_4_ = bf16[1024,128]{1,0:T(8,128)(2,1)S(1)} collective-permute-done((bf16[1024,128]{1,0:T(8,128)(2,1)S(1)}, bf16[1024,128]{1,0:T(8,128)(2,1)S(1)}, u32[]{:S(2)}, u32[]{:S(2)}) %collective-permute-start) | collective-permute-done | bytes 262176 | tf_op jit(solution)/shard_map/ppermute | solution.py:454
  53.3 5.2 %collective-permute-done.6.refs_5_ = bf16[1024,128]{1,0:T(8,128)(2,1)S(1)} collective-permute-done((bf16[1024,128]{1,0:T(8,128)(2,1)S(1)}, bf16[1024,128]{1,0:T(8,128)(2,1)S(1)}, u32[]{:S(2)}, u32[]{:S(2)}) %collective-permute-start.6) | collective-permute-done | bytes 262176 | tf_op jit(solution)/shard_map/ppermute | solution.py:454
  58.5 0.5 collective-permute-start.11
  59.1 1.1 collective-permute-start.1
  60.5 0.7 copy-done.1
  61.2 4.7 %early_products.1 = (bf16[16384,128]{1,0:T(8,128)(2,1)S(1)}, f32[8320,128]{1,0:T(8,128)S(1)}) custom-call(s32[5,660]{1,0:T(8,128)S(1)} %copy-done.1, bf16[1024,128]{1,0:T(8,128)(2,1)S(1)} %place_rows.2.refs_0_, bf16[1024,128]{1,0:T(8,128)(2,1)S(1)} %place_rows.3.refs_1_, bf16[1024,128]{1,0:T(8,128)(2,1)S(1)} %collective-permute-done.4.refs_2_, ...), custom_call_target="tpu_custom_call" | custom-call | flops 5000000000 | bytes 5000000 | tf_op jit(solution)/shard_map/early_products/pallas_call | solution.py:344
  65.9 2.7 %collective-permute-done.1.refs_0_ = bf16[1024,128]{1,0:T(8,128)(2,1)S(1)} collective-permute-done((bf16[1024,128]{1,0:T(8,128)(2,1)S(1)}, bf16[1024,128]{1,0:T(8,128)(2,1)S(1)}, u32[]{:S(2)}, u32[]{:S(2)}) %collective-permute-start.1) | collective-permute-done | bytes 262176 | tf_op jit(solution)/shard_map/ppermute | solution.py:454
  68.6 0.5 collective-permute-start.13
  69.1 1.0 collective-permute-done.12.refs_2_
  70.5 3.3 %late_products.1 = (bf16[16384,128]{1,0:T(8,128)(2,1)S(1)}, f32[8320,128]{1,0:T(8,128)S(1)}, bf16[2048,128]{1,0:T(8,128)(2,1)S(1)}, bf16[2048,128]{1,0:T(8,128)(...) custom-call(s32[5,660]{1,0:T(8,128)S(1)} %copy-done.1, ...), custom_call_target="tpu_custom_call", output_to_operand_aliasing={{0}: (6, {}), {1}: (7, {})} | custom-call | flops 5000000000 | bytes 5000000 | tf_op jit(solution)/shard_map/late_products/pallas_call | solution.py:362
  73.8 0.5 collective-permute-start.14
  74.4 1.1 collective-permute-start.15
  75.5 1.2 collective-permute-start.16
  77.0 8.7 %tile_products.2 = (bf16[2048,128]{1,0:T(8,128)(2,1)S(1)}, bf16[2048,128]{1,0:T(8,128)(2,1)S(1)}, bf16[2048,128]{1,0:T(8,128)(2,1)S(1)}, bf16[2048,128]{1,0:T(8,...) custom-call(s32[5,660]{1,0:T(8,128)S(1)} %copy-done.1, ...), custom_call_target="tpu_custom_call" | custom-call | flops 40000000000 | bytes 40000000 | tf_op jit(solution)/shard_map/tile_products/pallas_call | solution.py:330
  85.8 1.6 %collective-permute-done.14.refs_1_ = bf16[2048,128]{1,0:T(8,128)(2,1)S(1)} collective-permute-done((bf16[2048,128]{1,0:T(8,128)(2,1)S(1)}, bf16[2048,128]{1,0:T(8,128)(2,1)S(1)}, u32[]{:S(2)}, u32[]{:S(2)}) %collective-permute-start.14) | collective-permute-done | bytes 524320 | tf_op jit(solution)/shard_map/ppermute | solution.py:469
  87.4 3.2 %collective-permute-start.19 = (bf16[2048,128]{1,0:T(8,128)(2,1)S(1)}, bf16[2048,128]{1,0:T(8,128)(2,1)S(1)}, u32[]{:S(2)}, u32[]{:S(2)}) collective-permute-start(bf16[2048,128]{1,0:T(8,128)(2,1)S(1)} %get-tuple-element.69), channel_id=1, source_target_pairs={{0,12},{4,8},{8,4},{12,0},{1,13},{5,9},{9,5},{13,1},{2,14},{6,10},... | collective-permute-start | bytes 1572872 | tf_op jit(solution)/shard_map/ppermute | solution.py:469
  90.6 1.1 collective-permute-start.21
  92.1 2.7 %collective-permute-start.27 = (bf16[2048,128]{1,0:T(8,128)(2,1)S(1)}, bf16[2048,128]{1,0:T(8,128)(2,1)S(1)}, u32[]{:S(2)}, u32[]{:S(2)}) collective-permute-start(bf16[2048,128]{1,0:T(8,128)(2,1)S(1)} %get-tuple-element.64), channel_id=1, source_target_pairs={{0,12},{4,8},{8,4},{12,0},{1,13},{5,9},{9,5},{13,1},{2,14},{6,10},... | collective-permute-start | bytes 1572872 | tf_op jit(solution)/shard_map/ppermute | solution.py:469
  94.8 3.9 %collective-permute-done.18.refs_1_ = bf16[2048,128]{1,0:T(8,128)(2,1)S(1)} collective-permute-done((bf16[2048,128]{1,0:T(8,128)(2,1)S(1)}, bf16[2048,128]{1,0:T(8,128)(2,1)S(1)}, u32[]{:S(2)}, u32[]{:S(2)}) %collective-permute-start.18) | collective-permute-done | bytes 524320 | tf_op jit(solution)/shard_map/ppermute | solution.py:469
  98.7 1.7 %collective-permute-start.28 = (bf16[2048,128]{1,0:T(8,128)(2,1)S(1)}, bf16[2048,128]{1,0:T(8,128)(2,1)S(1)}, u32[]{:S(2)}, u32[]{:S(2)}) collective-permute-start(bf16[2048,128]{1,0:T(8,128)(2,1)S(1)} %get-tuple-element.65), channel_id=1, source_target_pairs={{0,4},{4,0},{8,12},{12,8},{1,5},{5,1},{9,13},{13,9},{2,6},{6,2},{1... | collective-permute-start | bytes 1572872 | tf_op jit(solution)/shard_map/ppermute | solution.py:469
  100.4 3.0 %collective-permute-done.19.refs_4_ = bf16[2048,128]{1,0:T(8,128)(2,1)S(1)} collective-permute-done((bf16[2048,128]{1,0:T(8,128)(2,1)S(1)}, bf16[2048,128]{1,0:T(8,128)(2,1)S(1)}, u32[]{:S(2)}, u32[]{:S(2)}) %collective-permute-start.19) | collective-permute-done | bytes 524320 | tf_op jit(solution)/shard_map/ppermute | solution.py:469
  103.5 1.9 %collective-permute-start.22 = (bf16[2048,128]{1,0:T(8,128)(2,1)S(1)}, bf16[2048,128]{1,0:T(8,128)(2,1)S(1)}, u32[]{:S(2)}, u32[]{:S(2)}) collective-permute-start(bf16[2048,128]{1,0:T(8,128)(2,1)S(1)} %get-tuple-element.66), channel_id=1, source_target_pairs={{0,3},{1,2},{2,1},{3,0},{4,7},{5,6},{6,5},{7,4},{8,11},{9,10},{10,... | collective-permute-start | bytes 1572872 | tf_op jit(solution)/shard_map/ppermute | solution.py:469
  105.4 1.1 collective-permute-start.23
  106.5 5.1 %tile_products.3 = (bf16[2048,128]{1,0:T(8,128)(2,1)S(1)}, bf16[2048,128]{1,0:T(8,128)(2,1)S(1)}, bf16[2048,128]{1,0:T(8,128)(2,1)S(1)}, bf16[2048,128]{1,0:T(8,128)(2,1)S(1)}) custom-call(s32[5,660]{1,0:T(8,128)S(1)} %copy-done.1, bf16[16384,128]{1,0:T(8,128)(2,1)S(1)} %get-tuple-element.55.x_ref, bf16[640,128,128]{2,1,0:T(8,128)(2,1)} %bitcast.10), custom_call_target="tpu_custom_call" | custom-call | flops 20000000000 | bytes 20000000 | tf_op jit(solution)/shard_map/tile_products/pallas_call | solution.py:330
  111.6 1.0 collective-permute-done.27.refs_2_
  113.0 2.3 %collective-permute-start.29 = (bf16[1024,128]{1,0:T(8,128)(2,1)S(1)}, bf16[1024,128]{1,0:T(8,128)(2,1)S(1)}, u32[]{:S(2)}, u32[]{:S(2)}) collective-permute-start(bf16[1024,128]{1,0:T(8,128)(2,1)S(1)} %get-tuple-element.86), channel_id=1, source_target_pairs={{0,1},{1,0},{2,3},{3,2},{4,5},{5,4},{6,7},{7,6},{8,9},{9,8},{10,11... | collective-permute-start | bytes 786440 | tf_op jit(solution)/shard_map/ppermute | solution.py:477
  115.7 2.3 %collective-permute-start.31 = (bf16[1024,128]{1,0:T(8,128)(2,1)S(1)}, bf16[1024,128]{1,0:T(8,128)(2,1)S(1)}, u32[]{:S(2)}, u32[]{:S(2)}) collective-permute-start(bf16[1024,128]{1,0:T(8,128)(2,1)S(1)} %get-tuple-element.88), channel_id=1, source_target_pairs={{0,3},{1,2},{2,1},{3,0},{4,7},{5,6},{6,5},{7,4},{8,11},{9,10},{10,... | collective-permute-start | bytes 786440 | tf_op jit(solution)/shard_map/ppermute | solution.py:477
  118.4 1.5 %collective-permute-start.24 = (bf16[1024,128]{1,0:T(8,128)(2,1)S(1)}, bf16[1024,128]{1,0:T(8,128)(2,1)S(1)}, u32[]{:S(2)}, u32[]{:S(2)}) collective-permute-start(bf16[1024,128]{1,0:T(8,128)(2,1)S(1)} %get-tuple-element.78), channel_id=1, source_target_pairs={{0,4},{4,0},{8,12},{12,8},{1,5},{5,1},{9,13},{13,9},{2,6},{6,2},{1... | collective-permute-start | bytes 786440 | tf_op jit(solution)/shard_map/ppermute | solution.py:477
  119.8 2.2 %collective-permute-start.25 = (bf16[1024,128]{1,0:T(8,128)(2,1)S(1)}, bf16[1024,128]{1,0:T(8,128)(2,1)S(1)}, u32[]{:S(2)}, u32[]{:S(2)}) collective-permute-start(bf16[1024,128]{1,0:T(8,128)(2,1)S(1)} %get-tuple-element.79), channel_id=1, source_target_pairs={{0,8},{4,12},{8,0},{12,4},{1,9},{5,13},{9,1},{13,5},{2,10},{6,14},... | collective-permute-start | bytes 786440 | tf_op jit(solution)/shard_map/ppermute | solution.py:477
  122.5 2.5 %collective-permute-start.26 = (bf16[1024,128]{1,0:T(8,128)(2,1)S(1)}, bf16[1024,128]{1,0:T(8,128)(2,1)S(1)}, u32[]{:S(2)}, u32[]{:S(2)}) collective-permute-start(bf16[1024,128]{1,0:T(8,128)(2,1)S(1)} %get-tuple-element.80), channel_id=1, source_target_pairs={{0,12},{4,8},{8,4},{12,0},{1,13},{5,9},{9,5},{13,1},{2,14},{6,10},... | collective-permute-start | bytes 786440 | tf_op jit(solution)/shard_map/ppermute | solution.py:477
  124.9 2.7 %collective-permute-done.30.refs_1_ = bf16[1024,128]{1,0:T(8,128)(2,1)S(1)} collective-permute-done((bf16[1024,128]{1,0:T(8,128)(2,1)S(1)}, bf16[1024,128]{1,0:T(8,128)(2,1)S(1)}, u32[]{:S(2)}, u32[]{:S(2)}) %collective-permute-start.30) | collective-permute-done | bytes 262176 | tf_op jit(solution)/shard_map/ppermute | solution.py:477
  127.7 0.7 collective-permute-done.31.refs_2_
  128.4 1.1 dense.2.refs_5_
  129.5 1.0 collective-permute-done.25.refs_1_
  130.5 2.7 %collective-permute-done.26.refs_2_ = bf16[1024,128]{1,0:T(8,128)(2,1)S(1)} collective-permute-done((bf16[1024,128]{1,0:T(8,128)(2,1)S(1)}, bf16[1024,128]{1,0:T(8,128)(2,1)S(1)}, u32[]{:S(2)}, u32[]{:S(2)}) %collective-permute-start.26) | collective-permute-done | bytes 262176 | tf_op jit(solution)/shard_map/ppermute | solution.py:477
  133.2 1.1 dense.3
  (42 shorter events, 3.4 us)
Async XLA Ops:
  0.0 19.8 %copy-start.3 = (s32[1,1,2,640]{3,2,1,0:T(2,128)S(1)}, s32[1,1,2,640]{3,2,1,0:T(2,128)}, u32[]{:S(2)}) copy-start(s32[1,1,2,640]{3,2,1,0:T(2,128)} %param.10) | copy-start | bytes 15364
  7.9 31.5 %all-to-all-start = ((bf16[128,40,128]{2,1,0:T(8,128)(2,1)}), bf16[128,40,128]{2,1,0:T(8,128)(2,1)S(1)}, u32[]{:S(2)}, u32[]{:S(2)}) async-start(bf16[128,40,128]{2,1,0:T(8,128)(2,1)} %pack_rows.1), calls=%async_computation | async-start | bytes 2621440 | tf_op jit(solution)/shard_map/all_to_all | solution.py:497
  42.0 9.0 %collective-permute-start.7 = (bf16[1024,128]{1,0:T(8,128)(2,1)S(1)}, bf16[1024,128]{1,0:T(8,128)(2,1)S(1)}, u32[]{:S(2)}, u32[]{:S(2)}) collective-permute-start(bf16[1024,128]{1,0:T(8,128)(2,1)S(1)} %place_rows.2.refs_0_), channel_id=1, source_target_pairs={{0,96},{32,64},{64,32},{96,0},{1,97},{33,65},{65,33},{97,1},{2,98}... | collective-permute-start | bytes 786440 | tf_op jit(solution)/shard_map/ppermute | solution.py:454
  44.2 6.8 %collective-permute-start.4 = (bf16[1024,128]{1,0:T(8,128)(2,1)S(1)}, bf16[1024,128]{1,0:T(8,128)(2,1)S(1)}, u32[]{:S(2)}, u32[]{:S(2)}) collective-permute-start(bf16[1024,128]{1,0:T(8,128)(2,1)S(1)} %place_rows.2.refs_0_), channel_id=1, source_target_pairs={{0,16},{16,0},{1,17},{17,1},{2,18},{18,2},{3,19},{19,3},{4,20},{20... | collective-permute-start | bytes 786440 | tf_op jit(solution)/shard_map/ppermute | solution.py:454
  44.2 9.1 %collective-permute-start = (bf16[1024,128]{1,0:T(8,128)(2,1)S(1)}, bf16[1024,128]{1,0:T(8,128)(2,1)S(1)}, u32[]{:S(2)}, u32[]{:S(2)}) collective-permute-start(bf16[1024,128]{1,0:T(8,128)(2,1)S(1)} %place_rows.2.refs_0_), channel_id=1, source_target_pairs={{0,32},{32,0},{64,96},{96,64},{1,33},{33,1},{65,97},{97,65},{2,34}... | collective-permute-start | bytes 786440 | tf_op jit(solution)/shard_map/ppermute | solution.py:454
  46.9 11.6 %collective-permute-start.6 = (bf16[1024,128]{1,0:T(8,128)(2,1)S(1)}, bf16[1024,128]{1,0:T(8,128)(2,1)S(1)}, u32[]{:S(2)}, u32[]{:S(2)}) collective-permute-start(bf16[1024,128]{1,0:T(8,128)(2,1)S(1)} %place_rows.3.refs_1_), channel_id=1, source_target_pairs={{0,32},{32,0},{64,96},{96,64},{1,33},{33,1},{65,97},{97,65},{2,34}... | collective-permute-start | bytes 786440 | tf_op jit(solution)/shard_map/ppermute | solution.py:454
  48.8 9.7 %collective-permute-start.2 = (bf16[1024,128]{1,0:T(8,128)(2,1)S(1)}, bf16[1024,128]{1,0:T(8,128)(2,1)S(1)}, u32[]{:S(2)}, u32[]{:S(2)}) collective-permute-start(bf16[1024,128]{1,0:T(8,128)(2,1)S(1)} %place_rows.3.refs_1_), channel_id=1, source_target_pairs={{0,96},{32,64},{64,32},{96,0},{1,97},{33,65},{65,33},{97,1},{2,98}... | collective-permute-start | bytes 786440 | tf_op jit(solution)/shard_map/ppermute | solution.py:454
  51.0 8.1 %collective-permute-start.5 = (bf16[1024,128]{1,0:T(8,128)(2,1)S(1)}, bf16[1024,128]{1,0:T(8,128)(2,1)S(1)}, u32[]{:S(2)}, u32[]{:S(2)}) collective-permute-start(bf16[1024,128]{1,0:T(8,128)(2,1)S(1)} %place_rows.3.refs_1_), channel_id=1, source_target_pairs={{0,16},{16,0},{1,17},{17,1},{2,18},{18,2},{3,19},{19,3},{4,20},{20... | collective-permute-start | bytes 786440 | tf_op jit(solution)/shard_map/ppermute | solution.py:454
  51.0 9.2 %collective-permute-start.10 = (bf16[1024,128]{1,0:T(8,128)(2,1)S(1)}, bf16[1024,128]{1,0:T(8,128)(2,1)S(1)}, u32[]{:S(2)}, u32[]{:S(2)}) collective-permute-start(bf16[1024,128]{1,0:T(8,128)(2,1)S(1)} %collective-permute-done.7.refs_6_), channel_id=1, source_target_pairs={{0,16},{16,0},{1,17},{17,1},{2,18},{18,2},{3,19},{19,3},{4,20},{20... | collective-permute-start | bytes 786440 | tf_op jit(solution)/shard_map/ppermute | solution.py:454
  53.3 6.9 %collective-permute-start.8 = (bf16[1024,128]{1,0:T(8,128)(2,1)S(1)}, bf16[1024,128]{1,0:T(8,128)(2,1)S(1)}, u32[]{:S(2)}, u32[]{:S(2)}) collective-permute-start(bf16[1024,128]{1,0:T(8,128)(2,1)S(1)} %collective-permute-done.refs_4_), channel_id=1, source_target_pairs={{0,16},{16,0},{1,17},{17,1},{2,18},{18,2},{3,19},{19,3},{4,20},{20... | collective-permute-start | bytes 786440 | tf_op jit(solution)/shard_map/ppermute | solution.py:454
  58.5 1.6 %collective-permute-start.9 = (bf16[1024,128]{1,0:T(8,128)(2,1)S(1)}, bf16[1024,128]{1,0:T(8,128)(2,1)S(1)}, u32[]{:S(2)}, u32[]{:S(2)}) collective-permute-start(bf16[1024,128]{1,0:T(8,128)(2,1)S(1)} %collective-permute-done.6.refs_5_), channel_id=1, source_target_pairs={{0,16},{16,0},{1,17},{17,1},{2,18},{18,2},{3,19},{19,3},{4,20},{20... | collective-permute-start | bytes 786440 | tf_op jit(solution)/shard_map/ppermute | solution.py:454
  58.5 1.9 %collective-permute-start.11 = (bf16[1024,128]{1,0:T(8,128)(2,1)S(1)}, bf16[1024,128]{1,0:T(8,128)(2,1)S(1)}, u32[]{:S(2)}, u32[]{:S(2)}) collective-permute-start(bf16[1024,128]{1,0:T(8,128)(2,1)S(1)} %collective-permute-done.2.refs_7_), channel_id=1, source_target_pairs={{0,16},{16,0},{1,17},{17,1},{2,18},{18,2},{3,19},{19,3},{4,20},{20... | collective-permute-start | bytes 786440 | tf_op jit(solution)/shard_map/ppermute | solution.py:454
  59.1 9.5 %collective-permute-start.1 = (bf16[1024,128]{1,0:T(8,128)(2,1)S(1)}, bf16[1024,128]{1,0:T(8,128)(2,1)S(1)}, u32[]{:S(2)}, u32[]{:S(2)}) collective-permute-start(bf16[1024,128]{1,0:T(8,128)(2,1)S(1)} %collective-permute-done.refs_4_), channel_id=1, source_target_pairs={{0,96},{32,64},{64,32},{96,0},{1,97},{33,65},{65,33},{97,1},{2,98}... | collective-permute-start | bytes 786440 | tf_op jit(solution)/shard_map/ppermute | solution.py:454
  60.2 8.4 %collective-permute-start.3 = (bf16[1024,128]{1,0:T(8,128)(2,1)S(1)}, bf16[1024,128]{1,0:T(8,128)(2,1)S(1)}, u32[]{:S(2)}, u32[]{:S(2)}) collective-permute-start(bf16[1024,128]{1,0:T(8,128)(2,1)S(1)} %collective-permute-done.2.refs_7_), channel_id=1, source_target_pairs={{0,32},{32,0},{64,96},{96,64},{1,33},{33,1},{65,97},{97,65},{2,34}... | collective-permute-start | bytes 786440 | tf_op jit(solution)/shard_map/ppermute | solution.py:454
  60.5 0.7 copy-start.1
  68.6 1.5 %collective-permute-start.12 = (bf16[1024,128]{1,0:T(8,128)(2,1)S(1)}, bf16[1024,128]{1,0:T(8,128)(2,1)S(1)}, u32[]{:S(2)}, u32[]{:S(2)}) collective-permute-start(bf16[1024,128]{1,0:T(8,128)(2,1)S(1)} %collective-permute-done.1.refs_0_), channel_id=1, source_target_pairs={{0,16},{16,0},{1,17},{17,1},{2,18},{18,2},{3,19},{19,3},{4,20},{20... | collective-permute-start | bytes 786440 | tf_op jit(solution)/shard_map/ppermute | solution.py:454
  68.6 1.9 %collective-permute-start.13 = (bf16[1024,128]{1,0:T(8,128)(2,1)S(1)}, bf16[1024,128]{1,0:T(8,128)(2,1)S(1)}, u32[]{:S(2)}, u32[]{:S(2)}) collective-permute-start(bf16[1024,128]{1,0:T(8,128)(2,1)S(1)} %collective-permute-done.3.refs_1_), channel_id=1, source_target_pairs={{0,16},{16,0},{1,17},{17,1},{2,18},{18,2},{3,19},{19,3},{4,20},{20... | collective-permute-start | bytes 786440 | tf_op jit(solution)/shard_map/ppermute | solution.py:454
  73.8 13.6 %collective-permute-start.14 = (bf16[2048,128]{1,0:T(8,128)(2,1)S(1)}, bf16[2048,128]{1,0:T(8,128)(2,1)S(1)}, u32[]{:S(2)}, u32[]{:S(2)}) collective-permute-start(bf16[2048,128]{1,0:T(8,128)(2,1)S(1)} %get-tuple-element.57), channel_id=1, source_target_pairs={{0,4},{4,0},{8,12},{12,8},{1,5},{5,1},{9,13},{13,9},{2,6},{6,2},{1... | collective-permute-start | bytes 1572872 | tf_op jit(solution)/shard_map/ppermute | solution.py:469
  74.4 16.2 %collective-permute-start.15 = (bf16[2048,128]{1,0:T(8,128)(2,1)S(1)}, bf16[2048,128]{1,0:T(8,128)(2,1)S(1)}, u32[]{:S(2)}, u32[]{:S(2)}) collective-permute-start(bf16[2048,128]{1,0:T(8,128)(2,1)S(1)} %get-tuple-element.59), channel_id=1, source_target_pairs={{0,12},{4,8},{8,4},{12,0},{1,13},{5,9},{9,5},{13,1},{2,14},{6,10},... | collective-permute-start | bytes 1572872 | tf_op jit(solution)/shard_map/ppermute | solution.py:469
  75.5 15.1 %collective-permute-start.16 = (bf16[2048,128]{1,0:T(8,128)(2,1)S(1)}, bf16[2048,128]{1,0:T(8,128)(2,1)S(1)}, u32[]{:S(2)}, u32[]{:S(2)}) collective-permute-start(bf16[2048,128]{1,0:T(8,128)(2,1)S(1)} %get-tuple-element.61), channel_id=1, source_target_pairs={{0,1},{1,0},{2,3},{3,2},{4,5},{5,4},{6,7},{7,6},{8,9},{9,8},{10,11... | collective-permute-start | bytes 1572872 | tf_op jit(solution)/shard_map/ppermute | solution.py:469
  76.7 15.0 %collective-permute-start.17 = (bf16[2048,128]{1,0:T(8,128)(2,1)S(1)}, bf16[2048,128]{1,0:T(8,128)(2,1)S(1)}, u32[]{:S(2)}, u32[]{:S(2)}) collective-permute-start(bf16[2048,128]{1,0:T(8,128)(2,1)S(1)} %get-tuple-element.63), channel_id=1, source_target_pairs={{0,3},{1,2},{2,1},{3,0},{4,7},{5,6},{6,5},{7,4},{8,11},{9,10},{10,... | collective-permute-start | bytes 1572872 | tf_op jit(solution)/shard_map/ppermute | solution.py:469
  85.7 13.0 %collective-permute-start.18 = (bf16[2048,128]{1,0:T(8,128)(2,1)S(1)}, bf16[2048,128]{1,0:T(8,128)(2,1)S(1)}, u32[]{:S(2)}, u32[]{:S(2)}) collective-permute-start(bf16[2048,128]{1,0:T(8,128)(2,1)S(1)} %get-tuple-element.68), channel_id=1, source_target_pairs={{0,4},{4,0},{8,12},{12,8},{1,5},{5,1},{9,13},{13,9},{2,6},{6,2},{1... | collective-permute-start | bytes 1572872 | tf_op jit(solution)/shard_map/ppermute | solution.py:469
  87.4 16.1 %collective-permute-start.19 = (bf16[2048,128]{1,0:T(8,128)(2,1)S(1)}, bf16[2048,128]{1,0:T(8,128)(2,1)S(1)}, u32[]{:S(2)}, u32[]{:S(2)}) collective-permute-start(bf16[2048,128]{1,0:T(8,128)(2,1)S(1)} %get-tuple-element.69), channel_id=1, source_target_pairs={{0,12},{4,8},{8,4},{12,0},{1,13},{5,9},{9,5},{13,1},{2,14},{6,10},... | collective-permute-start | bytes 1572872 | tf_op jit(solution)/shard_map/ppermute | solution.py:469
  90.6 14.8 %collective-permute-start.20 = (bf16[2048,128]{1,0:T(8,128)(2,1)S(1)}, bf16[2048,128]{1,0:T(8,128)(2,1)S(1)}, u32[]{:S(2)}, u32[]{:S(2)}) collective-permute-start(bf16[2048,128]{1,0:T(8,128)(2,1)S(1)} %get-tuple-element.70), channel_id=1, source_target_pairs={{0,1},{1,0},{2,3},{3,2},{4,5},{5,4},{6,7},{7,6},{8,9},{9,8},{10,11... | collective-permute-start | bytes 1572872 | tf_op jit(solution)/shard_map/ppermute | solution.py:469
  90.6 15.9 %collective-permute-start.21 = (bf16[2048,128]{1,0:T(8,128)(2,1)S(1)}, bf16[2048,128]{1,0:T(8,128)(2,1)S(1)}, u32[]{:S(2)}, u32[]{:S(2)}) collective-permute-start(bf16[2048,128]{1,0:T(8,128)(2,1)S(1)} %get-tuple-element.71), channel_id=1, source_target_pairs={{0,3},{1,2},{2,1},{3,0},{4,7},{5,6},{6,5},{7,4},{8,11},{9,10},{10,... | collective-permute-start | bytes 1572872 | tf_op jit(solution)/shard_map/ppermute | solution.py:469
  92.1 20.5 %collective-permute-start.27 = (bf16[2048,128]{1,0:T(8,128)(2,1)S(1)}, bf16[2048,128]{1,0:T(8,128)(2,1)S(1)}, u32[]{:S(2)}, u32[]{:S(2)}) collective-permute-start(bf16[2048,128]{1,0:T(8,128)(2,1)S(1)} %get-tuple-element.64), channel_id=1, source_target_pairs={{0,12},{4,8},{8,4},{12,0},{1,13},{5,9},{9,5},{13,1},{2,14},{6,10},... | collective-permute-start | bytes 1572872 | tf_op jit(solution)/shard_map/ppermute | solution.py:469
  98.7 13.9 %collective-permute-start.28 = (bf16[2048,128]{1,0:T(8,128)(2,1)S(1)}, bf16[2048,128]{1,0:T(8,128)(2,1)S(1)}, u32[]{:S(2)}, u32[]{:S(2)}) collective-permute-start(bf16[2048,128]{1,0:T(8,128)(2,1)S(1)} %get-tuple-element.65), channel_id=1, source_target_pairs={{0,4},{4,0},{8,12},{12,8},{1,5},{5,1},{9,13},{13,9},{2,6},{6,2},{1... | collective-permute-start | bytes 1572872 | tf_op jit(solution)/shard_map/ppermute | solution.py:469
  103.5 14.5 %collective-permute-start.22 = (bf16[2048,128]{1,0:T(8,128)(2,1)S(1)}, bf16[2048,128]{1,0:T(8,128)(2,1)S(1)}, u32[]{:S(2)}, u32[]{:S(2)}) collective-permute-start(bf16[2048,128]{1,0:T(8,128)(2,1)S(1)} %get-tuple-element.66), channel_id=1, source_target_pairs={{0,3},{1,2},{2,1},{3,0},{4,7},{5,6},{6,5},{7,4},{8,11},{9,10},{10,... | collective-permute-start | bytes 1572872 | tf_op jit(solution)/shard_map/ppermute | solution.py:469
  105.4 12.6 %collective-permute-start.23 = (bf16[2048,128]{1,0:T(8,128)(2,1)S(1)}, bf16[2048,128]{1,0:T(8,128)(2,1)S(1)}, u32[]{:S(2)}, u32[]{:S(2)}) collective-permute-start(bf16[2048,128]{1,0:T(8,128)(2,1)S(1)} %get-tuple-element.67), channel_id=1, source_target_pairs={{0,1},{1,0},{2,3},{3,2},{4,5},{5,4},{6,7},{7,6},{8,9},{9,8},{10,11... | collective-permute-start | bytes 1572872 | tf_op jit(solution)/shard_map/ppermute | solution.py:469
  111.6 16.8 %copy-start = (bf16[128,256]{1,0:T(8,128)(2,1)S(1)}, bf16[128,256]{1,0:T(8,128)(2,1)}, u32[]{:S(2)}) copy-start(bf16[128,256]{1,0:T(8,128)(2,1)} %refs_3_.3) | copy-start | bytes 196612
  111.6 16.8 %copy-start.2 = (f32[256]{0:T(256)S(1)}, f32[256]{0:T(256)}, u32[]{:S(2)}) copy-start(f32[256]{0:T(256)} %param.13) | copy-start | bytes 3076
  113.0 9.5 %collective-permute-start.29 = (bf16[1024,128]{1,0:T(8,128)(2,1)S(1)}, bf16[1024,128]{1,0:T(8,128)(2,1)S(1)}, u32[]{:S(2)}, u32[]{:S(2)}) collective-permute-start(bf16[1024,128]{1,0:T(8,128)(2,1)S(1)} %get-tuple-element.86), channel_id=1, source_target_pairs={{0,1},{1,0},{2,3},{3,2},{4,5},{5,4},{6,7},{7,6},{8,9},{9,8},{10,11... | collective-permute-start | bytes 786440 | tf_op jit(solution)/shard_map/ppermute | solution.py:477
  115.2 12.5 %collective-permute-start.30 = (bf16[1024,128]{1,0:T(8,128)(2,1)S(1)}, bf16[1024,128]{1,0:T(8,128)(2,1)S(1)}, u32[]{:S(2)}, u32[]{:S(2)}) collective-permute-start(bf16[1024,128]{1,0:T(8,128)(2,1)S(1)} %get-tuple-element.87), channel_id=1, source_target_pairs={{0,2},{1,3},{2,0},{3,1},{4,6},{5,7},{6,4},{7,5},{8,10},{9,11},{10,... | collective-permute-start | bytes 786440 | tf_op jit(solution)/shard_map/ppermute | solution.py:477
  115.7 12.7 %collective-permute-start.31 = (bf16[1024,128]{1,0:T(8,128)(2,1)S(1)}, bf16[1024,128]{1,0:T(8,128)(2,1)S(1)}, u32[]{:S(2)}, u32[]{:S(2)}) collective-permute-start(bf16[1024,128]{1,0:T(8,128)(2,1)S(1)} %get-tuple-element.88), channel_id=1, source_target_pairs={{0,3},{1,2},{2,1},{3,0},{4,7},{5,6},{6,5},{7,4},{8,11},{9,10},{10,... | collective-permute-start | bytes 786440 | tf_op jit(solution)/shard_map/ppermute | solution.py:477
  118.4 11.1 %collective-permute-start.24 = (bf16[1024,128]{1,0:T(8,128)(2,1)S(1)}, bf16[1024,128]{1,0:T(8,128)(2,1)S(1)}, u32[]{:S(2)}, u32[]{:S(2)}) collective-permute-start(bf16[1024,128]{1,0:T(8,128)(2,1)S(1)} %get-tuple-element.78), channel_id=1, source_target_pairs={{0,4},{4,0},{8,12},{12,8},{1,5},{5,1},{9,13},{13,9},{2,6},{6,2},{1... | collective-permute-start | bytes 786440 | tf_op jit(solution)/shard_map/ppermute | solution.py:477
  119.8 10.6 %collective-permute-start.25 = (bf16[1024,128]{1,0:T(8,128)(2,1)S(1)}, bf16[1024,128]{1,0:T(8,128)(2,1)S(1)}, u32[]{:S(2)}, u32[]{:S(2)}) collective-permute-start(bf16[1024,128]{1,0:T(8,128)(2,1)S(1)} %get-tuple-element.79), channel_id=1, source_target_pairs={{0,8},{4,12},{8,0},{12,4},{1,9},{5,13},{9,1},{13,5},{2,10},{6,14},... | collective-permute-start | bytes 786440 | tf_op jit(solution)/shard_map/ppermute | solution.py:477
  122.5 10.7 %collective-permute-start.26 = (bf16[1024,128]{1,0:T(8,128)(2,1)S(1)}, bf16[1024,128]{1,0:T(8,128)(2,1)S(1)}, u32[]{:S(2)}, u32[]{:S(2)}) collective-permute-start(bf16[1024,128]{1,0:T(8,128)(2,1)S(1)} %get-tuple-element.80), channel_id=1, source_target_pairs={{0,12},{4,8},{8,4},{12,0},{1,13},{5,9},{9,5},{13,1},{2,14},{6,10},... | collective-permute-start | bytes 786440 | tf_op jit(solution)/shard_map/ppermute | solution.py:477
